TPU v7x, 256 devices: a whole 4x4x8 slice. The times are simulated.
256 devices in a mesh: dp: 64 (over z_lo, y, x, core), mp: 4 (over z_hi).
Axes of the slice: x: 4, y: 4, z: 8 (z_hi: 4, z_lo: 2; z = z_hi * 2 + z_lo), core: 2. Of those that a mesh axis runs over, the one named last changes fastest.
Arguments:
- pooled_rows: float32 [8192, 1152], P('dp', 'mp'), may hold values from -8 to 8
- projection: float32 [1152, 1152], P('mp'), may hold values from -0.1875 to 0.1875
- text_rows: float32 [8192, 1152], P(('dp', 'mp')), may hold values from -8 to 8
- caption_row: int32 [8192], P('dp'), may hold values from 0 to 8191, as said below
Outputs:
- pooled_grad: float32 [8192, 1152], P('dp', 'mp')
- text_grad: float32 [8192, 1152], P(('dp', 'mp'))
Inputs may be any that keep to these rules, and one draw needn't show every extreme that they name: `caption_row`: every caption row is named by exactly one image. Of the 128 images of one index of dp, those whose caption row lies in the block of 128 rows of any one index (its own included) number 1 to 3; 3 is reached by some pair of indices.
All inputs are finite; a program needn't handle non-finite values.
Results may differ from a plain program's by a relative error of at most 0.0003.
Values sent between devices are 32-bit elements; how exact they have to be, the bound alone decides.
No kernel may reach another device: no remote copies, remote signals or barrier semaphores. Data moves between devices by JAX's collectives and lax.ppermute only.
A program may use at most 64 MiB of HBM per device.

v0:
```python
import jax
import jax.numpy as jnp
from jax import lax
from jax.experimental import pallas as pl
from jax.experimental.pallas import tpu as pltpu
from jax.sharding import Mesh, PartitionSpec as P

LOGIT_SCALE = 10.0
LOGIT_BIAS = -2.0
NORM_EPS = 1e-06

SIZES = {"zl": 2, "y": 4, "x": 4, "c": 2, "zh": 4}
DP = ("zl", "y", "x", "c")
COLUMN = ("zl", "zh")
HALF = 16
LINE = 4 * HALF
TAIL = 8


def pulled(value, axis, steps):
    count = SIZES[axis]
    return lax.ppermute(value, axis, [((i + steps) % count, i) for i in range(count)])


def pulls(value, axis):
    return [value] + [pulled(value, axis, k) for k in (1, 2, 3)]


def returned(terms, axis):
    return sum((pulled(terms[k], axis, -k) for k in (1, 2, 3)), terms[0])


def product(left, right, dims):
    return lax.dot_general(
        left,
        right,
        (dims, ((), ())),
        precision=lax.Precision.HIGHEST,
        preferred_element_type=jnp.float32,
    )


def unit_rows(raw):
    scale = lax.rsqrt(jnp.sum(raw * raw, axis=1) + NORM_EPS)
    return (raw * scale[:, None], scale)


def unit_back(unit, scale, grad):
    return scale[:, None] * (grad - unit * jnp.sum(unit * grad, axis=1, keepdims=True))


def parts(value):
    high = value.astype(jnp.bfloat16)
    return high, (value - high.astype(jnp.float32)).astype(jnp.bfloat16)


def dot3(left, right, dims):
    def one(a, b):
        return lax.dot_general(a, b, (dims, ((), ())), preferred_element_type=jnp.float32)

    return one(left[0], right[0]) + (one(left[0], right[1]) + one(left[1], right[0]))


def stack_kernel(a, b, c, d, out):
    for k, ref in enumerate((a, b, c, d)):
        out[k * HALF : (k + 1) * HALF, :] = ref[:HALF, :]
    rows = [ref[HALF : HALF + 1, :] for ref in (a, b, c, d)]
    out[LINE : LINE + TAIL, :] = jnp.concatenate(rows + [jnp.zeros((4, a.shape[1]), jnp.float32)])


def stacked(pieces):
    width = pieces[0].shape[1]
    return pl.pallas_call(
        stack_kernel, out_shape=jax.ShapeDtypeStruct((LINE + TAIL, width), jnp.float32)
    )(*pieces)


def pair_kernel(adds, *refs):
    lines, (own, other, held), refs = refs[:4], refs[4:7], refs[7:]
    before, refs = (refs[:3], refs[3:]) if adds else (None, refs)
    grads, sums = refs[:4], refs[4:6]
    images = parts(jnp.concatenate([r[:LINE, :] for r in lines]))
    captions = parts(jnp.concatenate([own[...], other[...]]))
    if adds:
        wanted = before[2][:, :1]
    else:
        columns = [r[LINE : LINE + TAIL, :128].T for r in lines]

        def spread(pick):
            return jnp.concatenate(
                [jnp.broadcast_to(pick(k, j), (HALF, 128)) for k in range(4) for j in range(4)]
            )

        wanted = spread(lambda k, j: columns[k][:HALF, j : j + 1])[:, :1]
        refs[6][...] = spread(lambda k, j: columns[j][HALF : 2 * HALF, k : k + 1])
    logits = LOGIT_SCALE * dot3(images, captions, ((1,), (1,))) + LOGIT_BIAS
    signs = jnp.where(wanted == held[...], 1.0, -1.0).astype(jnp.float32)
    weights = (-LOGIT_SCALE * signs) * jax.nn.sigmoid(-signs * logits)
    image_terms = dot3(parts(weights), captions, ((1,), (0,)))
    for k, ref in enumerate(grads):
        ref[...] = image_terms[k * LINE : (k + 1) * LINE]
    caption_terms = dot3(parts(weights.T), images, ((1,), (0,)))
    size = own.shape[0]
    for k, ref in enumerate(sums):
        term = caption_terms[k * size : (k + 1) * size]
        ref[...] = term + before[k][...] if adds else term


def pair_terms(lines, captions, held, before):
    rows, width = captions[0].shape
    adds = before is not None
    shapes = [(LINE, width)] * 4 + [(rows, width)] * 2 + ([] if adds else [(4 * LINE, 128)])
    out = pl.pallas_call(
        lambda *refs: pair_kernel(adds, *refs),
        out_shape=[jax.ShapeDtypeStruct(shape, jnp.float32) for shape in shapes],
        compiler_params=pltpu.CompilerParams(vmem_limit_bytes=48 << 20),
        name="pairs",
    )(*lines, *captions, held, *(before or []))
    return out[:4], out[4:]


def scattered(grads, first, second):
    line = returned(grads, second)
    return returned([line[k * HALF : (k + 1) * HALF] for k in range(4)], first)


def local(pooled_rows, projection, text_rows, caption_row):
    zl, y, x, c, zh = (lax.axis_index(a) for a in ("zl", "y", "x", "c", "zh"))
    per_shard = pooled_rows.shape[0]
    count, width = text_rows.shape
    captions, caption_scale = unit_rows(text_rows)

    partial = product(pooled_rows, projection, ((1,), (0,)))
    projected = returned(
        [lax.dynamic_slice_in_dim(partial, count * ((zh + k) % 4), count, 0) for k in range(4)], "zh"
    )
    images, image_scale = unit_rows(projected)

    named = lax.dynamic_slice_in_dim(caption_row, count * zh, count, 0).astype(jnp.float32)
    tail = jnp.pad(named[None, :], ((0, TAIL - 1), (0, width - count)))

    column = lax.all_to_all(jnp.concatenate([captions] * 8), COLUMN, 0, 0, tiled=True)
    across = pulled(column, "c", 1)
    z = jnp.array([0, 2, 4, 6, 1, 3, 5, 7], jnp.int32)
    shard = (((z % 2) * 4 + y) * 4 + x) * 2 + jnp.stack([c, 1 - c])[:, None]
    held = (shard * per_shard + (z // 2) * count)[:, :, None] + jnp.arange(count, dtype=jnp.int32)
    held = held.reshape(1, -1).astype(jnp.float32)

    first = pulls(stacked(pulls(jnp.concatenate([images[:HALF], tail]), "x")), "y")
    second = pulls(jnp.concatenate(pulls(images[HALF:], "y")), "x")

    grads_first, sums = pair_terms(first, (column, across), held, None)
    grads_second, sums = pair_terms(second, (column, across), held, sums)

    column_sum = sums[0] + pulled(sums[1], "c", 1)
    caption_terms = lax.all_to_all(column_sum, COLUMN, 0, 0, tiled=True)
    caption_grad = jnp.sum(caption_terms.reshape(8, count, width), axis=0)
    text_grad = unit_back(captions, caption_scale, caption_grad)

    image_grad = jnp.concatenate(
        [scattered(grads_first, "x", "y"), scattered(grads_second, "y", "x")]
    )
    raw_grad = unit_back(images, image_scale, image_grad)
    raw_rows = jnp.concatenate(pulls(raw_grad, "zh"))
    pooled_grad = jnp.roll(product(raw_rows, projection, ((1,), (1,))), count * zh, axis=0)
    return (pooled_grad, text_grad)


def solution(mesh):
    grid = Mesh(mesh.devices.reshape(tuple(SIZES.values())), tuple(SIZES))
    return jax.shard_map(
        local,
        mesh=grid,
        in_specs=(P(DP, "zh"), P("zh", None), P((*DP, "zh"), None), P(DP)),
        out_specs=(P(DP, "zh"), P((*DP, "zh"), None)),
        check_vma=False,
    )
```

profile of v0, /device:TPU:6, one launch (start us, length us, event | category | flops | bytes accessed | tf_op | source)
XLA Modules:
  0.0 183.4 jit_solution(6093645278776046779)
XLA Ops:
  7.2 8.6 %all-to-all-start = ((f32[8,32,1152]{2,1,0:T(8,128)}), f32[8,32,1152]{2,1,0:T(8,128)S(1)}, u32[]{:S(2)}, u32[]{:S(2)}) async-start(f32[8,32,1152]{2,1,0:T(8,128)} %bitcast.13), calls=%async_computation | async-start | bytes 2359296 | tf_op jit(solution)/shard_map/all_to_all | solution.py:142
  17.9 2.9 %collective-permute-start = (f32[32,1152]{1,0:T(8,128)}, f32[32,1152]{1,0:T(8,128)S(1)}, u32[]{:S(2)}, u32[]{:S(2)}) collective-permute-start(f32[32,1152]{1,0:T(8,128)} %get-tuple-element.30), channel_id=1, source_target_pairs={{3,0},{0,1},{1,2},{2,3},{7,4},{4,5},{5,6},{6,7},{11,8},{8,9},{9,10... | collective-permute-start | bytes 442376 | tf_op jit(solution)/shard_map/ppermute | solution.py:22
  22.1 5.9 %collective-permute-start.1 = (f32[32,1152]{1,0:T(8,128)}, f32[32,1152]{1,0:T(8,128)S(1)}, u32[]{:S(2)}, u32[]{:S(2)}) collective-permute-start(f32[32,1152]{1,0:T(8,128)} %get-tuple-element.32), channel_id=1, source_target_pairs={{2,0},{3,1},{0,2},{1,3},{6,4},{7,5},{4,6},{5,7},{10,8},{11,9},{8,1... | collective-permute-start | bytes 442376 | tf_op jit(solution)/shard_map/ppermute | solution.py:22
  28.1 26.0 %collective-permute-done = f32[32,1152]{1,0:T(8,128)S(1)} collective-permute-done((f32[32,1152]{1,0:T(8,128)}, f32[32,1152]{1,0:T(8,128)S(1)}, u32[]{:S(2)}, u32[]{:S(2)}) %collective-permute-start) | collective-permute-done | bytes 147488 | tf_op jit(solution)/shard_map/ppermute | solution.py:22
  54.1 6.1 %collective-permute-done.1 = f32[32,1152]{1,0:T(8,128)S(1)} collective-permute-done((f32[32,1152]{1,0:T(8,128)}, f32[32,1152]{1,0:T(8,128)S(1)}, u32[]{:S(2)}, u32[]{:S(2)}) %collective-permute-start.1) | collective-permute-done | bytes 147488 | tf_op jit(solution)/shard_map/ppermute | solution.py:22
  61.7 2.4 %collective-permute-start.4 = (f32[24,1152]{1,0:T(8,128)S(1)}, f32[24,1152]{1,0:T(8,128)S(1)}, u32[]{:S(2)}, u32[]{:S(2)}) collective-permute-start(f32[24,1152]{1,0:T(8,128)S(1)} %select_maximum_fusion.a), channel_id=1, source_target_pairs={{16,0},{24,8},{0,16},{8,24},{17,1},{25,9},{1,17},{9,25},{18,2},{26... | collective-permute-start | bytes 331784 | tf_op jit(solution)/shard_map/ppermute | solution.py:22
  65.7 2.9 %collective-permute-start.17 = (f32[16,1152]{1,0:T(8,128)S(1)}, f32[16,1152]{1,0:T(8,128)}, u32[]{:S(2)}, u32[]{:S(2)}) collective-permute-start(f32[16,1152]{1,0:T(8,128)S(1)} %get-tuple-element.40), channel_id=1, source_target_pairs={{64,0},{96,32},{0,64},{32,96},{65,1},{97,33},{1,65},{33,97},{66,2}... | collective-permute-start | bytes 221192 | tf_op jit(solution)/shard_map/ppermute | solution.py:22
  71.1 4.9 %collective-permute-done.3.b = f32[24,1152]{1,0:T(8,128)S(1)} collective-permute-done((f32[24,1152]{1,0:T(8,128)S(1)}, f32[24,1152]{1,0:T(8,128)S(1)}, u32[]{:S(2)}, u32[]{:S(2)}) %collective-permute-start.3) | collective-permute-done | bytes 110624 | tf_op jit(solution)/shard_map/ppermute | solution.py:22
  79.0 2.6 %collective-permute-start.7 = (f32[72,1152]{1,0:T(8,128)}, f32[72,1152]{1,0:T(8,128)S(1)}, u32[]{:S(2)}, u32[]{:S(2)}) collective-permute-start(f32[72,1152]{1,0:T(8,128)} %shard_map.68.refs_0_), channel_id=1, source_target_pairs={{64,0},{96,32},{0,64},{32,96},{65,1},{97,33},{1,65},{33,97},{66,2}... | collective-permute-start | bytes 995336 | tf_op jit(solution)/shard_map/ppermute | solution.py:22
  89.0 6.9 %collective-permute-done.7.refs_2_ = f32[72,1152]{1,0:T(8,128)S(1)} collective-permute-done((f32[72,1152]{1,0:T(8,128)}, f32[72,1152]{1,0:T(8,128)S(1)}, u32[]{:S(2)}, u32[]{:S(2)}) %collective-permute-start.7) | collective-permute-done | bytes 331808 | tf_op jit(solution)/shard_map/ppermute | solution.py:22
  97.1 4.9 %pairs.2 = (f32[64,1152]{1,0:T(8,128)S(1)}, f32[64,1152]{1,0:T(8,128)S(1)}, f32[64,1152]{1,0:T(8,128)S(1)}, f32[64,1152]{1,0:T(8,128)S(1)}, f32[256,1152]{1,0:T(...) custom-call(f32[72,1152]{1,0:T(8,128)S(1)} %copy-done.1, f32[72,1152]{1,0:T(8,128)} %collective-permute-done.6.refs_1_, ...), custom_call_target="tpu_custom_call" | custom-call | tf_op jit(solution)/shard_map/pairs/pallas_call | solution.py:113
  109.3 5.7 %pairs.3 = (f32[64,1152]{1,0:T(8,128)S(1)}, f32[64,1152]{1,0:T(8,128)S(1)}, f32[64,1152]{1,0:T(8,128)S(1)}, f32[64,1152]{1,0:T(8,128)S(1)}, f32[256,1152]{1,0:T(8,128)S(1)}, /*index=5*/f32[256,1152]{1,0:T(8,128)S(1)}) custom-call(f32[64,1152]{1,0:T(8,128)S(1)} %pad_maximum_fusion.refs_0_, f32[64,1152]{1,0:T(8,128)} %collective-permute-done.19.refs_1_, ...), custom_call_target="tpu_custom_call" | custom-call | tf_op jit(solution)/shard_map/pairs/pallas_call | solution.py:113
  119.5 3.3 %collective-permute-start.13 = (f32[16,1152]{1,0:T(8,128)S(1)}, f32[16,1152]{1,0:T(8,128)S(1)}, u32[]{:S(2)}, u32[]{:S(2)}) collective-permute-start(f32[16,1152]{1,0:T(8,128)S(1)} %get-tuple-element.33), channel_id=1, source_target_pairs={{24,0},{0,8},{8,16},{16,24},{25,1},{1,9},{9,17},{17,25},{26,2},{2,... | collective-permute-start | bytes 221192 | tf_op jit(solution)/shard_map/ppermute | solution.py:22
  122.8 2.2 %collective-permute-done.22 = f32[64,1152]{1,0:T(8,128)S(1)} collective-permute-done((f32[64,1152]{1,0:T(8,128)S(1)}, f32[64,1152]{1,0:T(8,128)S(1)}, u32[]{:S(2)}, u32[]{:S(2)}) %collective-permute-start.22) | collective-permute-done | bytes 294944 | tf_op jit(solution)/shard_map/ppermute | solution.py:22
  125.0 5.2 %collective-permute-start.15 = (f32[16,1152]{1,0:T(8,128)S(1)}, f32[16,1152]{1,0:T(8,128)S(1)}, u32[]{:S(2)}, u32[]{:S(2)}) collective-permute-start(f32[16,1152]{1,0:T(8,128)S(1)} %get-tuple-element.34), channel_id=1, source_target_pairs={{8,0},{16,8},{24,16},{0,24},{9,1},{17,9},{25,17},{1,25},{10,2},{18... | collective-permute-start | bytes 221192 | tf_op jit(solution)/shard_map/ppermute | solution.py:22
  130.6 2.2 %collective-permute-done.24 = f32[64,1152]{1,0:T(8,128)S(1)} collective-permute-done((f32[64,1152]{1,0:T(8,128)S(1)}, f32[64,1152]{1,0:T(8,128)S(1)}, u32[]{:S(2)}, u32[]{:S(2)}) %collective-permute-start.24) | collective-permute-done | bytes 294944 | tf_op jit(solution)/shard_map/ppermute | solution.py:22
  134.0 3.6 %all-to-all-start.1 = ((f32[8,32,1152]{2,1,0:T(8,128)}), f32[8,32,1152]{2,1,0:T(8,128)S(1)}, u32[]{:S(2)}, u32[]{:S(2)}) async-start(f32[8,32,1152]{2,1,0:T(8,128)} %bitcast.5), calls=%async_computation.1 | async-start | bytes 2359296 | tf_op jit(solution)/shard_map/all_to_all | solution.py:156
  137.7 2.4 %collective-permute-start.25 = (f32[16,1152]{1,0:T(8,128)S(1)}, f32[16,1152]{1,0:T(8,128)S(1)}, u32[]{:S(2)}, u32[]{:S(2)}) collective-permute-start(f32[16,1152]{1,0:T(8,128)S(1)} %get-tuple-element.36), channel_id=1, source_target_pairs={{96,0},{0,32},{32,64},{64,96},{97,1},{1,33},{33,65},{65,97},{98,2}... | collective-permute-start | bytes 221192 | tf_op jit(solution)/shard_map/ppermute | solution.py:22
  144.4 2.4 %collective-permute-done.26 = f32[16,1152]{1,0:T(8,128)S(1)} collective-permute-done((f32[16,1152]{1,0:T(8,128)S(1)}, f32[16,1152]{1,0:T(8,128)S(1)}, u32[]{:S(2)}, u32[]{:S(2)}) %collective-permute-start.26) | collective-permute-done | bytes 73760 | tf_op jit(solution)/shard_map/ppermute | solution.py:22
  147.2 2.9 %collective-permute-start.30 = (f32[32,1152]{1,0:T(8,128)S(1)}, f32[32,1152]{1,0:T(8,128)S(1)}, u32[]{:S(2)}, u32[]{:S(2)}) collective-permute-start(f32[32,1152]{1,0:T(8,128)S(1)} %subtract_multiply_fusion.1), channel_id=1, source_target_pairs={{3,0},{0,1},{1,2},{2,3},{7,4},{4,5},{5,6},{6,7},{11,8},{8,9},{9,10... | collective-permute-start | bytes 442376 | tf_op jit(solution)/shard_map/ppermute | solution.py:22
  150.0 3.6 %collective-permute-start.29 = (f32[32,1152]{1,0:T(8,128)S(1)}, f32[32,1152]{1,0:T(8,128)S(1)}, u32[]{:S(2)}, u32[]{:S(2)}) collective-permute-start(f32[32,1152]{1,0:T(8,128)S(1)} %subtract_multiply_fusion.1), channel_id=1, source_target_pairs={{2,0},{3,1},{0,2},{1,3},{6,4},{7,5},{4,6},{5,7},{10,8},{11,9},{8,1... | collective-permute-start | bytes 442376 | tf_op jit(solution)/shard_map/ppermute | solution.py:22
  153.6 3.6 %collective-permute-start.28 = (f32[32,1152]{1,0:T(8,128)S(1)}, f32[32,1152]{1,0:T(8,128)S(1)}, u32[]{:S(2)}, u32[]{:S(2)}) collective-permute-start(f32[32,1152]{1,0:T(8,128)S(1)} %subtract_multiply_fusion.1), channel_id=1, source_target_pairs={{1,0},{2,1},{3,2},{0,3},{5,4},{6,5},{7,6},{4,7},{9,8},{10,9},{11,1... | collective-permute-start | bytes 442376 | tf_op jit(solution)/shard_map/ppermute | solution.py:22
  157.2 16.6 %collective-permute-done.30 = f32[32,1152]{1,0:T(8,128)S(1)} collective-permute-done((f32[32,1152]{1,0:T(8,128)S(1)}, f32[32,1152]{1,0:T(8,128)S(1)}, u32[]{:S(2)}, u32[]{:S(2)}) %collective-permute-start.30) | collective-permute-done | bytes 147488 | tf_op jit(solution)/shard_map/ppermute | solution.py:22
  173.8 6.5 %collective-permute-done.29 = f32[32,1152]{1,0:T(8,128)S(1)} collective-permute-done((f32[32,1152]{1,0:T(8,128)S(1)}, f32[32,1152]{1,0:T(8,128)S(1)}, u32[]{:S(2)}, u32[]{:S(2)}) %collective-permute-start.29) | collective-permute-done | bytes 147488 | tf_op jit(solution)/shard_map/ppermute | solution.py:22
  (119 shorter events, 48.1 us)
Async XLA Ops:
  7.2 53.8 %all-to-all-start = ((f32[8,32,1152]{2,1,0:T(8,128)}), f32[8,32,1152]{2,1,0:T(8,128)S(1)}, u32[]{:S(2)}, u32[]{:S(2)}) async-start(f32[8,32,1152]{2,1,0:T(8,128)} %bitcast.13), calls=%async_computation | async-start | bytes 2359296 | tf_op jit(solution)/shard_map/all_to_all | solution.py:142
  17.9 36.1 %collective-permute-start = (f32[32,1152]{1,0:T(8,128)}, f32[32,1152]{1,0:T(8,128)S(1)}, u32[]{:S(2)}, u32[]{:S(2)}) collective-permute-start(f32[32,1152]{1,0:T(8,128)} %get-tuple-element.30), channel_id=1, source_target_pairs={{3,0},{0,1},{1,2},{2,3},{7,4},{4,5},{5,6},{6,7},{11,8},{8,9},{9,10... | collective-permute-start | bytes 442376 | tf_op jit(solution)/shard_map/ppermute | solution.py:22
  20.8 33.2 %collective-permute-start.2 = (f32[32,1152]{1,0:T(8,128)}, f32[32,1152]{1,0:T(8,128)S(1)}, u32[]{:S(2)}, u32[]{:S(2)}) collective-permute-start(f32[32,1152]{1,0:T(8,128)} %get-tuple-element.31), channel_id=1, source_target_pairs={{1,0},{2,1},{3,2},{0,3},{5,4},{6,5},{7,6},{4,7},{9,8},{10,9},{11,1... | collective-permute-start | bytes 442376 | tf_op jit(solution)/shard_map/ppermute | solution.py:22
  22.1 38.1 %collective-permute-start.1 = (f32[32,1152]{1,0:T(8,128)}, f32[32,1152]{1,0:T(8,128)S(1)}, u32[]{:S(2)}, u32[]{:S(2)}) collective-permute-start(f32[32,1152]{1,0:T(8,128)} %get-tuple-element.32), channel_id=1, source_target_pairs={{2,0},{3,1},{0,2},{1,3},{6,4},{7,5},{4,6},{5,7},{10,8},{11,9},{8,1... | collective-permute-start | bytes 442376 | tf_op jit(solution)/shard_map/ppermute | solution.py:22
  61.0 35.1 %collective-permute-start.9 = (f32[256,1152]{1,0:T(8,128)S(1)}, f32[256,1152]{1,0:T(8,128)}, u32[]{:S(2)}, u32[]{:S(2)}) collective-permute-start(f32[256,1152]{1,0:T(8,128)S(1)} %bitcast.10), channel_id=1, source_target_pairs={{4,0},{0,4},{5,1},{1,5},{6,2},{2,6},{7,3},{3,7},{12,8},{8,12},{13,... | collective-permute-start | bytes 3538952 | tf_op jit(solution)/shard_map/ppermute | solution.py:22
  64.1 15.0 %collective-permute-start.18 = (f32[16,1152]{1,0:T(8,128)S(1)}, f32[16,1152]{1,0:T(8,128)}, u32[]{:S(2)}, u32[]{:S(2)}) collective-permute-start(f32[16,1152]{1,0:T(8,128)S(1)} %get-tuple-element.40), channel_id=1, source_target_pairs={{96,0},{0,32},{32,64},{64,96},{97,1},{1,33},{33,65},{65,97},{98,2}... | collective-permute-start | bytes 221192 | tf_op jit(solution)/shard_map/ppermute | solution.py:22
  65.7 16.0 %collective-permute-start.17 = (f32[16,1152]{1,0:T(8,128)S(1)}, f32[16,1152]{1,0:T(8,128)}, u32[]{:S(2)}, u32[]{:S(2)}) collective-permute-start(f32[16,1152]{1,0:T(8,128)S(1)} %get-tuple-element.40), channel_id=1, source_target_pairs={{64,0},{96,32},{0,64},{32,96},{65,1},{97,33},{1,65},{33,97},{66,2}... | collective-permute-start | bytes 221192 | tf_op jit(solution)/shard_map/ppermute | solution.py:22
  68.6 13.1 %collective-permute-start.16 = (f32[16,1152]{1,0:T(8,128)S(1)}, f32[16,1152]{1,0:T(8,128)}, u32[]{:S(2)}, u32[]{:S(2)}) collective-permute-start(f32[16,1152]{1,0:T(8,128)S(1)} %get-tuple-element.40), channel_id=1, source_target_pairs={{32,0},{64,32},{96,64},{0,96},{33,1},{65,33},{97,65},{1,97},{34,2}... | collective-permute-start | bytes 221192 | tf_op jit(solution)/shard_map/ppermute | solution.py:22
  79.0 16.9 %collective-permute-start.7 = (f32[72,1152]{1,0:T(8,128)}, f32[72,1152]{1,0:T(8,128)S(1)}, u32[]{:S(2)}, u32[]{:S(2)}) collective-permute-start(f32[72,1152]{1,0:T(8,128)} %shard_map.68.refs_0_), channel_id=1, source_target_pairs={{64,0},{96,32},{0,64},{32,96},{65,1},{97,33},{1,65},{33,97},{66,2}... | collective-permute-start | bytes 995336 | tf_op jit(solution)/shard_map/ppermute | solution.py:22
  82.6 24.9 %collective-permute-start.21 = (f32[64,1152]{1,0:T(8,128)S(1)}, f32[64,1152]{1,0:T(8,128)}, u32[]{:S(2)}, u32[]{:S(2)}) collective-permute-start(f32[64,1152]{1,0:T(8,128)S(1)} %pad_maximum_fusion.refs_0_), channel_id=1, source_target_pairs={{24,0},{0,8},{8,16},{16,24},{25,1},{1,9},{9,17},{17,25},{26,2},{2,... | collective-permute-start | bytes 884744 | tf_op jit(solution)/shard_map/ppermute | solution.py:22
  88.2 21.0 %collective-permute-start.20 = (f32[64,1152]{1,0:T(8,128)S(1)}, f32[64,1152]{1,0:T(8,128)}, u32[]{:S(2)}, u32[]{:S(2)}) collective-permute-start(f32[64,1152]{1,0:T(8,128)S(1)} %pad_maximum_fusion.refs_0_), channel_id=1, source_target_pairs={{16,0},{24,8},{0,16},{8,24},{17,1},{25,9},{1,17},{9,25},{18,2},{26... | collective-permute-start | bytes 884744 | tf_op jit(solution)/shard_map/ppermute | solution.py:22
  95.9 13.3 %collective-permute-start.19 = (f32[64,1152]{1,0:T(8,128)S(1)}, f32[64,1152]{1,0:T(8,128)}, u32[]{:S(2)}, u32[]{:S(2)}) collective-permute-start(f32[64,1152]{1,0:T(8,128)S(1)} %pad_maximum_fusion.refs_0_), channel_id=1, source_target_pairs={{8,0},{16,8},{24,16},{0,24},{9,1},{17,9},{25,17},{1,25},{10,2},{18... | collective-permute-start | bytes 884744 | tf_op jit(solution)/shard_map/ppermute | solution.py:22
  104.0 14.5 %collective-permute-start.10 = (f32[64,1152]{1,0:T(8,128)S(1)}, f32[64,1152]{1,0:T(8,128)S(1)}, u32[]{:S(2)}, u32[]{:S(2)}) collective-permute-start(f32[64,1152]{1,0:T(8,128)S(1)} %get-tuple-element.16), channel_id=1, source_target_pairs={{96,0},{0,32},{32,64},{64,96},{97,1},{1,33},{33,65},{65,97},{98,2}... | collective-permute-start | bytes 884744 | tf_op jit(solution)/shard_map/ppermute | solution.py:22
  105.6 13.8 %collective-permute-start.11 = (f32[64,1152]{1,0:T(8,128)S(1)}, f32[64,1152]{1,0:T(8,128)S(1)}, u32[]{:S(2)}, u32[]{:S(2)}) collective-permute-start(f32[64,1152]{1,0:T(8,128)S(1)} %get-tuple-element.17), channel_id=1, source_target_pairs={{64,0},{96,32},{0,64},{32,96},{65,1},{97,33},{1,65},{33,97},{66,2}... | collective-permute-start | bytes 884744 | tf_op jit(solution)/shard_map/ppermute | solution.py:22
  116.8 13.4 %collective-permute-start.23 = (f32[64,1152]{1,0:T(8,128)S(1)}, f32[64,1152]{1,0:T(8,128)S(1)}, u32[]{:S(2)}, u32[]{:S(2)}) collective-permute-start(f32[64,1152]{1,0:T(8,128)S(1)} %get-tuple-element.24), channel_id=1, source_target_pairs={{16,0},{24,8},{0,16},{8,24},{17,1},{25,9},{1,17},{9,25},{18,2},{26... | collective-permute-start | bytes 884744 | tf_op jit(solution)/shard_map/ppermute | solution.py:22
  118.5 14.3 %collective-permute-start.24 = (f32[64,1152]{1,0:T(8,128)S(1)}, f32[64,1152]{1,0:T(8,128)S(1)}, u32[]{:S(2)}, u32[]{:S(2)}) collective-permute-start(f32[64,1152]{1,0:T(8,128)S(1)} %get-tuple-element.25), channel_id=1, source_target_pairs={{8,0},{16,8},{24,16},{0,24},{9,1},{17,9},{25,17},{1,25},{10,2},{18... | collective-permute-start | bytes 884744 | tf_op jit(solution)/shard_map/ppermute | solution.py:22
  119.4 13.4 %collective-permute-start.31 = (f32[256,1152]{1,0:T(8,128)S(1)}, f32[256,1152]{1,0:T(8,128)S(1)}, u32[]{:S(2)}, u32[]{:S(2)}) collective-permute-start(f32[256,1152]{1,0:T(8,128)S(1)} %get-tuple-element.27), channel_id=1, source_target_pairs={{4,0},{0,4},{5,1},{1,5},{6,2},{2,6},{7,3},{3,7},{12,8},{8,12},{13,... | collective-permute-start | bytes 3538952 | tf_op jit(solution)/shard_map/ppermute | solution.py:22
  119.5 21.4 %collective-permute-start.13 = (f32[16,1152]{1,0:T(8,128)S(1)}, f32[16,1152]{1,0:T(8,128)S(1)}, u32[]{:S(2)}, u32[]{:S(2)}) collective-permute-start(f32[16,1152]{1,0:T(8,128)S(1)} %get-tuple-element.33), channel_id=1, source_target_pairs={{24,0},{0,8},{8,16},{16,24},{25,1},{1,9},{9,17},{17,25},{26,2},{2,... | collective-permute-start | bytes 221192 | tf_op jit(solution)/shard_map/ppermute | solution.py:22
  125.0 17.4 %collective-permute-start.15 = (f32[16,1152]{1,0:T(8,128)S(1)}, f32[16,1152]{1,0:T(8,128)S(1)}, u32[]{:S(2)}, u32[]{:S(2)}) collective-permute-start(f32[16,1152]{1,0:T(8,128)S(1)} %get-tuple-element.34), channel_id=1, source_target_pairs={{8,0},{16,8},{24,16},{0,24},{9,1},{17,9},{25,17},{1,25},{10,2},{18... | collective-permute-start | bytes 221192 | tf_op jit(solution)/shard_map/ppermute | solution.py:22
  130.3 12.2 %collective-permute-start.14 = (f32[16,1152]{1,0:T(8,128)S(1)}, f32[16,1152]{1,0:T(8,128)S(1)}, u32[]{:S(2)}, u32[]{:S(2)}) collective-permute-start(f32[16,1152]{1,0:T(8,128)S(1)} %get-tuple-element.35), channel_id=1, source_target_pairs={{16,0},{24,8},{0,16},{8,24},{17,1},{25,9},{1,17},{9,25},{18,2},{26... | collective-permute-start | bytes 221192 | tf_op jit(solution)/shard_map/ppermute | solution.py:22
  134.0 48.4 %all-to-all-start.1 = ((f32[8,32,1152]{2,1,0:T(8,128)}), f32[8,32,1152]{2,1,0:T(8,128)S(1)}, u32[]{:S(2)}, u32[]{:S(2)}) async-start(f32[8,32,1152]{2,1,0:T(8,128)} %bitcast.5), calls=%async_computation.1 | async-start | bytes 2359296 | tf_op jit(solution)/shard_map/all_to_all | solution.py:156
  147.2 26.7 %collective-permute-start.30 = (f32[32,1152]{1,0:T(8,128)S(1)}, f32[32,1152]{1,0:T(8,128)S(1)}, u32[]{:S(2)}, u32[]{:S(2)}) collective-permute-start(f32[32,1152]{1,0:T(8,128)S(1)} %subtract_multiply_fusion.1), channel_id=1, source_target_pairs={{3,0},{0,1},{1,2},{2,3},{7,4},{4,5},{5,6},{6,7},{11,8},{8,9},{9,10... | collective-permute-start | bytes 442376 | tf_op jit(solution)/shard_map/ppermute | solution.py:22
  150.0 30.3 %collective-permute-start.29 = (f32[32,1152]{1,0:T(8,128)S(1)}, f32[32,1152]{1,0:T(8,128)S(1)}, u32[]{:S(2)}, u32[]{:S(2)}) collective-permute-start(f32[32,1152]{1,0:T(8,128)S(1)} %subtract_multiply_fusion.1), channel_id=1, source_target_pairs={{2,0},{3,1},{0,2},{1,3},{6,4},{7,5},{4,6},{5,7},{10,8},{11,9},{8,1... | collective-permute-start | bytes 442376 | tf_op jit(solution)/shard_map/ppermute | solution.py:22
  153.6 26.7 %collective-permute-start.28 = (f32[32,1152]{1,0:T(8,128)S(1)}, f32[32,1152]{1,0:T(8,128)S(1)}, u32[]{:S(2)}, u32[]{:S(2)}) collective-permute-start(f32[32,1152]{1,0:T(8,128)S(1)} %subtract_multiply_fusion.1), channel_id=1, source_target_pairs={{1,0},{2,1},{3,2},{0,3},{5,4},{6,5},{7,6},{4,7},{9,8},{10,9},{11,1... | collective-permute-start | bytes 442376 | tf_op jit(solution)/shard_map/ppermute | solution.py:22
  (27 other events, 239.2 us)
where the time goes:
time: 184 us; the launch traced here: 183 us
  waiting for transfers between devices  78.5 us (43%)
  starting transfers between devices  71.3 us (39%)
  Pallas kernels  12.5 us (7%)
  other arithmetic  11.5 us (6%)
  local copies, waits for them, and re-layouts  6.22 us (3%)
  matrix products  2.54 us (1%)
    ppermute x32, waiting for transfers between devices, pulled(): lax.ppermute(value, axis, [((i + steps) % count, i) for i in range(count)])  78.5 us
    ppermute x32, starting transfers between devices, pulled(): lax.ppermute(value, axis, [((i + steps) % count, i) for i in range(count)])  59.1 us
    pallas_call x2, Pallas kernels, pair_terms(): pl.pallas_call(lambda *refs: pair_kernel(adds, *refs), out_shape=[jax.Sha...  10.6 us
    all_to_all x1, starting transfers between devices, local(): lax.all_to_all(jnp.concatenate([captions] * 8), COLUMN, 0, 0, tiled=True)  8.6 us
    unnamed x34, local copies, waits for them, and re-layouts  5.31 us
    unnamed x7, other arithmetic  4.22 us
  transfers between devices with their start and end apart: 34, of which 13 were waited for; matrix products, arithmetic and copies ran while one was open for 5% of the time, Pallas kernels for 7%

commit v1 on v0

v1 whole, which is shorter than its diff:
```python
import jax
import jax.numpy as jnp
from jax import lax
from jax.experimental import pallas as pl
from jax.experimental.pallas import tpu as pltpu
from jax.sharding import Mesh, PartitionSpec as P

LOGIT_SCALE = 10.0
LOGIT_BIAS = -2.0
NORM_EPS = 1e-06

SIZES = {"zl": 2, "y": 4, "x": 4, "c": 2, "zh": 4}
DP = ("zl", "y", "x", "c")


def pulled(value, axis, steps):
    count = SIZES[axis]
    return lax.ppermute(value, axis, [((i + steps) % count, i) for i in range(count)])


def pulls(value, axis):
    return [value] + [pulled(value, axis, k) for k in (1, 2, 3)]


def returned(terms, axis):
    return sum((pulled(terms[k], axis, -k) for k in (1, 2, 3)), terms[0])


def product(left, right, dims):
    return lax.dot_general(
        left,
        right,
        (dims, ((), ())),
        precision=lax.Precision.HIGHEST,
        preferred_element_type=jnp.float32,
    )


def unit_rows(raw):
    scale = lax.rsqrt(jnp.sum(raw * raw, axis=1) + NORM_EPS)
    return (raw * scale[:, None], scale)


def unit_back(unit, scale, grad):
    return scale[:, None] * (grad - unit * jnp.sum(unit * grad, axis=1, keepdims=True))


def parts(value):
    high = value.astype(jnp.bfloat16)
    return high, (value - high.astype(jnp.float32)).astype(jnp.bfloat16)


def dot3(left, right, dims):
    def one(a, b):
        return lax.dot_general(a, b, (dims, ((), ())), preferred_element_type=jnp.float32)

    return one(left[0], right[0]) + (one(left[0], right[1]) + one(left[1], right[0]))


def image_kernel(adds, *refs):
    own, other, wanted, held = refs[:4]
    blocks, refs = refs[4:8], refs[8:]
    before, refs = (refs[:2], refs[2:]) if adds else (None, refs)
    grads, weights_out = refs[:2], refs[2]
    images = parts(jnp.concatenate([own[...], other[...]]))
    captions = parts(jnp.concatenate([r[...] for r in blocks]))
    logits = LOGIT_SCALE * dot3(images, captions, ((1,), (1,))) + LOGIT_BIAS
    signs = jnp.where(wanted[:, :1] == held[...], 1.0, -1.0).astype(jnp.float32)
    weights = (-LOGIT_SCALE * signs) * jax.nn.sigmoid(-signs * logits)
    weights_out[...] = weights
    image_terms = dot3(parts(weights), captions, ((1,), (0,)))
    size = own.shape[0]
    for k, ref in enumerate(grads):
        term = image_terms[k * size : (k + 1) * size]
        ref[...] = term + before[k][...] if adds else term


def caption_kernel(own, other, weights, *sums):
    images = parts(jnp.concatenate([own[...], other[...]]))
    caption_terms = dot3(parts(weights[...].T), images, ((1,), (0,)))
    size = sums[0].shape[0]
    for k, ref in enumerate(sums):
        ref[...] = caption_terms[k * size : (k + 1) * size]


def called(kernel, name, shapes, *args):
    return pl.pallas_call(
        kernel,
        out_shape=[jax.ShapeDtypeStruct(shape, jnp.float32) for shape in shapes],
        compiler_params=pltpu.CompilerParams(vmem_limit_bytes=48 << 20),
        name=name,
    )(*args)


def image_terms(images, wanted, held, blocks, before):
    shapes = [images[0].shape] * 2 + [(wanted.shape[0], held.shape[1])]
    out = called(
        lambda *refs: image_kernel(before is not None, *refs),
        "image_terms", shapes, *images, wanted, held, *blocks, *(before or []),
    )
    return out[:2], out[2]


def caption_terms(images, weights, shape):
    return called(caption_kernel, "caption_terms", [shape] * 4, *images, weights)


def shared(rows):
    rows = jnp.broadcast_to(rows[None], (4, *rows.shape)).reshape(-1, rows.shape[1])
    return lax.all_to_all(rows, "zh", 0, 0, tiled=True)


def line_parts(line):
    size = line.shape[0] // 4
    return [line[k * size : (k + 1) * size] for k in range(4)]


def local(pooled_rows, projection, text_rows, caption_row):
    zl, y, x, c, zh = (lax.axis_index(a) for a in ("zl", "y", "x", "c", "zh"))
    per_shard = pooled_rows.shape[0]
    count, width = text_rows.shape
    captions, caption_scale = unit_rows(text_rows)

    partial = product(pooled_rows, projection, ((1,), (0,)))
    partial, moved = lax.optimization_barrier((partial, pulled(captions, "zl", 1)))
    projected = jnp.sum(
        lax.all_to_all(partial, "zh", 0, 0, tiled=True).reshape(4, count, width), axis=0
    )

    near_line = jnp.concatenate(pulls(captions, "x"))
    far_line = jnp.concatenate(pulls(moved, "y"))
    near_line, far_line, projected = lax.optimization_barrier((near_line, far_line, projected))
    near = pulls(near_line, "y")
    far = pulls(far_line, "x")
    images, image_scale = unit_rows(projected)
    shard_images = shared(images)
    chip_images = [shard_images, pulled(shard_images, "c", 1)]

    named = caption_row.astype(jnp.float32)
    wanted = jnp.concatenate([named, pulled(named, "c", 1)])
    wanted = jnp.broadcast_to(wanted[:, None], (2 * per_shard, 128))

    steps = jnp.arange(4, dtype=jnp.int32)
    rows = jnp.arange(count, dtype=jnp.int32)

    def numbers(zl, y, x):
        shard = ((zl * 4 + y % 4) * 4 + x % 4) * 2 + c
        held = (shard * per_shard + zh * count)[:, :, None] + rows
        return held.reshape(1, -1).astype(jnp.float32)

    near_held = numbers(zl, (y + steps)[:, None], (x + steps)[None, :])
    far_held = numbers(1 - zl, (y + steps)[None, :], (x + steps)[:, None])

    grads, near_weights = image_terms(chip_images, wanted, near_held, near, None)
    grads, far_weights = image_terms(chip_images, wanted, far_held, far, grads)
    grads, near_weights = lax.optimization_barrier((grads, near_weights))
    near_sums = caption_terms(chip_images, near_weights, near[0].shape)
    shard_grad = grads[0] + pulled(grads[1], "c", 1)
    shard_grad, far_weights = lax.optimization_barrier((shard_grad, far_weights))
    far_sums = caption_terms(chip_images, far_weights, far[0].shape)

    image_grad = jnp.sum(
        lax.all_to_all(shard_grad, "zh", 0, 0, tiled=True).reshape(4, count, width), axis=0
    )
    near_line = returned(near_sums, "y")
    far_line = returned(far_sums, "x")
    near_line, far_line, image_grad = lax.optimization_barrier((near_line, far_line, image_grad))
    far_sum = returned(line_parts(far_line), "y")
    caption_grad = returned(line_parts(near_line), "x") + pulled(far_sum, "zl", 1)
    raw_grad = unit_back(images, image_scale, image_grad)
    pooled_grad = product(shared(raw_grad), projection, ((1,), (1,)))

    text_grad = unit_back(captions, caption_scale, caption_grad)
    return (pooled_grad, text_grad)


def solution(mesh):
    grid = Mesh(mesh.devices.reshape(tuple(SIZES.values())), tuple(SIZES))
    return jax.shard_map(
        local,
        mesh=grid,
        in_specs=(P(DP, "zh"), P("zh", None), P((*DP, "zh"), None), P(DP)),
        out_specs=(P(DP, "zh"), P((*DP, "zh"), None)),
        check_vma=False,
    )
```

time: 184 us -> 167 us (0.908)
  waiting for transfers between devices: 78.5 us -> 60.2 us
  matrix products: 2.54 us -> 4.94 us
  starting transfers between devices: 71.3 us -> 68.9 us
    ppermute x32 -> x29, waiting for transfers between devices: 78.5 us -> 55.4 us  [pulled(): lax.ppermute(value, axis, [((i + steps) % count, i) for i in range(count)])]
    ppermute x32 -> x29, starting transfers between devices: 59.1 us -> 43.3 us  [pulled(): lax.ppermute(value, axis, [((i + steps) % count, i) for i in range(count)])]
    all_to_all x2 -> x4, starting transfers between devices: 12.2 us -> 25.6 us  [the longest x2 10.3 us: shared(): return lax.all_to_all(rows, 'zh', 0, 0, tiled=True)]
    all_to_all x2 -> x4, waiting for transfers between devices: 0.01 us -> 4.78 us  [the longest x2 2.78 us: shared(): return lax.all_to_all(rows, 'zh', 0, 0, tiled=True)]
    unnamed x7 -> x0, other arithmetic: 4.22 us -> none
    add x4 -> x3, other arithmetic: 0.15 us -> 4.02 us  [returned(): return sum((pulled(terms[k], axis, -k) for k in (1, 2, 3)), terms[0])]
    dot_general x2, matrix products: 2.54 us -> 4.94 us  [product(): lax.dot_general(left, right, (dims, ((), ())), precision=lax.Precision.HI...]
    unnamed x34 -> x20, local copies, waits for them, and re-layouts: 5.31 us -> 4.45 us
  transfers between devices with their start and end apart: 34 -> 33, of which waited for: 13 -> 16; matrix products, arithmetic and copies ran while one was open for 5% -> 7% of each run, Pallas kernels for 7% -> 5%
where the time goes in v1:
time: 167 us; the launch traced here: 166 us
  starting transfers between devices  68.9 us (41%)
  waiting for transfers between devices  60.2 us (36%)
  Pallas kernels  12.5 us (7%)
  other arithmetic  10.8 us (6%)
  local copies, waits for them, and re-layouts  7.93 us (5%)
  matrix products  4.94 us (3%)
    ppermute x29, waiting for transfers between devices, pulled(): lax.ppermute(value, axis, [((i + steps) % count, i) for i in range(count)])  55.4 us
    ppermute x29, starting transfers between devices, pulled(): lax.ppermute(value, axis, [((i + steps) % count, i) for i in range(count)])  43.3 us
    pallas_call x4, Pallas kernels, called(): pl.pallas_call(kernel, out_shape=[jax.ShapeDtypeStruct(shape, jnp.float32...  12.5 us
    all_to_all x2, starting transfers between devices, shared(): return lax.all_to_all(rows, 'zh', 0, 0, tiled=True)  10.3 us
    all_to_all x1, starting transfers between devices, local(): lax.all_to_all(partial, 'zh', 0, 0, tiled=True).reshape(4, count, width)  8.28 us
    all_to_all x1, starting transfers between devices, local(): lax.all_to_all(shard_grad, 'zh', 0, 0, tiled=True).reshape(4, count, width)  7.06 us
    dot_general x2, matrix products, product(): lax.dot_general(left, right, (dims, ((), ())), precision=lax.Precision.HI...  4.94 us
    unnamed x20, local copies, waits for them, and re-layouts  4.45 us
  transfers between devices with their start and end apart: 33, of which 16 were waited for; matrix products, arithmetic and copies ran while one was open for 7% of the time, Pallas kernels for 5%

profile of v1, /device:TPU:6, one launch (start us, length us, event | category | flops | bytes accessed | tf_op | source)
XLA Modules:
  0.0 166.0 jit_solution(7687744362880190583)
XLA Ops:
  4.8 3.0 %fusion.4 = f32[128,1152]{1,0:T(8,128)} fusion(f32[128,288]{0,1:T(8,128)} %param.4, f32[288,1152]{1,0:T(8,128)S(1)} %copy-done), kind=kOutput, calls=%fused_computation.33 | convolution fusion | flops 509607936 | bytes 2064384 | tf_op jit(solution)/shard_map/dot_general | solution.py:30
  8.6 8.3 %all-to-all-start = ((f32[4,32,1152]{2,1,0:T(8,128)}), f32[4,32,1152]{2,1,0:T(8,128)S(1)}, u32[]{:S(2)}, u32[]{:S(2)}) async-start(f32[4,32,1152]{2,1,0:T(8,128)} %bitcast), calls=%async_computation | async-start | bytes 1179648 | tf_op jit(solution)/shard_map/all_to_all | solution.py:127
  18.9 2.1 %collective-permute-start.2 = (f32[32,1152]{1,0:T(8,128)S(1)}, f32[32,1152]{1,0:T(8,128)S(1)}, u32[]{:S(2)}, u32[]{:S(2)}) collective-permute-start(f32[32,1152]{1,0:T(8,128)S(1)} %broadcast_multiply_fusion.1), channel_id=1, source_target_pairs={{24,0},{0,8},{8,16},{16,24},{25,1},{1,9},{9,17},{17,25},{26,2},{2,... | collective-permute-start | bytes 442376 | tf_op jit(solution)/shard_map/ppermute | solution.py:18
  21.0 3.0 %collective-permute-start.4 = (f32[32,1152]{1,0:T(8,128)S(1)}, f32[32,1152]{1,0:T(8,128)S(1)}, u32[]{:S(2)}, u32[]{:S(2)}) collective-permute-start(f32[32,1152]{1,0:T(8,128)S(1)} %collective-permute-done.3), channel_id=1, source_target_pairs={{32,0},{64,32},{96,64},{0,96},{33,1},{65,33},{97,65},{1,97},{34,2}... | collective-permute-start | bytes 442376 | tf_op jit(solution)/shard_map/ppermute | solution.py:18
  28.3 2.4 %collective-permute-done.5 = f32[32,1152]{1,0:T(8,128)S(1)} collective-permute-done((f32[32,1152]{1,0:T(8,128)S(1)}, f32[32,1152]{1,0:T(8,128)S(1)}, u32[]{:S(2)}, u32[]{:S(2)}) %collective-permute-start.5) | collective-permute-done | bytes 147488 | tf_op jit(solution)/shard_map/ppermute | solution.py:18
  34.1 6.5 %all-to-all-start.1 = ((f32[4,32,1152]{2,1,0:T(8,128)}), f32[4,32,1152]{2,1,0:T(8,128)S(1)}, u32[]{:S(2)}, u32[]{:S(2)}) async-start(f32[4,32,1152]{2,1,0:T(8,128)} %broadcast_in_dim.6), calls=%async_computation.1 | async-start | bytes 1179648 | tf_op jit(solution)/shard_map/all_to_all | solution.py:110
  46.2 17.9 %collective-permute-done.12.refs_5_ = f32[128,1152]{1,0:T(8,128)S(1)} collective-permute-done((f32[128,1152]{1,0:T(8,128)}, f32[128,1152]{1,0:T(8,128)S(1)}, u32[]{:S(2)}, u32[]{:S(2)}) %collective-permute-start.12) | collective-permute-done | bytes 589856 | tf_op jit(solution)/shard_map/ppermute | solution.py:18
  69.0 3.8 %image_terms.2 = (f32[128,1152]{1,0:T(8,128)S(1)}, f32[128,1152]{1,0:T(8,128)S(1)}, f32[256,512]{1,0:T(8,128)S(1)}) custom-call(f32[128,1152]{1,0:T(8,128)S(1)} %bitcast.9, f32[128,1152]{1,0:T(8,128)S(1)} %collective-permute-done.7.refs_1_.other, f32[256,128]{1,0:T(8,128)S(1)} %broadcast_in_dim.7.refs_2_, f32[1,512]{1,0:T(1,128)S(1)} %convert_element_type.17.refs_3_, ...), custom_call_target="tpu_custom_call" | custom-call | tf_op jit(solution)/shard_map/image_terms/pallas_call | solution.py:87
  73.6 2.5 %collective-permute-done.9.refs_5_ = f32[128,1152]{1,0:T(8,128)} collective-permute-done((f32[128,1152]{1,0:T(8,128)S(1)}, f32[128,1152]{1,0:T(8,128)}, u32[]{:S(2)}, u32[]{:S(2)}) %collective-permute-start.9) | collective-permute-done | bytes 589856 | tf_op jit(solution)/shard_map/ppermute | solution.py:18
  76.2 4.0 %image_terms.3 = (f32[128,1152]{1,0:T(8,128)S(1)}, f32[128,1152]{1,0:T(8,128)S(1)}, f32[256,512]{1,0:T(8,128)S(1)}) custom-call(f32[128,1152]{1,0:T(8,128)S(1)} %bitcast.10, f32[128,1152]{1,0:T(8,128)S(1)} %collective-permute-done.7.refs_1_.other, f32[256,128]{1,0:T(8,128)S(1)} %broadcast_in_dim.7.refs_2_, f32[1,512]{1,0:T(1,128)S(1)} %convert_element_type.15.refs_3_, ...), custom_call_target="tpu_custom_call" | custom-call | tf_op jit(solution)/shard_map/image_terms/pallas_call | solution.py:87
  80.3 2.2 %caption_terms.2 = (f32[128,1152]{1,0:T(8,128)S(1)}, f32[128,1152]{1,0:T(8,128)S(1)}, f32[128,1152]{1,0:T(8,128)}, f32[128,1152]{1,0:T(8,128)}) custom-call(f32[128,1152]{1,0:T(8,128)S(1)} %bitcast.11, f32[128,1152]{1,0:T(8,128)S(1)} %collective-permute-done.7.refs_1_.other, f32[256,512]{1,0:T(8,128)S(1)} %get-tuple-element.39.weights), custom_call_target="tpu_custom_call" | custom-call | tf_op jit(solution)/shard_map/caption_terms/pallas_call | solution.py:87
  82.5 5.0 %collective-permute-start.16 = (f32[128,1152]{1,0:T(8,128)}, f32[128,1152]{1,0:T(8,128)}, u32[]{:S(2)}, u32[]{:S(2)}) collective-permute-start(f32[128,1152]{1,0:T(8,128)} %get-tuple-element.42), channel_id=1, source_target_pairs={{64,0},{96,32},{0,64},{32,96},{65,1},{97,33},{1,65},{33,97},{66,2}... | collective-permute-start | bytes 1769480 | tf_op jit(solution)/shard_map/ppermute | solution.py:18
  88.4 2.4 %caption_terms.3 = (f32[128,1152]{1,0:T(8,128)S(1)}, f32[128,1152]{1,0:T(8,128)}, f32[128,1152]{1,0:T(8,128)}, f32[128,1152]{1,0:T(8,128)}) custom-call(f32[128,1152]{1,0:T(8,128)S(1)} %bitcast.12, f32[128,1152]{1,0:T(8,128)S(1)} %collective-permute-done.7.refs_1_.other, f32[256,512]{1,0:T(8,128)S(1)} %get-tuple-element.47.weights), custom_call_target="tpu_custom_call" | custom-call | tf_op jit(solution)/shard_map/caption_terms/pallas_call | solution.py:87
  93.4 6.7 %collective-permute-done.15 = f32[128,1152]{1,0:T(8,128)S(1)} collective-permute-done((f32[128,1152]{1,0:T(8,128)S(1)}, f32[128,1152]{1,0:T(8,128)S(1)}, u32[]{:S(2)}, u32[]{:S(2)}) %collective-permute-start.15) | collective-permute-done | bytes 589856 | tf_op jit(solution)/shard_map/ppermute | solution.py:18
  100.9 7.1 %all-to-all-start.2 = ((f32[4,32,1152]{2,1,0:T(8,128)}), f32[4,32,1152]{2,1,0:T(8,128)}, u32[]{:S(2)}, u32[]{:S(2)}) async-start(f32[4,32,1152]{2,1,0:T(8,128)} %bitcast.13), calls=%async_computation.2 | async-start | bytes 1179648 | tf_op jit(solution)/shard_map/all_to_all | solution.py:163
  108.0 6.0 %collective-permute-done.16 = f32[128,1152]{1,0:T(8,128)} collective-permute-done((f32[128,1152]{1,0:T(8,128)}, f32[128,1152]{1,0:T(8,128)}, u32[]{:S(2)}, u32[]{:S(2)}) %collective-permute-start.16) | collective-permute-done | bytes 589856 | tf_op jit(solution)/shard_map/ppermute | solution.py:18
  115.4 5.9 %collective-permute-done.21 = f32[128,1152]{1,0:T(8,128)} collective-permute-done((f32[128,1152]{1,0:T(8,128)}, f32[128,1152]{1,0:T(8,128)}, u32[]{:S(2)}, u32[]{:S(2)}) %collective-permute-start.21) | collective-permute-done | bytes 589856 | tf_op jit(solution)/shard_map/ppermute | solution.py:18
  126.5 3.5 %collective-permute-start.26 = (f32[32,1152]{1,0:T(8,128)}, f32[32,1152]{1,0:T(8,128)}, u32[]{:S(2)}, u32[]{:S(2)}) collective-permute-start(f32[32,1152]{1,0:T(8,128)} %get-tuple-element.63), channel_id=1, source_target_pairs={{64,0},{96,32},{0,64},{32,96},{65,1},{97,33},{1,65},{33,97},{66,2}... | collective-permute-start | bytes 442376 | tf_op jit(solution)/shard_map/ppermute | solution.py:18
  130.8 4.5 %collective-permute-start.22 = (f32[32,1152]{1,0:T(8,128)}, f32[32,1152]{1,0:T(8,128)S(1)}, u32[]{:S(2)}, u32[]{:S(2)}) collective-permute-start(f32[32,1152]{1,0:T(8,128)} %get-tuple-element.58), channel_id=1, source_target_pairs={{24,0},{0,8},{8,16},{16,24},{25,1},{1,9},{9,17},{17,25},{26,2},{2,... | collective-permute-start | bytes 442376 | tf_op jit(solution)/shard_map/ppermute | solution.py:18
  135.3 8.7 %collective-permute-start.23 = (f32[32,1152]{1,0:T(8,128)}, f32[32,1152]{1,0:T(8,128)S(1)}, u32[]{:S(2)}, u32[]{:S(2)}) collective-permute-start(f32[32,1152]{1,0:T(8,128)} %get-tuple-element.60), channel_id=1, source_target_pairs={{16,0},{24,8},{0,16},{8,24},{17,1},{25,9},{1,17},{9,25},{18,2},{26... | collective-permute-start | bytes 442376 | tf_op jit(solution)/shard_map/ppermute | solution.py:18
  145.2 3.7 %all-to-all-start.3 = ((f32[4,32,1152]{2,1,0:T(8,128)}), f32[4,32,1152]{2,1,0:T(8,128)S(1)}, u32[]{:S(2)}, u32[]{:S(2)}) async-start(f32[4,32,1152]{2,1,0:T(8,128)} %broadcast_in_dim.8), calls=%async_computation.3 | async-start | bytes 1179648 | tf_op jit(solution)/shard_map/all_to_all | solution.py:110
  151.6 3.8 %collective-permute-done.24 = f32[32,1152]{1,0:T(8,128)S(1)} collective-permute-done((f32[32,1152]{1,0:T(8,128)}, f32[32,1152]{1,0:T(8,128)S(1)}, u32[]{:S(2)}, u32[]{:S(2)}) %collective-permute-start.24) | collective-permute-done | bytes 147488 | tf_op jit(solution)/shard_map/ppermute | solution.py:18
  155.5 4.9 %collective-permute-done.28 = f32[32,1152]{1,0:T(8,128)S(1)} collective-permute-done((f32[32,1152]{1,0:T(8,128)S(1)}, f32[32,1152]{1,0:T(8,128)S(1)}, u32[]{:S(2)}, u32[]{:S(2)}) %collective-permute-start.28) | collective-permute-done | bytes 147488 | tf_op jit(solution)/shard_map/ppermute | solution.py:18
  161.4 2.8 %all-to-all-done.3 = f32[4,32,1152]{2,1,0:T(8,128)S(1)} async-done(((f32[4,32,1152]{2,1,0:T(8,128)}), f32[4,32,1152]{2,1,0:T(8,128)S(1)}, u32[]{:S(2)}, u32[]{:S(2)}) %all-to-all-start.3) | async-done | bytes 589856 | tf_op jit(solution)/shard_map/all_to_all | solution.py:110
  (100 shorter events, 44.3 us)
Async XLA Ops:
  8.6 24.3 %all-to-all-start = ((f32[4,32,1152]{2,1,0:T(8,128)}), f32[4,32,1152]{2,1,0:T(8,128)S(1)}, u32[]{:S(2)}, u32[]{:S(2)}) async-start(f32[4,32,1152]{2,1,0:T(8,128)} %bitcast), calls=%async_computation | async-start | bytes 1179648 | tf_op jit(solution)/shard_map/all_to_all | solution.py:127
  16.9 8.8 %collective-permute-start = (f32[32,1152]{1,0:T(8,128)S(1)}, f32[32,1152]{1,0:T(8,128)S(1)}, u32[]{:S(2)}, u32[]{:S(2)}) collective-permute-start(f32[32,1152]{1,0:T(8,128)S(1)} %broadcast_multiply_fusion.1), channel_id=1, source_target_pairs={{8,0},{16,8},{24,16},{0,24},{9,1},{17,9},{25,17},{1,25},{10,2},{18... | collective-permute-start | bytes 442376 | tf_op jit(solution)/shard_map/ppermute | solution.py:18
  17.8 9.6 %collective-permute-start.1 = (f32[32,1152]{1,0:T(8,128)S(1)}, f32[32,1152]{1,0:T(8,128)S(1)}, u32[]{:S(2)}, u32[]{:S(2)}) collective-permute-start(f32[32,1152]{1,0:T(8,128)S(1)} %broadcast_multiply_fusion.1), channel_id=1, source_target_pairs={{16,0},{24,8},{0,16},{8,24},{17,1},{25,9},{1,17},{9,25},{18,2},{26... | collective-permute-start | bytes 442376 | tf_op jit(solution)/shard_map/ppermute | solution.py:18
  34.1 31.8 %all-to-all-start.1 = ((f32[4,32,1152]{2,1,0:T(8,128)}), f32[4,32,1152]{2,1,0:T(8,128)S(1)}, u32[]{:S(2)}, u32[]{:S(2)}) async-start(f32[4,32,1152]{2,1,0:T(8,128)} %broadcast_in_dim.6), calls=%async_computation.1 | async-start | bytes 1179648 | tf_op jit(solution)/shard_map/all_to_all | solution.py:110
  40.6 23.6 %collective-permute-start.12 = (f32[128,1152]{1,0:T(8,128)}, f32[128,1152]{1,0:T(8,128)S(1)}, u32[]{:S(2)}, u32[]{:S(2)}) collective-permute-start(f32[128,1152]{1,0:T(8,128)} %pad_maximum_fusion.refs_4_), channel_id=1, source_target_pairs={{32,0},{64,32},{96,64},{0,96},{33,1},{65,33},{97,65},{1,97},{34,2}... | collective-permute-start | bytes 1769480 | tf_op jit(solution)/shard_map/ppermute | solution.py:18
  42.0 23.8 %collective-permute-start.13 = (f32[128,1152]{1,0:T(8,128)}, f32[128,1152]{1,0:T(8,128)}, u32[]{:S(2)}, u32[]{:S(2)}) collective-permute-start(f32[128,1152]{1,0:T(8,128)} %pad_maximum_fusion.refs_4_), channel_id=1, source_target_pairs={{64,0},{96,32},{0,64},{32,96},{65,1},{97,33},{1,65},{33,97},{66,2}... | collective-permute-start | bytes 1769480 | tf_op jit(solution)/shard_map/ppermute | solution.py:18
  42.7 25.2 %collective-permute-start.14 = (f32[128,1152]{1,0:T(8,128)}, f32[128,1152]{1,0:T(8,128)}, u32[]{:S(2)}, u32[]{:S(2)}) collective-permute-start(f32[128,1152]{1,0:T(8,128)} %pad_maximum_fusion.refs_4_), channel_id=1, source_target_pairs={{96,0},{0,32},{32,64},{64,96},{97,1},{1,33},{33,65},{65,97},{98,2}... | collective-permute-start | bytes 1769480 | tf_op jit(solution)/shard_map/ppermute | solution.py:18
  43.7 29.9 %collective-permute-start.10 = (f32[128,1152]{1,0:T(8,128)S(1)}, f32[128,1152]{1,0:T(8,128)}, u32[]{:S(2)}, u32[]{:S(2)}) collective-permute-start(f32[128,1152]{1,0:T(8,128)S(1)} %pad_maximum_fusion.1.refs_4_), channel_id=1, source_target_pairs={{16,0},{24,8},{0,16},{8,24},{17,1},{25,9},{1,17},{9,25},{18,2},{26... | collective-permute-start | bytes 1769480 | tf_op jit(solution)/shard_map/ppermute | solution.py:18
  45.0 28.7 %collective-permute-start.11 = (f32[128,1152]{1,0:T(8,128)S(1)}, f32[128,1152]{1,0:T(8,128)}, u32[]{:S(2)}, u32[]{:S(2)}) collective-permute-start(f32[128,1152]{1,0:T(8,128)S(1)} %pad_maximum_fusion.1.refs_4_), channel_id=1, source_target_pairs={{24,0},{0,8},{8,16},{16,24},{25,1},{1,9},{9,17},{17,25},{26,2},{2,... | collective-permute-start | bytes 1769480 | tf_op jit(solution)/shard_map/ppermute | solution.py:18
  65.0 11.2 %collective-permute-start.9 = (f32[128,1152]{1,0:T(8,128)S(1)}, f32[128,1152]{1,0:T(8,128)}, u32[]{:S(2)}, u32[]{:S(2)}) collective-permute-start(f32[128,1152]{1,0:T(8,128)S(1)} %pad_maximum_fusion.1.refs_4_), channel_id=1, source_target_pairs={{8,0},{16,8},{24,16},{0,24},{9,1},{17,9},{25,17},{1,25},{10,2},{18... | collective-permute-start | bytes 1769480 | tf_op jit(solution)/shard_map/ppermute | solution.py:18
  82.5 17.5 %collective-permute-start.15 = (f32[128,1152]{1,0:T(8,128)S(1)}, f32[128,1152]{1,0:T(8,128)S(1)}, u32[]{:S(2)}, u32[]{:S(2)}) collective-permute-start(f32[128,1152]{1,0:T(8,128)S(1)} %get-tuple-element.41), channel_id=1, source_target_pairs={{96,0},{0,32},{32,64},{64,96},{97,1},{1,33},{33,65},{65,97},{98,2}... | collective-permute-start | bytes 1769480 | tf_op jit(solution)/shard_map/ppermute | solution.py:18
  82.5 31.5 %collective-permute-start.16 = (f32[128,1152]{1,0:T(8,128)}, f32[128,1152]{1,0:T(8,128)}, u32[]{:S(2)}, u32[]{:S(2)}) collective-permute-start(f32[128,1152]{1,0:T(8,128)} %get-tuple-element.42), channel_id=1, source_target_pairs={{64,0},{96,32},{0,64},{32,96},{65,1},{97,33},{1,65},{33,97},{66,2}... | collective-permute-start | bytes 1769480 | tf_op jit(solution)/shard_map/ppermute | solution.py:18
  87.5 26.4 %collective-permute-start.17 = (f32[128,1152]{1,0:T(8,128)}, f32[128,1152]{1,0:T(8,128)}, u32[]{:S(2)}, u32[]{:S(2)}) collective-permute-start(f32[128,1152]{1,0:T(8,128)} %get-tuple-element.43), channel_id=1, source_target_pairs={{32,0},{64,32},{96,64},{0,96},{33,1},{65,33},{97,65},{1,97},{34,2}... | collective-permute-start | bytes 1769480 | tf_op jit(solution)/shard_map/ppermute | solution.py:18
  91.7 23.7 %collective-permute-start.19 = (f32[128,1152]{1,0:T(8,128)}, f32[128,1152]{1,0:T(8,128)}, u32[]{:S(2)}, u32[]{:S(2)}) collective-permute-start(f32[128,1152]{1,0:T(8,128)} %get-tuple-element.49), channel_id=1, source_target_pairs={{24,0},{0,8},{8,16},{16,24},{25,1},{1,9},{9,17},{17,25},{26,2},{2,... | collective-permute-start | bytes 1769480 | tf_op jit(solution)/shard_map/ppermute | solution.py:18
  91.7 23.7 %collective-permute-start.20 = (f32[128,1152]{1,0:T(8,128)}, f32[128,1152]{1,0:T(8,128)}, u32[]{:S(2)}, u32[]{:S(2)}) collective-permute-start(f32[128,1152]{1,0:T(8,128)} %get-tuple-element.50), channel_id=1, source_target_pairs={{16,0},{24,8},{0,16},{8,24},{17,1},{25,9},{1,17},{9,25},{18,2},{26... | collective-permute-start | bytes 1769480 | tf_op jit(solution)/shard_map/ppermute | solution.py:18
  100.9 20.4 %collective-permute-start.21 = (f32[128,1152]{1,0:T(8,128)}, f32[128,1152]{1,0:T(8,128)}, u32[]{:S(2)}, u32[]{:S(2)}) collective-permute-start(f32[128,1152]{1,0:T(8,128)} %get-tuple-element.51), channel_id=1, source_target_pairs={{8,0},{16,8},{24,16},{0,24},{9,1},{17,9},{25,17},{1,25},{10,2},{18... | collective-permute-start | bytes 1769480 | tf_op jit(solution)/shard_map/ppermute | solution.py:18
  100.9 23.2 %all-to-all-start.2 = ((f32[4,32,1152]{2,1,0:T(8,128)}), f32[4,32,1152]{2,1,0:T(8,128)}, u32[]{:S(2)}, u32[]{:S(2)}) async-start(f32[4,32,1152]{2,1,0:T(8,128)} %bitcast.13), calls=%async_computation.2 | async-start | bytes 1179648 | tf_op jit(solution)/shard_map/all_to_all | solution.py:163
  126.0 22.9 %collective-permute-start.25 = (f32[32,1152]{1,0:T(8,128)}, f32[32,1152]{1,0:T(8,128)}, u32[]{:S(2)}, u32[]{:S(2)}) collective-permute-start(f32[32,1152]{1,0:T(8,128)} %get-tuple-element.61), channel_id=1, source_target_pairs={{96,0},{0,32},{32,64},{64,96},{97,1},{1,33},{33,65},{65,97},{98,2}... | collective-permute-start | bytes 442376 | tf_op jit(solution)/shard_map/ppermute | solution.py:18
  126.5 22.4 %collective-permute-start.26 = (f32[32,1152]{1,0:T(8,128)}, f32[32,1152]{1,0:T(8,128)}, u32[]{:S(2)}, u32[]{:S(2)}) collective-permute-start(f32[32,1152]{1,0:T(8,128)} %get-tuple-element.63), channel_id=1, source_target_pairs={{64,0},{96,32},{0,64},{32,96},{65,1},{97,33},{1,65},{33,97},{66,2}... | collective-permute-start | bytes 442376 | tf_op jit(solution)/shard_map/ppermute | solution.py:18
  130.0 18.9 %collective-permute-start.27 = (f32[32,1152]{1,0:T(8,128)}, f32[32,1152]{1,0:T(8,128)}, u32[]{:S(2)}, u32[]{:S(2)}) collective-permute-start(f32[32,1152]{1,0:T(8,128)} %get-tuple-element.62), channel_id=1, source_target_pairs={{32,0},{64,32},{96,64},{0,96},{33,1},{65,33},{97,65},{1,97},{34,2}... | collective-permute-start | bytes 442376 | tf_op jit(solution)/shard_map/ppermute | solution.py:18
  130.8 20.8 %collective-permute-start.22 = (f32[32,1152]{1,0:T(8,128)}, f32[32,1152]{1,0:T(8,128)S(1)}, u32[]{:S(2)}, u32[]{:S(2)}) collective-permute-start(f32[32,1152]{1,0:T(8,128)} %get-tuple-element.58), channel_id=1, source_target_pairs={{24,0},{0,8},{8,16},{16,24},{25,1},{1,9},{9,17},{17,25},{26,2},{2,... | collective-permute-start | bytes 442376 | tf_op jit(solution)/shard_map/ppermute | solution.py:18
  135.3 16.3 %collective-permute-start.23 = (f32[32,1152]{1,0:T(8,128)}, f32[32,1152]{1,0:T(8,128)S(1)}, u32[]{:S(2)}, u32[]{:S(2)}) collective-permute-start(f32[32,1152]{1,0:T(8,128)} %get-tuple-element.60), channel_id=1, source_target_pairs={{16,0},{24,8},{0,16},{8,24},{17,1},{25,9},{1,17},{9,25},{18,2},{26... | collective-permute-start | bytes 442376 | tf_op jit(solution)/shard_map/ppermute | solution.py:18
  145.2 19.0 %all-to-all-start.3 = ((f32[4,32,1152]{2,1,0:T(8,128)}), f32[4,32,1152]{2,1,0:T(8,128)S(1)}, u32[]{:S(2)}, u32[]{:S(2)}) async-start(f32[4,32,1152]{2,1,0:T(8,128)} %broadcast_in_dim.8), calls=%async_computation.3 | async-start | bytes 1179648 | tf_op jit(solution)/shard_map/all_to_all | solution.py:110
  150.0 10.4 %collective-permute-start.28 = (f32[32,1152]{1,0:T(8,128)S(1)}, f32[32,1152]{1,0:T(8,128)S(1)}, u32[]{:S(2)}, u32[]{:S(2)}) collective-permute-start(f32[32,1152]{1,0:T(8,128)S(1)} %add_add_fusion.2), channel_id=1, source_target_pairs={{128,0},{0,128},{129,1},{1,129},{130,2},{2,130},{131,3},{3,131},{1... | collective-permute-start | bytes 442376 | tf_op jit(solution)/shard_map/ppermute | solution.py:18
  (19 other events, 107.8 us)

commit v2 on v1

--- a/solution.py
+++ b/solution.py
@@ -11,6 +11,7 @@
 
 SIZES = {"zl": 2, "y": 4, "x": 4, "c": 2, "zh": 4}
 DP = ("zl", "y", "x", "c")
+LONG = pl.CostEstimate(flops=30_000_000_000, transcendentals=0, bytes_accessed=100_000_000)
 
 
 def pulled(value, axis, steps):
@@ -34,11 +35,6 @@
         precision=lax.Precision.HIGHEST,
         preferred_element_type=jnp.float32,
     )
-
-
-def unit_rows(raw):
-    scale = lax.rsqrt(jnp.sum(raw * raw, axis=1) + NORM_EPS)
-    return (raw * scale[:, None], scale)
 
 
 def unit_back(unit, scale, grad):
@@ -83,12 +79,13 @@
         ref[...] = caption_terms[k * size : (k + 1) * size]
 
 
-def called(kernel, name, shapes, *args):
+def called(kernel, name, shapes, *args, cost=None):
     return pl.pallas_call(
         kernel,
         out_shape=[jax.ShapeDtypeStruct(shape, jnp.float32) for shape in shapes],
         compiler_params=pltpu.CompilerParams(vmem_limit_bytes=48 << 20),
         name=name,
+        cost_estimate=cost,
     )(*args)
 
 
@@ -101,13 +98,42 @@
     return out[:2], out[2]
 
 
-def caption_terms(images, weights, shape):
-    return called(caption_kernel, "caption_terms", [shape] * 4, *images, weights)
-
-
-def shared(rows):
-    rows = jnp.broadcast_to(rows[None], (4, *rows.shape)).reshape(-1, rows.shape[1])
-    return lax.all_to_all(rows, "zh", 0, 0, tiled=True)
+def caption_terms(images, weights, shape, cost=None):
+    return called(caption_kernel, "caption_terms", [shape] * 4, *images, weights, cost=cost)
+
+
+def sum_kernel(a, b, c, d, out):
+    out[...] = (a[...] + b[...]) + (c[...] + d[...])
+
+
+def summed(parts, cost=None):
+    return called(sum_kernel, "line_sum", [parts[0].shape], *parts, cost=cost)[0]
+
+
+def unit_kernel(raw, unit, scale):
+    rows = raw[...]
+    factor = lax.rsqrt(jnp.sum(rows * rows, axis=1, keepdims=True) + NORM_EPS)
+    unit[...] = rows * factor
+    scale[...] = jnp.broadcast_to(factor, scale.shape)
+
+
+def image_unit_kernel(raw, unit, scale, sent):
+    size = unit.shape[0]
+    rows = sum(raw[k * size : (k + 1) * size] for k in range(4))
+    factor = lax.rsqrt(jnp.sum(rows * rows, axis=1, keepdims=True) + NORM_EPS)
+    unit[...] = rows * factor
+    scale[...] = jnp.broadcast_to(factor, scale.shape)
+    for k in range(4):
+        sent[k * size : (k + 1) * size] = rows * factor
+
+
+def raw_kernel(terms, unit, scale, sent):
+    size = unit.shape[0]
+    grad = sum(terms[k * size : (k + 1) * size] for k in range(4))
+    dot = jnp.sum(unit[...] * grad, axis=1, keepdims=True)
+    raw = scale[:, :1] * (grad - unit[...] * dot)
+    for k in range(4):
+        sent[k * size : (k + 1) * size] = raw
 
 
 def line_parts(line):
@@ -119,21 +145,23 @@
     zl, y, x, c, zh = (lax.axis_index(a) for a in ("zl", "y", "x", "c", "zh"))
     per_shard = pooled_rows.shape[0]
     count, width = text_rows.shape
-    captions, caption_scale = unit_rows(text_rows)
+    captions, caption_scale = called(
+        unit_kernel, "caption_rows", [(count, width), (count, 128)], text_rows
+    )
 
     partial = product(pooled_rows, projection, ((1,), (0,)))
     partial, moved = lax.optimization_barrier((partial, pulled(captions, "zl", 1)))
-    projected = jnp.sum(
-        lax.all_to_all(partial, "zh", 0, 0, tiled=True).reshape(4, count, width), axis=0
-    )
+    arrived = lax.all_to_all(partial, "zh", 0, 0, tiled=True)
 
     near_line = jnp.concatenate(pulls(captions, "x"))
     far_line = jnp.concatenate(pulls(moved, "y"))
-    near_line, far_line, projected = lax.optimization_barrier((near_line, far_line, projected))
+    near_line, far_line, arrived = lax.optimization_barrier((near_line, far_line, arrived))
     near = pulls(near_line, "y")
     far = pulls(far_line, "x")
-    images, image_scale = unit_rows(projected)
-    shard_images = shared(images)
+    images, image_scale, sent = called(
+        image_unit_kernel, "image_rows", [(count, width), (count, 128), partial.shape], arrived
+    )
+    shard_images = lax.all_to_all(sent, "zh", 0, 0, tiled=True)
     chip_images = [shard_images, pulled(shard_images, "c", 1)]
 
     named = caption_row.astype(jnp.float32)
@@ -153,24 +181,35 @@
 
     grads, near_weights = image_terms(chip_images, wanted, near_held, near, None)
     grads, far_weights = image_terms(chip_images, wanted, far_held, far, grads)
-    grads, near_weights = lax.optimization_barrier((grads, near_weights))
-    near_sums = caption_terms(chip_images, near_weights, near[0].shape)
+    grads, far_weights = lax.optimization_barrier((grads, far_weights))
+    far_sums = caption_terms(chip_images, far_weights, far[0].shape)
     shard_grad = grads[0] + pulled(grads[1], "c", 1)
-    shard_grad, far_weights = lax.optimization_barrier((shard_grad, far_weights))
-    far_sums = caption_terms(chip_images, far_weights, far[0].shape)
-
-    image_grad = jnp.sum(
-        lax.all_to_all(shard_grad, "zh", 0, 0, tiled=True).reshape(4, count, width), axis=0
-    )
-    near_line = returned(near_sums, "y")
-    far_line = returned(far_sums, "x")
-    near_line, far_line, image_grad = lax.optimization_barrier((near_line, far_line, image_grad))
-    far_sum = returned(line_parts(far_line), "y")
-    caption_grad = returned(line_parts(near_line), "x") + pulled(far_sum, "zl", 1)
-    raw_grad = unit_back(images, image_scale, image_grad)
-    pooled_grad = product(shared(raw_grad), projection, ((1,), (1,)))
-
-    text_grad = unit_back(captions, caption_scale, caption_grad)
+    shard_grad, near_weights = lax.optimization_barrier((shard_grad, near_weights))
+    near_sums = caption_terms(chip_images, near_weights, near[0].shape, cost=LONG)
+
+    (sent,) = called(
+        raw_kernel,
+        "image_back",
+        [shard_grad.shape],
+        lax.all_to_all(shard_grad, "zh", 0, 0, tiled=True),
+        images,
+        image_scale,
+    )
+    near_parts = [near_sums[0]] + [pulled(near_sums[k], "y", -k) for k in (1, 2, 3)]
+    far_parts = [far_sums[0]] + [pulled(far_sums[k], "x", -k) for k in (1, 2, 3)]
+    raw_rows = lax.all_to_all(sent, "zh", 0, 0, tiled=True)
+
+    far_parts, sent = lax.optimization_barrier((far_parts, sent))
+    far_line = summed(far_parts, cost=LONG)
+    near_parts, _ = lax.optimization_barrier((near_parts, far_line))
+    far_own, *far_rest = line_parts(far_line)
+    far_rest = [pulled(part, "y", -k) for k, part in enumerate(far_rest, 1)]
+    far_own, raw_rows = lax.optimization_barrier((far_own, raw_rows))
+    pooled_grad = product(raw_rows, projection, ((1,), (1,)))
+    far_sum = sum(far_rest, far_own)
+    near_sum = returned(line_parts(summed(near_parts)), "x")
+    caption_grad = near_sum + pulled(far_sum, "zl", 1)
+    text_grad = unit_back(captions, caption_scale[:, 0], caption_grad)
     return (pooled_grad, text_grad)
 
 

time: 167 us -> 160 us (0.958)
  other arithmetic: 10.8 us -> 4.03 us
  Pallas kernels: 12.5 us -> 17.7 us
  waiting for transfers between devices: 60.2 us -> 55.2 us
  starting transfers between devices: 68.9 us -> 66.7 us
    ppermute x29, waiting for transfers between devices: 55.4 us -> 41.1 us  [pulled(): lax.ppermute(value, axis, [((i + steps) % count, i) for i in range(count)])]
    all_to_all x4, waiting for transfers between devices: 4.78 us -> 14.1 us  [the longest x1 7.38 us: local(): lax.all_to_all(shard_grad, 'zh', 0, 0, tiled=True)]
    ppermute x29, starting transfers between devices: 43.3 us -> 38 us  [pulled(): lax.ppermute(value, axis, [((i + steps) % count, i) for i in range(count)])]
    pallas_call x4 -> x9, Pallas kernels: 12.5 us -> 17.7 us  [called(): pl.pallas_call(kernel, out_shape=[jax.ShapeDtypeStruct(shape, jnp.float32...]
    all_to_all x4, starting transfers between devices: 25.6 us -> 28.6 us  [the longest x1 8.28 us: local(): arrived = lax.all_to_all(partial, 'zh', 0, 0, tiled=True)]
    add x3 -> x1, other arithmetic: 4.02 us -> 1.08 us  [local(): far_sum = sum(far_rest, far_own)]
    reduce_sum x4 -> x0, other arithmetic: 2.39 us -> none  [the longest x2 1.25 us: unit_rows(): scale = lax.rsqrt(jnp.sum(raw * raw, axis=1) + NORM_EPS)]
    unnamed x20 -> x24, local copies, waits for them, and re-layouts: 4.45 us -> 6.36 us
  transfers between devices with their start and end apart: 33 -> 33, of which waited for: 16 -> 13; matrix products, arithmetic and copies ran while one was open for 7% -> 6% of each run, Pallas kernels for 5% -> 8%
where the time goes in v2:
time: 160 us; the launch traced here: 158 us
  starting transfers between devices  66.7 us (42%)
  waiting for transfers between devices  55.2 us (34%)
  Pallas kernels  17.7 us (11%)
  local copies, waits for them, and re-layouts  7.52 us (5%)
  matrix products  5.95 us (4%)
  other arithmetic  4.03 us (3%)
    ppermute x29, waiting for transfers between devices, pulled(): lax.ppermute(value, axis, [((i + steps) % count, i) for i in range(count)])  41.1 us
    ppermute x29, starting transfers between devices, pulled(): lax.ppermute(value, axis, [((i + steps) % count, i) for i in range(count)])  38 us
    pallas_call x9, Pallas kernels, called(): pl.pallas_call(kernel, out_shape=[jax.ShapeDtypeStruct(shape, jnp.float32...  17.7 us
    all_to_all x1, starting transfers between devices, local(): arrived = lax.all_to_all(partial, 'zh', 0, 0, tiled=True)  8.28 us
    all_to_all x1, waiting for transfers between devices, local(): lax.all_to_all(shard_grad, 'zh', 0, 0, tiled=True)  7.38 us
    all_to_all x1, starting transfers between devices, local(): raw_rows = lax.all_to_all(sent, 'zh', 0, 0, tiled=True)  6.92 us
    all_to_all x1, starting transfers between devices, local(): lax.all_to_all(shard_grad, 'zh', 0, 0, tiled=True)  6.92 us
    all_to_all x1, starting transfers between devices, local(): shard_images = lax.all_to_all(sent, 'zh', 0, 0, tiled=True)  6.52 us
  transfers between devices with their start and end apart: 33, of which 13 were waited for; matrix products, arithmetic and copies ran while one was open for 6% of the time, Pallas kernels for 8%

profile of v2, /device:TPU:6, one launch (start us, length us, event | category | flops | bytes accessed | tf_op | source)
XLA Modules:
  0.0 157.9 jit_solution(1659548032204731439)
XLA Ops:
  1.8 2.0 %collective-permute-start.3 = (f32[32,1152]{1,0:T(8,128)S(1)}, f32[32,1152]{1,0:T(8,128)S(1)}, u32[]{:S(2)}, u32[]{:S(2)}) collective-permute-start(f32[32,1152]{1,0:T(8,128)S(1)} %get-tuple-element.38), channel_id=1, source_target_pairs={{128,0},{0,128},{129,1},{1,129},{130,2},{2,130},{131,3},{3,131},{1... | collective-permute-start | bytes 442376 | tf_op jit(solution)/shard_map/ppermute | solution.py:19
  3.8 3.0 %fusion.8 = f32[128,1152]{1,0:T(8,128)} fusion(f32[128,288]{0,1:T(8,128)} %param.4, f32[288,1152]{1,0:T(8,128)S(1)} %copy-done), kind=kOutput, calls=%fused_computation.27 | convolution fusion | flops 509607936 | bytes 2064384 | tf_op jit(solution)/shard_map/dot_general | solution.py:31
  7.6 8.3 %all-to-all-start = ((f32[4,32,1152]{2,1,0:T(8,128)}), f32[4,32,1152]{2,1,0:T(8,128)S(1)}, u32[]{:S(2)}, u32[]{:S(2)}) async-start(f32[4,32,1152]{2,1,0:T(8,128)} %bitcast), calls=%async_computation | async-start | bytes 1179648 | tf_op jit(solution)/shard_map/all_to_all | solution.py:154
  17.8 2.1 %collective-permute-start.2 = (f32[32,1152]{1,0:T(8,128)S(1)}, f32[32,1152]{1,0:T(8,128)S(1)}, u32[]{:S(2)}, u32[]{:S(2)}) collective-permute-start(f32[32,1152]{1,0:T(8,128)S(1)} %get-tuple-element.38), channel_id=1, source_target_pairs={{24,0},{0,8},{8,16},{16,24},{25,1},{1,9},{9,17},{17,25},{26,2},{2,... | collective-permute-start | bytes 442376 | tf_op jit(solution)/shard_map/ppermute | solution.py:19
  19.9 3.0 %collective-permute-start.4 = (f32[32,1152]{1,0:T(8,128)S(1)}, f32[32,1152]{1,0:T(8,128)S(1)}, u32[]{:S(2)}, u32[]{:S(2)}) collective-permute-start(f32[32,1152]{1,0:T(8,128)S(1)} %collective-permute-done.3), channel_id=1, source_target_pairs={{32,0},{64,32},{96,64},{0,96},{33,1},{65,33},{97,65},{1,97},{34,2}... | collective-permute-start | bytes 442376 | tf_op jit(solution)/shard_map/ppermute | solution.py:19
  27.3 2.4 %collective-permute-done.5 = f32[32,1152]{1,0:T(8,128)S(1)} collective-permute-done((f32[32,1152]{1,0:T(8,128)S(1)}, f32[32,1152]{1,0:T(8,128)S(1)}, u32[]{:S(2)}, u32[]{:S(2)}) %collective-permute-start.5) | collective-permute-done | bytes 147488 | tf_op jit(solution)/shard_map/ppermute | solution.py:19
  32.9 6.5 %all-to-all-start.1 = ((f32[4,32,1152]{2,1,0:T(8,128)}), f32[4,32,1152]{2,1,0:T(8,128)S(1)}, u32[]{:S(2)}, u32[]{:S(2)}) async-start(f32[4,32,1152]{2,1,0:T(8,128)} %bitcast.2), calls=%async_computation.1 | async-start | bytes 1179648 | tf_op jit(solution)/shard_map/all_to_all | solution.py:164
  45.0 17.9 %collective-permute-done.12.refs_5_ = f32[128,1152]{1,0:T(8,128)S(1)} collective-permute-done((f32[128,1152]{1,0:T(8,128)}, f32[128,1152]{1,0:T(8,128)S(1)}, u32[]{:S(2)}, u32[]{:S(2)}) %collective-permute-start.12) | collective-permute-done | bytes 589856 | tf_op jit(solution)/shard_map/ppermute | solution.py:19
  65.1 1.6 %collective-permute-done.14.refs_7_ = f32[128,1152]{1,0:T(8,128)} collective-permute-done((f32[128,1152]{1,0:T(8,128)}, f32[128,1152]{1,0:T(8,128)}, u32[]{:S(2)}, u32[]{:S(2)}) %collective-permute-start.14) | collective-permute-done | bytes 589856 | tf_op jit(solution)/shard_map/ppermute | solution.py:19
  67.8 3.9 %image_terms.2 = (f32[128,1152]{1,0:T(8,128)S(1)}, f32[128,1152]{1,0:T(8,128)S(1)}, f32[256,512]{1,0:T(8,128)S(1)}) custom-call(f32[128,1152]{1,0:T(8,128)S(1)} %bitcast.13, f32[128,1152]{1,0:T(8,128)S(1)} %collective-permute-done.7.refs_1_.other, f32[256,128]{1,0:T(8,128)S(1)} %broadcast_in_dim.2.refs_2_, f32[1,512]{1,0:T(1,128)S(1)} %convert_element_type.17.refs_3_, ...), custom_call_target="tpu_custom_call" | custom-call | tf_op jit(solution)/shard_map/image_terms/pallas_call | solution.py:83
  73.3 1.7 %collective-permute-done.9.refs_5_ = f32[128,1152]{1,0:T(8,128)} collective-permute-done((f32[128,1152]{1,0:T(8,128)S(1)}, f32[128,1152]{1,0:T(8,128)}, u32[]{:S(2)}, u32[]{:S(2)}) %collective-permute-start.9) | collective-permute-done | bytes 589856 | tf_op jit(solution)/shard_map/ppermute | solution.py:19
  75.0 4.0 %image_terms.3 = (f32[128,1152]{1,0:T(8,128)S(1)}, f32[128,1152]{1,0:T(8,128)S(1)}, f32[256,512]{1,0:T(8,128)S(1)}) custom-call(f32[128,1152]{1,0:T(8,128)S(1)} %bitcast.14, f32[128,1152]{1,0:T(8,128)S(1)} %collective-permute-done.7.refs_1_.other, f32[256,128]{1,0:T(8,128)S(1)} %broadcast_in_dim.2.refs_2_, f32[1,512]{1,0:T(1,128)S(1)} %convert_element_type.15.refs_3_, ...), custom_call_target="tpu_custom_call" | custom-call | tf_op jit(solution)/shard_map/image_terms/pallas_call | solution.py:83
  79.2 2.4 %caption_terms.2 = (f32[128,1152]{1,0:T(8,128)S(1)}, f32[128,1152]{1,0:T(8,128)}, f32[128,1152]{1,0:T(8,128)}, f32[128,1152]{1,0:T(8,128)}) custom-call(f32[128,1152]{1,0:T(8,128)S(1)} %bitcast.15, f32[128,1152]{1,0:T(8,128)S(1)} %collective-permute-done.7.refs_1_.other, f32[256,512]{1,0:T(8,128)S(1)} %get-tuple-element.47.weights), custom_call_target="tpu_custom_call" | custom-call | tf_op jit(solution)/shard_map/caption_terms/pallas_call | solution.py:83
  84.6 6.9 %all-to-all-start.2 = ((f32[4,32,1152]{2,1,0:T(8,128)}), f32[4,32,1152]{2,1,0:T(8,128)S(1)}, u32[]{:S(2)}, u32[]{:S(2)}) async-start(f32[4,32,1152]{2,1,0:T(8,128)} %bitcast.19), calls=%async_computation.2 | async-start | bytes 1179648 | tf_op jit(solution)/shard_map/all_to_all | solution.py:194
  92.5 2.5 %caption_terms.3 = (f32[128,1152]{1,0:T(8,128)S(1)}, f32[128,1152]{1,0:T(8,128)}, f32[128,1152]{1,0:T(8,128)}, f32[128,1152]{1,0:T(8,128)}) custom-call(f32[128,1152]{1,0:T(8,128)S(1)} %bitcast.16, f32[128,1152]{1,0:T(8,128)S(1)} %collective-permute-done.7.refs_1_.other, f32[256,512]{1,0:T(8,128)S(1)} %copy-done.10), custom_call_target="tpu_custom_call" | custom-call | flops 30000001024 | bytes 100000000 | tf_op jit(solution)/shard_map/caption_terms/pallas_call | solution.py:83
  95.9 4.9 %collective-permute-start.20 = (f32[128,1152]{1,0:T(8,128)}, f32[128,1152]{1,0:T(8,128)}, u32[]{:S(2)}, u32[]{:S(2)}) collective-permute-start(f32[128,1152]{1,0:T(8,128)} %get-tuple-element.67), channel_id=1, source_target_pairs={{64,0},{96,32},{0,64},{32,96},{65,1},{97,33},{1,65},{33,97},{66,2}... | collective-permute-start | bytes 1769480 | tf_op jit(solution)/shard_map/ppermute | solution.py:19
  100.8 7.4 %all-to-all-done.2 = f32[4,32,1152]{2,1,0:T(8,128)S(1)} async-done(((f32[4,32,1152]{2,1,0:T(8,128)}), f32[4,32,1152]{2,1,0:T(8,128)S(1)}, u32[]{:S(2)}, u32[]{:S(2)}) %all-to-all-start.2) | async-done | bytes 589856 | tf_op jit(solution)/shard_map/all_to_all | solution.py:194
  109.2 3.3 %collective-permute-start.21 = (f32[128,1152]{1,0:T(8,128)}, f32[128,1152]{1,0:T(8,128)S(1)}, u32[]{:S(2)}, u32[]{:S(2)}) collective-permute-start(f32[128,1152]{1,0:T(8,128)} %get-tuple-element.68), channel_id=1, source_target_pairs={{32,0},{64,32},{96,64},{0,96},{33,1},{65,33},{97,65},{1,97},{34,2}... | collective-permute-start | bytes 1769480 | tf_op jit(solution)/shard_map/ppermute | solution.py:19
  114.1 12.6 %collective-permute-done.20.c = f32[128,1152]{1,0:T(8,128)} collective-permute-done((f32[128,1152]{1,0:T(8,128)}, f32[128,1152]{1,0:T(8,128)}, u32[]{:S(2)}, u32[]{:S(2)}) %collective-permute-start.20) | collective-permute-done | bytes 589856 | tf_op jit(solution)/shard_map/ppermute | solution.py:19
  126.7 6.9 %all-to-all-start.3 = ((f32[4,32,1152]{2,1,0:T(8,128)}), f32[4,32,1152]{2,1,0:T(8,128)}, u32[]{:S(2)}, u32[]{:S(2)}) async-start(f32[4,32,1152]{2,1,0:T(8,128)} %bitcast.6), calls=%async_computation.3 | async-start | bytes 1179648 | tf_op jit(solution)/shard_map/all_to_all | solution.py:200
  134.3 3.4 %collective-permute-start.26 = (f32[32,1152]{1,0:T(8,128)}, f32[32,1152]{1,0:T(8,128)}, u32[]{:S(2)}, u32[]{:S(2)}) collective-permute-start(f32[32,1152]{1,0:T(8,128)} %get-tuple-element.81), channel_id=1, source_target_pairs={{64,0},{96,32},{0,64},{32,96},{65,1},{97,33},{1,65},{33,97},{66,2}... | collective-permute-start | bytes 442376 | tf_op jit(solution)/shard_map/ppermute | solution.py:19
  139.2 2.7 %collective-permute-start.22 = (f32[32,1152]{1,0:T(8,128)S(1)}, f32[32,1152]{1,0:T(8,128)S(1)}, u32[]{:S(2)}, u32[]{:S(2)}) collective-permute-start(f32[32,1152]{1,0:T(8,128)S(1)} %get-tuple-element.76), channel_id=1, source_target_pairs={{24,0},{0,8},{8,16},{16,24},{25,1},{1,9},{9,17},{17,25},{26,2},{2,... | collective-permute-start | bytes 442376 | tf_op jit(solution)/shard_map/ppermute | solution.py:19
  143.2 6.0 %all-to-all-done.3 = f32[4,32,1152]{2,1,0:T(8,128)} async-done(((f32[4,32,1152]{2,1,0:T(8,128)}), f32[4,32,1152]{2,1,0:T(8,128)}, u32[]{:S(2)}, u32[]{:S(2)}) %all-to-all-start.3) | async-done | bytes 589856 | tf_op jit(solution)/shard_map/all_to_all | solution.py:200
  152.8 3.0 %fusion.9 = f32[128,288]{0,1:T(8,128)} fusion(f32[128,1152]{1,0:T(8,128)} %bitcast.7, f32[288,1152]{1,0:T(8,128)S(1)} %copy-done), kind=kOutput, calls=%fused_computation.28 | convolution fusion | flops 509607936 | bytes 2064384 | tf_op jit(solution)/shard_map/dot_general | solution.py:31
  (96 shorter events, 38.6 us)
Async XLA Ops:
  7.6 24.3 %all-to-all-start = ((f32[4,32,1152]{2,1,0:T(8,128)}), f32[4,32,1152]{2,1,0:T(8,128)S(1)}, u32[]{:S(2)}, u32[]{:S(2)}) async-start(f32[4,32,1152]{2,1,0:T(8,128)} %bitcast), calls=%async_computation | async-start | bytes 1179648 | tf_op jit(solution)/shard_map/all_to_all | solution.py:154
  15.9 8.8 %collective-permute-start = (f32[32,1152]{1,0:T(8,128)S(1)}, f32[32,1152]{1,0:T(8,128)S(1)}, u32[]{:S(2)}, u32[]{:S(2)}) collective-permute-start(f32[32,1152]{1,0:T(8,128)S(1)} %get-tuple-element.38), channel_id=1, source_target_pairs={{8,0},{16,8},{24,16},{0,24},{9,1},{17,9},{25,17},{1,25},{10,2},{18... | collective-permute-start | bytes 442376 | tf_op jit(solution)/shard_map/ppermute | solution.py:19
  16.7 9.6 %collective-permute-start.1 = (f32[32,1152]{1,0:T(8,128)S(1)}, f32[32,1152]{1,0:T(8,128)S(1)}, u32[]{:S(2)}, u32[]{:S(2)}) collective-permute-start(f32[32,1152]{1,0:T(8,128)S(1)} %get-tuple-element.38), channel_id=1, source_target_pairs={{16,0},{24,8},{0,16},{8,24},{17,1},{25,9},{1,17},{9,25},{18,2},{26... | collective-permute-start | bytes 442376 | tf_op jit(solution)/shard_map/ppermute | solution.py:19
  17.8 8.4 %collective-permute-start.2 = (f32[32,1152]{1,0:T(8,128)S(1)}, f32[32,1152]{1,0:T(8,128)S(1)}, u32[]{:S(2)}, u32[]{:S(2)}) collective-permute-start(f32[32,1152]{1,0:T(8,128)S(1)} %get-tuple-element.38), channel_id=1, source_target_pairs={{24,0},{0,8},{8,16},{16,24},{25,1},{1,9},{9,17},{17,25},{26,2},{2,... | collective-permute-start | bytes 442376 | tf_op jit(solution)/shard_map/ppermute | solution.py:19
  32.9 31.7 %all-to-all-start.1 = ((f32[4,32,1152]{2,1,0:T(8,128)}), f32[4,32,1152]{2,1,0:T(8,128)S(1)}, u32[]{:S(2)}, u32[]{:S(2)}) async-start(f32[4,32,1152]{2,1,0:T(8,128)} %bitcast.2), calls=%async_computation.1 | async-start | bytes 1179648 | tf_op jit(solution)/shard_map/all_to_all | solution.py:164
  39.4 23.6 %collective-permute-start.12 = (f32[128,1152]{1,0:T(8,128)}, f32[128,1152]{1,0:T(8,128)S(1)}, u32[]{:S(2)}, u32[]{:S(2)}) collective-permute-start(f32[128,1152]{1,0:T(8,128)} %pad_maximum_fusion.refs_4_), channel_id=1, source_target_pairs={{32,0},{64,32},{96,64},{0,96},{33,1},{65,33},{97,65},{1,97},{34,2}... | collective-permute-start | bytes 1769480 | tf_op jit(solution)/shard_map/ppermute | solution.py:19
  40.8 23.8 %collective-permute-start.13 = (f32[128,1152]{1,0:T(8,128)}, f32[128,1152]{1,0:T(8,128)}, u32[]{:S(2)}, u32[]{:S(2)}) collective-permute-start(f32[128,1152]{1,0:T(8,128)} %pad_maximum_fusion.refs_4_), channel_id=1, source_target_pairs={{64,0},{96,32},{0,64},{32,96},{65,1},{97,33},{1,65},{33,97},{66,2}... | collective-permute-start | bytes 1769480 | tf_op jit(solution)/shard_map/ppermute | solution.py:19
  41.5 25.2 %collective-permute-start.14 = (f32[128,1152]{1,0:T(8,128)}, f32[128,1152]{1,0:T(8,128)}, u32[]{:S(2)}, u32[]{:S(2)}) collective-permute-start(f32[128,1152]{1,0:T(8,128)} %pad_maximum_fusion.refs_4_), channel_id=1, source_target_pairs={{96,0},{0,32},{32,64},{64,96},{97,1},{1,33},{33,65},{65,97},{98,2}... | collective-permute-start | bytes 1769480 | tf_op jit(solution)/shard_map/ppermute | solution.py:19
  42.6 30.8 %collective-permute-start.10 = (f32[128,1152]{1,0:T(8,128)S(1)}, f32[128,1152]{1,0:T(8,128)}, u32[]{:S(2)}, u32[]{:S(2)}) collective-permute-start(f32[128,1152]{1,0:T(8,128)S(1)} %pad_maximum_fusion.1.refs_4_), channel_id=1, source_target_pairs={{16,0},{24,8},{0,16},{8,24},{17,1},{25,9},{1,17},{9,25},{18,2},{26... | collective-permute-start | bytes 1769480 | tf_op jit(solution)/shard_map/ppermute | solution.py:19
  43.8 29.5 %collective-permute-start.11 = (f32[128,1152]{1,0:T(8,128)S(1)}, f32[128,1152]{1,0:T(8,128)}, u32[]{:S(2)}, u32[]{:S(2)}) collective-permute-start(f32[128,1152]{1,0:T(8,128)S(1)} %pad_maximum_fusion.1.refs_4_), channel_id=1, source_target_pairs={{24,0},{0,8},{8,16},{16,24},{25,1},{1,9},{9,17},{17,25},{26,2},{2,... | collective-permute-start | bytes 1769480 | tf_op jit(solution)/shard_map/ppermute | solution.py:19
  63.8 11.2 %collective-permute-start.9 = (f32[128,1152]{1,0:T(8,128)S(1)}, f32[128,1152]{1,0:T(8,128)}, u32[]{:S(2)}, u32[]{:S(2)}) collective-permute-start(f32[128,1152]{1,0:T(8,128)S(1)} %pad_maximum_fusion.1.refs_4_), channel_id=1, source_target_pairs={{8,0},{16,8},{24,16},{0,24},{9,1},{17,9},{25,17},{1,25},{10,2},{18... | collective-permute-start | bytes 1769480 | tf_op jit(solution)/shard_map/ppermute | solution.py:19
  81.6 27.6 %collective-permute-start.15 = (f32[128,1152]{1,0:T(8,128)}, f32[128,1152]{1,0:T(8,128)}, u32[]{:S(2)}, u32[]{:S(2)}) collective-permute-start(f32[128,1152]{1,0:T(8,128)} %get-tuple-element.49), channel_id=1, source_target_pairs={{24,0},{0,8},{8,16},{16,24},{25,1},{1,9},{9,17},{17,25},{26,2},{2,... | collective-permute-start | bytes 1769480 | tf_op jit(solution)/shard_map/ppermute | solution.py:19
  82.5 30.0 %collective-permute-start.16 = (f32[128,1152]{1,0:T(8,128)}, f32[128,1152]{1,0:T(8,128)}, u32[]{:S(2)}, u32[]{:S(2)}) collective-permute-start(f32[128,1152]{1,0:T(8,128)} %get-tuple-element.50), channel_id=1, source_target_pairs={{16,0},{24,8},{0,16},{8,24},{17,1},{25,9},{1,17},{9,25},{18,2},{26... | collective-permute-start | bytes 1769480 | tf_op jit(solution)/shard_map/ppermute | solution.py:19
  83.3 29.2 %collective-permute-start.17 = (f32[128,1152]{1,0:T(8,128)}, f32[128,1152]{1,0:T(8,128)}, u32[]{:S(2)}, u32[]{:S(2)}) collective-permute-start(f32[128,1152]{1,0:T(8,128)} %get-tuple-element.51), channel_id=1, source_target_pairs={{8,0},{16,8},{24,16},{0,24},{9,1},{17,9},{25,17},{1,25},{10,2},{18... | collective-permute-start | bytes 1769480 | tf_op jit(solution)/shard_map/ppermute | solution.py:19
  84.6 23.7 %all-to-all-start.2 = ((f32[4,32,1152]{2,1,0:T(8,128)}), f32[4,32,1152]{2,1,0:T(8,128)S(1)}, u32[]{:S(2)}, u32[]{:S(2)}) async-start(f32[4,32,1152]{2,1,0:T(8,128)} %bitcast.19), calls=%async_computation.2 | async-start | bytes 1179648 | tf_op jit(solution)/shard_map/all_to_all | solution.py:194
  95.8 18.3 %collective-permute-start.19 = (f32[128,1152]{1,0:T(8,128)}, f32[128,1152]{1,0:T(8,128)}, u32[]{:S(2)}, u32[]{:S(2)}) collective-permute-start(f32[128,1152]{1,0:T(8,128)} %get-tuple-element.66), channel_id=1, source_target_pairs={{96,0},{0,32},{32,64},{64,96},{97,1},{1,33},{33,65},{65,97},{98,2}... | collective-permute-start | bytes 1769480 | tf_op jit(solution)/shard_map/ppermute | solution.py:19
  95.9 30.8 %collective-permute-start.20 = (f32[128,1152]{1,0:T(8,128)}, f32[128,1152]{1,0:T(8,128)}, u32[]{:S(2)}, u32[]{:S(2)}) collective-permute-start(f32[128,1152]{1,0:T(8,128)} %get-tuple-element.67), channel_id=1, source_target_pairs={{64,0},{96,32},{0,64},{32,96},{65,1},{97,33},{1,65},{33,97},{66,2}... | collective-permute-start | bytes 1769480 | tf_op jit(solution)/shard_map/ppermute | solution.py:19
  109.2 17.5 %collective-permute-start.21 = (f32[128,1152]{1,0:T(8,128)}, f32[128,1152]{1,0:T(8,128)S(1)}, u32[]{:S(2)}, u32[]{:S(2)}) collective-permute-start(f32[128,1152]{1,0:T(8,128)} %get-tuple-element.68), channel_id=1, source_target_pairs={{32,0},{64,32},{96,64},{0,96},{33,1},{65,33},{97,65},{1,97},{34,2}... | collective-permute-start | bytes 1769480 | tf_op jit(solution)/shard_map/ppermute | solution.py:19
  126.7 22.6 %all-to-all-start.3 = ((f32[4,32,1152]{2,1,0:T(8,128)}), f32[4,32,1152]{2,1,0:T(8,128)}, u32[]{:S(2)}, u32[]{:S(2)}) async-start(f32[4,32,1152]{2,1,0:T(8,128)} %bitcast.6), calls=%async_computation.3 | async-start | bytes 1179648 | tf_op jit(solution)/shard_map/all_to_all | solution.py:200
  134.3 14.9 %collective-permute-start.25 = (f32[32,1152]{1,0:T(8,128)}, f32[32,1152]{1,0:T(8,128)}, u32[]{:S(2)}, u32[]{:S(2)}) collective-permute-start(f32[32,1152]{1,0:T(8,128)} %get-tuple-element.79), channel_id=1, source_target_pairs={{96,0},{0,32},{32,64},{64,96},{97,1},{1,33},{33,65},{65,97},{98,2}... | collective-permute-start | bytes 442376 | tf_op jit(solution)/shard_map/ppermute | solution.py:19
  134.3 16.3 %collective-permute-start.26 = (f32[32,1152]{1,0:T(8,128)}, f32[32,1152]{1,0:T(8,128)}, u32[]{:S(2)}, u32[]{:S(2)}) collective-permute-start(f32[32,1152]{1,0:T(8,128)} %get-tuple-element.81), channel_id=1, source_target_pairs={{64,0},{96,32},{0,64},{32,96},{65,1},{97,33},{1,65},{33,97},{66,2}... | collective-permute-start | bytes 442376 | tf_op jit(solution)/shard_map/ppermute | solution.py:19
  137.8 12.9 %collective-permute-start.27 = (f32[32,1152]{1,0:T(8,128)S(1)}, f32[32,1152]{1,0:T(8,128)}, u32[]{:S(2)}, u32[]{:S(2)}) collective-permute-start(f32[32,1152]{1,0:T(8,128)S(1)} %get-tuple-element.80), channel_id=1, source_target_pairs={{32,0},{64,32},{96,64},{0,96},{33,1},{65,33},{97,65},{1,97},{34,2}... | collective-permute-start | bytes 442376 | tf_op jit(solution)/shard_map/ppermute | solution.py:19
  139.2 16.6 %collective-permute-start.22 = (f32[32,1152]{1,0:T(8,128)S(1)}, f32[32,1152]{1,0:T(8,128)S(1)}, u32[]{:S(2)}, u32[]{:S(2)}) collective-permute-start(f32[32,1152]{1,0:T(8,128)S(1)} %get-tuple-element.76), channel_id=1, source_target_pairs={{24,0},{0,8},{8,16},{16,24},{25,1},{1,9},{9,17},{17,25},{26,2},{2,... | collective-permute-start | bytes 442376 | tf_op jit(solution)/shard_map/ppermute | solution.py:19
  141.9 13.8 %collective-permute-start.23 = (f32[32,1152]{1,0:T(8,128)S(1)}, f32[32,1152]{1,0:T(8,128)S(1)}, u32[]{:S(2)}, u32[]{:S(2)}) collective-permute-start(f32[32,1152]{1,0:T(8,128)S(1)} %get-tuple-element.78), channel_id=1, source_target_pairs={{16,0},{24,8},{0,16},{8,24},{17,1},{25,9},{1,17},{9,25},{18,2},{26... | collective-permute-start | bytes 442376 | tf_op jit(solution)/shard_map/ppermute | solution.py:19
  (21 other events, 114.2 us)

commit v3 on v2

--- a/solution.py
+++ b/solution.py
@@ -53,22 +53,20 @@
     return one(left[0], right[0]) + (one(left[0], right[1]) + one(left[1], right[0]))
 
 
-def image_kernel(adds, *refs):
-    own, other, wanted, held = refs[:4]
-    blocks, refs = refs[4:8], refs[8:]
-    before, refs = (refs[:2], refs[2:]) if adds else (None, refs)
-    grads, weights_out = refs[:2], refs[2]
+def image_kernel(own, other, wanted, held, *refs):
+    blocks, grads, weights_out = refs[:8], refs[8:10], refs[10:]
     images = parts(jnp.concatenate([own[...], other[...]]))
-    captions = parts(jnp.concatenate([r[...] for r in blocks]))
-    logits = LOGIT_SCALE * dot3(images, captions, ((1,), (1,))) + LOGIT_BIAS
-    signs = jnp.where(wanted[:, :1] == held[...], 1.0, -1.0).astype(jnp.float32)
-    weights = (-LOGIT_SCALE * signs) * jax.nn.sigmoid(-signs * logits)
-    weights_out[...] = weights
-    image_terms = dot3(parts(weights), captions, ((1,), (0,)))
+    terms = 0.0
+    for h, out in enumerate(weights_out):
+        captions = parts(jnp.concatenate([r[...] for r in blocks[4 * h : 4 * h + 4]]))
+        logits = LOGIT_SCALE * dot3(images, captions, ((1,), (1,))) + LOGIT_BIAS
+        signs = jnp.where(wanted[:, :1] == held[h : h + 1, :], 1.0, -1.0).astype(jnp.float32)
+        weights = (-LOGIT_SCALE * signs) * jax.nn.sigmoid(-signs * logits)
+        out[...] = weights
+        terms = terms + dot3(parts(weights), captions, ((1,), (0,)))
     size = own.shape[0]
     for k, ref in enumerate(grads):
-        term = image_terms[k * size : (k + 1) * size]
-        ref[...] = term + before[k][...] if adds else term
+        ref[...] = terms[k * size : (k + 1) * size]
 
 
 def caption_kernel(own, other, weights, *sums):
@@ -89,13 +87,10 @@
     )(*args)
 
 
-def image_terms(images, wanted, held, blocks, before):
-    shapes = [images[0].shape] * 2 + [(wanted.shape[0], held.shape[1])]
-    out = called(
-        lambda *refs: image_kernel(before is not None, *refs),
-        "image_terms", shapes, *images, wanted, held, *blocks, *(before or []),
-    )
-    return out[:2], out[2]
+def image_terms(images, wanted, held, blocks):
+    shapes = [images[0].shape] * 2 + [(wanted.shape[0], held.shape[1])] * 2
+    out = called(image_kernel, "image_terms", shapes, *images, wanted, held, *blocks)
+    return out[:2], out[2], out[3]
 
 
 def caption_terms(images, weights, shape, cost=None):
@@ -179,8 +174,8 @@
     near_held = numbers(zl, (y + steps)[:, None], (x + steps)[None, :])
     far_held = numbers(1 - zl, (y + steps)[None, :], (x + steps)[:, None])
 
-    grads, near_weights = image_terms(chip_images, wanted, near_held, near, None)
-    grads, far_weights = image_terms(chip_images, wanted, far_held, far, grads)
+    held = jnp.concatenate([near_held, far_held])
+    grads, near_weights, far_weights = image_terms(chip_images, wanted, held, [*near, *far])
     grads, far_weights = lax.optimization_barrier((grads, far_weights))
     far_sums = caption_terms(chip_images, far_weights, far[0].shape)
     shard_grad = grads[0] + pulled(grads[1], "c", 1)

time: 160 us -> 151 us (0.944)
  starting transfers between devices: 66.7 us -> 60.4 us
    all_to_all x1, waiting for transfers between devices: 6.04 us -> 0.01 us  [local(): raw_rows = lax.all_to_all(sent, 'zh', 0, 0, tiled=True)]
    all_to_all x1, waiting for transfers between devices: 7.38 us -> 10.1 us  [local(): lax.all_to_all(shard_grad, 'zh', 0, 0, tiled=True)]
    all_to_all x1, starting transfers between devices: 6.92 us -> 4.31 us  [local(): raw_rows = lax.all_to_all(sent, 'zh', 0, 0, tiled=True)]
    ppermute x29, starting transfers between devices: 38 us -> 36 us  [pulled(): lax.ppermute(value, axis, [((i + steps) % count, i) for i in range(count)])]
    all_to_all x1, starting transfers between devices: 6.52 us -> 4.58 us  [local(): shard_images = lax.all_to_all(sent, 'zh', 0, 0, tiled=True)]
    all_to_all x1, waiting for transfers between devices: 0.69 us -> 2.63 us  [local(): arrived = lax.all_to_all(partial, 'zh', 0, 0, tiled=True)]
    pallas_call x9 -> x8, Pallas kernels: 17.7 us -> 16.2 us  [called(): pl.pallas_call(kernel, out_shape=[jax.ShapeDtypeStruct(shape, jnp.float32...]
    unnamed x24 -> x22, local copies, waits for them, and re-layouts: 6.36 us -> 6.62 us
  transfers between devices with their start and end apart: 33 -> 33, of which waited for: 13 -> 15; matrix products, arithmetic and copies ran while one was open for 6% -> 7% of each run, Pallas kernels for 8% -> 6%
where the time goes in v3:
time: 151 us; the launch traced here: 150 us
  starting transfers between devices  60.4 us (40%)
  waiting for transfers between devices  54.9 us (36%)
  Pallas kernels  16.2 us (11%)
  local copies, waits for them, and re-layouts  8.52 us (6%)
  matrix products  4.89 us (3%)
  other arithmetic  4.07 us (3%)
    ppermute x29, waiting for transfers between devices, pulled(): lax.ppermute(value, axis, [((i + steps) % count, i) for i in range(count)])  42.1 us
    ppermute x29, starting transfers between devices, pulled(): lax.ppermute(value, axis, [((i + steps) % count, i) for i in range(count)])  36 us
    pallas_call x8, Pallas kernels, called(): pl.pallas_call(kernel, out_shape=[jax.ShapeDtypeStruct(shape, jnp.float32...  16.2 us
    all_to_all x1, waiting for transfers between devices, local(): lax.all_to_all(shard_grad, 'zh', 0, 0, tiled=True)  10.1 us
    all_to_all x1, starting transfers between devices, local(): arrived = lax.all_to_all(partial, 'zh', 0, 0, tiled=True)  8.28 us
    all_to_all x1, starting transfers between devices, local(): lax.all_to_all(shard_grad, 'zh', 0, 0, tiled=True)  7.2 us
    unnamed x22, local copies, waits for them, and re-layouts  6.62 us
    dot_general x2, matrix products, product(): lax.dot_general(left, right, (dims, ((), ())), precision=lax.Precision.HI...  4.89 us
  transfers between devices with their start and end apart: 33, of which 15 were waited for; matrix products, arithmetic and copies ran while one was open for 7% of the time, Pallas kernels for 6%

profile of v3, /device:TPU:6, one launch (start us, length us, event | category | flops | bytes accessed | tf_op | source)
XLA Modules:
  0.0 149.7 jit_solution(14271517457506845276)
XLA Ops:
  1.8 2.0 %collective-permute-start.3 = (f32[32,1152]{1,0:T(8,128)S(1)}, f32[32,1152]{1,0:T(8,128)S(1)}, u32[]{:S(2)}, u32[]{:S(2)}) collective-permute-start(f32[32,1152]{1,0:T(8,128)S(1)} %get-tuple-element.39), channel_id=1, source_target_pairs={{128,0},{0,128},{129,1},{1,129},{130,2},{2,130},{131,3},{3,131},{1... | collective-permute-start | bytes 442376 | tf_op jit(solution)/shard_map/ppermute | solution.py:19
  3.8 3.0 %fusion.8 = f32[128,1152]{1,0:T(8,128)} fusion(f32[128,288]{0,1:T(8,128)} %param.4, f32[288,1152]{1,0:T(8,128)S(1)} %copy-done), kind=kOutput, calls=%fused_computation.28 | convolution fusion | flops 509607936 | bytes 2064384 | tf_op jit(solution)/shard_map/dot_general | solution.py:31
  7.6 8.3 %all-to-all-start = ((f32[4,32,1152]{2,1,0:T(8,128)}), f32[4,32,1152]{2,1,0:T(8,128)S(1)}, u32[]{:S(2)}, u32[]{:S(2)}) async-start(f32[4,32,1152]{2,1,0:T(8,128)} %bitcast), calls=%async_computation | async-start | bytes 1179648 | tf_op jit(solution)/shard_map/all_to_all | solution.py:149
  16.4 2.4 %collective-permute-start.1 = (f32[32,1152]{1,0:T(8,128)S(1)}, f32[32,1152]{1,0:T(8,128)S(1)}, u32[]{:S(2)}, u32[]{:S(2)}) collective-permute-start(f32[32,1152]{1,0:T(8,128)S(1)} %get-tuple-element.39), channel_id=1, source_target_pairs={{16,0},{24,8},{0,16},{8,24},{17,1},{25,9},{1,17},{9,25},{18,2},{26... | collective-permute-start | bytes 442376 | tf_op jit(solution)/shard_map/ppermute | solution.py:19
  20.4 2.9 %collective-permute-start.5 = (f32[32,1152]{1,0:T(8,128)S(1)}, f32[32,1152]{1,0:T(8,128)S(1)}, u32[]{:S(2)}, u32[]{:S(2)}) collective-permute-start(f32[32,1152]{1,0:T(8,128)S(1)} %collective-permute-done.3), channel_id=1, source_target_pairs={{64,0},{96,32},{0,64},{32,96},{65,1},{97,33},{1,65},{33,97},{66,2}... | collective-permute-start | bytes 442376 | tf_op jit(solution)/shard_map/ppermute | solution.py:19
  29.3 2.6 %all-to-all-done = f32[4,32,1152]{2,1,0:T(8,128)S(1)} async-done(((f32[4,32,1152]{2,1,0:T(8,128)}), f32[4,32,1152]{2,1,0:T(8,128)S(1)}, u32[]{:S(2)}, u32[]{:S(2)}) %all-to-all-start) | async-done | bytes 589856 | tf_op jit(solution)/shard_map/all_to_all | solution.py:149
  32.9 4.6 %all-to-all-start.1 = ((f32[4,32,1152]{2,1,0:T(8,128)}), f32[4,32,1152]{2,1,0:T(8,128)S(1)}, u32[]{:S(2)}, u32[]{:S(2)}) async-start(f32[4,32,1152]{2,1,0:T(8,128)} %bitcast.2), calls=%async_computation.1 | async-start | bytes 1179648 | tf_op jit(solution)/shard_map/all_to_all | solution.py:159
  39.0 2.5 %collective-permute-start.10 = (f32[128,1152]{1,0:T(8,128)S(1)}, f32[128,1152]{1,0:T(8,128)}, u32[]{:S(2)}, u32[]{:S(2)}) collective-permute-start(f32[128,1152]{1,0:T(8,128)S(1)} %pad_maximum_fusion.refs_0_), channel_id=1, source_target_pairs={{64,0},{96,32},{0,64},{32,96},{65,1},{97,33},{1,65},{33,97},{66,2}... | collective-permute-start | bytes 1769480 | tf_op jit(solution)/shard_map/ppermute | solution.py:19
  42.8 3.1 %collective-permute-start.14 = (f32[128,1152]{1,0:T(8,128)}, f32[128,1152]{1,0:T(8,128)}, u32[]{:S(2)}, u32[]{:S(2)}) collective-permute-start(f32[128,1152]{1,0:T(8,128)} %pad_maximum_fusion.1.refs_4_), channel_id=1, source_target_pairs={{24,0},{0,8},{8,16},{16,24},{25,1},{1,9},{9,17},{17,25},{26,2},{2,... | collective-permute-start | bytes 1769480 | tf_op jit(solution)/shard_map/ppermute | solution.py:19
  45.9 7.5 %collective-permute-done.11.refs_3_ = f32[128,1152]{1,0:T(8,128)S(1)} collective-permute-done((f32[128,1152]{1,0:T(8,128)S(1)}, f32[128,1152]{1,0:T(8,128)S(1)}, u32[]{:S(2)}, u32[]{:S(2)}) %collective-permute-start.11) | collective-permute-done | bytes 589856 | tf_op jit(solution)/shard_map/ppermute | solution.py:19
  55.9 8.8 %collective-permute-done.10.refs_2_ = f32[128,1152]{1,0:T(8,128)} collective-permute-done((f32[128,1152]{1,0:T(8,128)S(1)}, f32[128,1152]{1,0:T(8,128)}, u32[]{:S(2)}, u32[]{:S(2)}) %collective-permute-start.10) | collective-permute-done | bytes 589856 | tf_op jit(solution)/shard_map/ppermute | solution.py:19
  65.0 6.8 %collective-permute-done.14.refs_7_ = f32[128,1152]{1,0:T(8,128)} collective-permute-done((f32[128,1152]{1,0:T(8,128)}, f32[128,1152]{1,0:T(8,128)}, u32[]{:S(2)}, u32[]{:S(2)}) %collective-permute-start.14) | collective-permute-done | bytes 589856 | tf_op jit(solution)/shard_map/ppermute | solution.py:19
  71.8 3.7 %collective-permute-done.12.refs_5_ = f32[128,1152]{1,0:T(8,128)} collective-permute-done((f32[128,1152]{1,0:T(8,128)}, f32[128,1152]{1,0:T(8,128)}, u32[]{:S(2)}, u32[]{:S(2)}) %collective-permute-start.12) | collective-permute-done | bytes 589856 | tf_op jit(solution)/shard_map/ppermute | solution.py:19
  76.7 6.6 %image_terms.1 = (f32[128,1152]{1,0:T(8,128)S(1)}, f32[128,1152]{1,0:T(8,128)S(1)}, f32[256,512]{1,0:T(8,128)S(1)}, f32[256,512]{1,0:T(8,128)S(1)}) custom-call(f32[128,1152]{1,0:T(8,128)S(1)} %bitcast.13, f32[128,1152]{1,0:T(8,128)S(1)} %collective-permute-done.7.other, f32[256,128]{1,0:T(8,128)S(1)} %broadcast_in_dim.2.wanted, ...), custom_call_target="tpu_custom_call" | custom-call | tf_op jit(solution)/shard_map/image_terms/pallas_call | solution.py:81
  84.2 2.4 %caption_terms.2 = (f32[128,1152]{1,0:T(8,128)S(1)}, f32[128,1152]{1,0:T(8,128)}, f32[128,1152]{1,0:T(8,128)}, f32[128,1152]{1,0:T(8,128)}) custom-call(f32[128,1152]{1,0:T(8,128)S(1)} %bitcast.14, f32[128,1152]{1,0:T(8,128)S(1)} %collective-permute-done.7.other, f32[256,512]{1,0:T(8,128)S(1)} %get-tuple-element.49.weights), custom_call_target="tpu_custom_call" | custom-call | tf_op jit(solution)/shard_map/caption_terms/pallas_call | solution.py:81
  89.6 7.2 %all-to-all-start.2 = ((f32[4,32,1152]{2,1,0:T(8,128)}), f32[4,32,1152]{2,1,0:T(8,128)S(1)}, u32[]{:S(2)}, u32[]{:S(2)}) async-start(f32[4,32,1152]{2,1,0:T(8,128)} %bitcast.18), calls=%async_computation.2 | async-start | bytes 1179648 | tf_op jit(solution)/shard_map/all_to_all | solution.py:189
  97.9 2.4 %caption_terms.3 = (f32[128,1152]{1,0:T(8,128)S(1)}, f32[128,1152]{1,0:T(8,128)}, f32[128,1152]{1,0:T(8,128)}, f32[128,1152]{1,0:T(8,128)}) custom-call(f32[128,1152]{1,0:T(8,128)S(1)} %bitcast.15, f32[128,1152]{1,0:T(8,128)S(1)} %collective-permute-done.7.other, f32[256,512]{1,0:T(8,128)S(1)} %copy-done.9), custom_call_target="tpu_custom_call" | custom-call | flops 30000001024 | bytes 100000000 | tf_op jit(solution)/shard_map/caption_terms/pallas_call | solution.py:81
  103.2 10.1 %all-to-all-done.2 = f32[4,32,1152]{2,1,0:T(8,128)S(1)} async-done(((f32[4,32,1152]{2,1,0:T(8,128)}), f32[4,32,1152]{2,1,0:T(8,128)S(1)}, u32[]{:S(2)}, u32[]{:S(2)}) %all-to-all-start.2) | async-done | bytes 589856 | tf_op jit(solution)/shard_map/all_to_all | solution.py:189
  114.3 4.3 %all-to-all-start.3 = ((f32[4,32,1152]{2,1,0:T(8,128)}), f32[4,32,1152]{2,1,0:T(8,128)S(1)}, u32[]{:S(2)}, u32[]{:S(2)}) async-start(f32[4,32,1152]{2,1,0:T(8,128)} %bitcast.6), calls=%async_computation.3 | async-start | bytes 1179648 | tf_op jit(solution)/shard_map/all_to_all | solution.py:195
  125.6 6.0 %collective-permute-done.19.b = f32[128,1152]{1,0:T(8,128)S(1)} collective-permute-done((f32[128,1152]{1,0:T(8,128)}, f32[128,1152]{1,0:T(8,128)S(1)}, u32[]{:S(2)}, u32[]{:S(2)}) %collective-permute-start.19) | collective-permute-done | bytes 589856 | tf_op jit(solution)/shard_map/ppermute | solution.py:19
  131.6 3.5 %collective-permute-done.21.d = f32[128,1152]{1,0:T(8,128)S(1)} collective-permute-done((f32[128,1152]{1,0:T(8,128)}, f32[128,1152]{1,0:T(8,128)S(1)}, u32[]{:S(2)}, u32[]{:S(2)}) %collective-permute-start.21) | collective-permute-done | bytes 589856 | tf_op jit(solution)/shard_map/ppermute | solution.py:19
  137.1 2.7 %collective-permute-start.22 = (f32[32,1152]{1,0:T(8,128)}, f32[32,1152]{1,0:T(8,128)S(1)}, u32[]{:S(2)}, u32[]{:S(2)}) collective-permute-start(f32[32,1152]{1,0:T(8,128)} %get-tuple-element.78), channel_id=1, source_target_pairs={{24,0},{0,8},{8,16},{16,24},{25,1},{1,9},{9,17},{17,25},{26,2},{2,... | collective-permute-start | bytes 442376 | tf_op jit(solution)/shard_map/ppermute | solution.py:19
  139.7 2.8 %collective-permute-start.23 = (f32[32,1152]{1,0:T(8,128)}, f32[32,1152]{1,0:T(8,128)S(1)}, u32[]{:S(2)}, u32[]{:S(2)}) collective-permute-start(f32[32,1152]{1,0:T(8,128)} %get-tuple-element.80), channel_id=1, source_target_pairs={{16,0},{24,8},{0,16},{8,24},{17,1},{25,9},{1,17},{9,25},{18,2},{26... | collective-permute-start | bytes 442376 | tf_op jit(solution)/shard_map/ppermute | solution.py:19
  145.3 1.9 %fusion.9 = f32[128,288]{0,1:T(8,128)} fusion(f32[128,1152]{1,0:T(8,128)S(1)} %bitcast.19, f32[288,1152]{1,0:T(8,128)S(1)} %copy-done), kind=kOutput, calls=%fused_computation.29 | convolution fusion | flops 509607936 | bytes 2064384 | tf_op jit(solution)/shard_map/dot_general | solution.py:31
  (94 shorter events, 40.9 us)
Async XLA Ops:
  7.6 24.3 %all-to-all-start = ((f32[4,32,1152]{2,1,0:T(8,128)}), f32[4,32,1152]{2,1,0:T(8,128)S(1)}, u32[]{:S(2)}, u32[]{:S(2)}) async-start(f32[4,32,1152]{2,1,0:T(8,128)} %bitcast), calls=%async_computation | async-start | bytes 1179648 | tf_op jit(solution)/shard_map/all_to_all | solution.py:149
  16.4 8.6 %collective-permute-start.1 = (f32[32,1152]{1,0:T(8,128)S(1)}, f32[32,1152]{1,0:T(8,128)S(1)}, u32[]{:S(2)}, u32[]{:S(2)}) collective-permute-start(f32[32,1152]{1,0:T(8,128)S(1)} %get-tuple-element.39), channel_id=1, source_target_pairs={{16,0},{24,8},{0,16},{8,24},{17,1},{25,9},{1,17},{9,25},{18,2},{26... | collective-permute-start | bytes 442376 | tf_op jit(solution)/shard_map/ppermute | solution.py:19
  32.9 31.8 %all-to-all-start.1 = ((f32[4,32,1152]{2,1,0:T(8,128)}), f32[4,32,1152]{2,1,0:T(8,128)S(1)}, u32[]{:S(2)}, u32[]{:S(2)}) async-start(f32[4,32,1152]{2,1,0:T(8,128)} %bitcast.2), calls=%async_computation.1 | async-start | bytes 1179648 | tf_op jit(solution)/shard_map/all_to_all | solution.py:159
  37.5 15.9 %collective-permute-start.11 = (f32[128,1152]{1,0:T(8,128)S(1)}, f32[128,1152]{1,0:T(8,128)S(1)}, u32[]{:S(2)}, u32[]{:S(2)}) collective-permute-start(f32[128,1152]{1,0:T(8,128)S(1)} %pad_maximum_fusion.refs_0_), channel_id=1, source_target_pairs={{96,0},{0,32},{32,64},{64,96},{97,1},{1,33},{33,65},{65,97},{98,2}... | collective-permute-start | bytes 1769480 | tf_op jit(solution)/shard_map/ppermute | solution.py:19
  39.0 25.7 %collective-permute-start.10 = (f32[128,1152]{1,0:T(8,128)S(1)}, f32[128,1152]{1,0:T(8,128)}, u32[]{:S(2)}, u32[]{:S(2)}) collective-permute-start(f32[128,1152]{1,0:T(8,128)S(1)} %pad_maximum_fusion.refs_0_), channel_id=1, source_target_pairs={{64,0},{96,32},{0,64},{32,96},{65,1},{97,33},{1,65},{33,97},{66,2}... | collective-permute-start | bytes 1769480 | tf_op jit(solution)/shard_map/ppermute | solution.py:19
  41.7 23.4 %collective-permute-start.9 = (f32[128,1152]{1,0:T(8,128)S(1)}, f32[128,1152]{1,0:T(8,128)}, u32[]{:S(2)}, u32[]{:S(2)}) collective-permute-start(f32[128,1152]{1,0:T(8,128)S(1)} %pad_maximum_fusion.refs_0_), channel_id=1, source_target_pairs={{32,0},{64,32},{96,64},{0,96},{33,1},{65,33},{97,65},{1,97},{34,2}... | collective-permute-start | bytes 1769480 | tf_op jit(solution)/shard_map/ppermute | solution.py:19
  42.8 29.0 %collective-permute-start.14 = (f32[128,1152]{1,0:T(8,128)}, f32[128,1152]{1,0:T(8,128)}, u32[]{:S(2)}, u32[]{:S(2)}) collective-permute-start(f32[128,1152]{1,0:T(8,128)} %pad_maximum_fusion.1.refs_4_), channel_id=1, source_target_pairs={{24,0},{0,8},{8,16},{16,24},{25,1},{1,9},{9,17},{17,25},{26,2},{2,... | collective-permute-start | bytes 1769480 | tf_op jit(solution)/shard_map/ppermute | solution.py:19
  45.9 25.9 %collective-permute-start.13 = (f32[128,1152]{1,0:T(8,128)}, f32[128,1152]{1,0:T(8,128)}, u32[]{:S(2)}, u32[]{:S(2)}) collective-permute-start(f32[128,1152]{1,0:T(8,128)} %pad_maximum_fusion.1.refs_4_), channel_id=1, source_target_pairs={{16,0},{24,8},{0,16},{8,24},{17,1},{25,9},{1,17},{9,25},{18,2},{26... | collective-permute-start | bytes 1769480 | tf_op jit(solution)/shard_map/ppermute | solution.py:19
  54.2 21.3 %collective-permute-start.12 = (f32[128,1152]{1,0:T(8,128)}, f32[128,1152]{1,0:T(8,128)}, u32[]{:S(2)}, u32[]{:S(2)}) collective-permute-start(f32[128,1152]{1,0:T(8,128)} %pad_maximum_fusion.1.refs_4_), channel_id=1, source_target_pairs={{8,0},{16,8},{24,16},{0,24},{9,1},{17,9},{25,17},{1,25},{10,2},{18... | collective-permute-start | bytes 1769480 | tf_op jit(solution)/shard_map/ppermute | solution.py:19
  64.7 10.8 %collective-permute-start.7 = (f32[128,1152]{1,0:T(8,128)S(1)}, f32[128,1152]{1,0:T(8,128)S(1)}, u32[]{:S(2)}, u32[]{:S(2)}) collective-permute-start(f32[128,1152]{1,0:T(8,128)S(1)} %bitcast.12), channel_id=1, source_target_pairs={{4,0},{0,4},{5,1},{1,5},{6,2},{2,6},{7,3},{3,7},{12,8},{8,12},{13,... | collective-permute-start | bytes 1769480 | tf_op jit(solution)/shard_map/ppermute | solution.py:19
  86.7 32.0 %collective-permute-start.15 = (f32[128,1152]{1,0:T(8,128)}, f32[128,1152]{1,0:T(8,128)}, u32[]{:S(2)}, u32[]{:S(2)}) collective-permute-start(f32[128,1152]{1,0:T(8,128)} %get-tuple-element.51), channel_id=1, source_target_pairs={{24,0},{0,8},{8,16},{16,24},{25,1},{1,9},{9,17},{17,25},{26,2},{2,... | collective-permute-start | bytes 1769480 | tf_op jit(solution)/shard_map/ppermute | solution.py:19
  87.3 31.7 %collective-permute-start.16 = (f32[128,1152]{1,0:T(8,128)}, f32[128,1152]{1,0:T(8,128)}, u32[]{:S(2)}, u32[]{:S(2)}) collective-permute-start(f32[128,1152]{1,0:T(8,128)} %get-tuple-element.52), channel_id=1, source_target_pairs={{16,0},{24,8},{0,16},{8,24},{17,1},{25,9},{1,17},{9,25},{18,2},{26... | collective-permute-start | bytes 1769480 | tf_op jit(solution)/shard_map/ppermute | solution.py:19
  87.6 31.4 %collective-permute-start.17 = (f32[128,1152]{1,0:T(8,128)}, f32[128,1152]{1,0:T(8,128)}, u32[]{:S(2)}, u32[]{:S(2)}) collective-permute-start(f32[128,1152]{1,0:T(8,128)} %get-tuple-element.53), channel_id=1, source_target_pairs={{8,0},{16,8},{24,16},{0,24},{9,1},{17,9},{25,17},{1,25},{10,2},{18... | collective-permute-start | bytes 1769480 | tf_op jit(solution)/shard_map/ppermute | solution.py:19
  89.6 23.7 %all-to-all-start.2 = ((f32[4,32,1152]{2,1,0:T(8,128)}), f32[4,32,1152]{2,1,0:T(8,128)S(1)}, u32[]{:S(2)}, u32[]{:S(2)}) async-start(f32[4,32,1152]{2,1,0:T(8,128)} %bitcast.18), calls=%async_computation.2 | async-start | bytes 1179648 | tf_op jit(solution)/shard_map/all_to_all | solution.py:189
  101.1 30.5 %collective-permute-start.19 = (f32[128,1152]{1,0:T(8,128)}, f32[128,1152]{1,0:T(8,128)S(1)}, u32[]{:S(2)}, u32[]{:S(2)}) collective-permute-start(f32[128,1152]{1,0:T(8,128)} %get-tuple-element.68), channel_id=1, source_target_pairs={{96,0},{0,32},{32,64},{64,96},{97,1},{1,33},{33,65},{65,97},{98,2}... | collective-permute-start | bytes 1769480 | tf_op jit(solution)/shard_map/ppermute | solution.py:19
  102.1 29.5 %collective-permute-start.20 = (f32[128,1152]{1,0:T(8,128)}, f32[128,1152]{1,0:T(8,128)}, u32[]{:S(2)}, u32[]{:S(2)}) collective-permute-start(f32[128,1152]{1,0:T(8,128)} %get-tuple-element.69), channel_id=1, source_target_pairs={{64,0},{96,32},{0,64},{32,96},{65,1},{97,33},{1,65},{33,97},{66,2}... | collective-permute-start | bytes 1769480 | tf_op jit(solution)/shard_map/ppermute | solution.py:19
  114.3 25.4 %all-to-all-start.3 = ((f32[4,32,1152]{2,1,0:T(8,128)}), f32[4,32,1152]{2,1,0:T(8,128)S(1)}, u32[]{:S(2)}, u32[]{:S(2)}) async-start(f32[4,32,1152]{2,1,0:T(8,128)} %bitcast.6), calls=%async_computation.3 | async-start | bytes 1179648 | tf_op jit(solution)/shard_map/all_to_all | solution.py:195
  118.6 16.5 %collective-permute-start.21 = (f32[128,1152]{1,0:T(8,128)}, f32[128,1152]{1,0:T(8,128)S(1)}, u32[]{:S(2)}, u32[]{:S(2)}) collective-permute-start(f32[128,1152]{1,0:T(8,128)} %get-tuple-element.70), channel_id=1, source_target_pairs={{32,0},{64,32},{96,64},{0,96},{33,1},{65,33},{97,65},{1,97},{34,2}... | collective-permute-start | bytes 1769480 | tf_op jit(solution)/shard_map/ppermute | solution.py:19
  122.4 17.3 %collective-permute-start.25 = (f32[32,1152]{1,0:T(8,128)}, f32[32,1152]{1,0:T(8,128)}, u32[]{:S(2)}, u32[]{:S(2)}) collective-permute-start(f32[32,1152]{1,0:T(8,128)} %get-tuple-element.81), channel_id=1, source_target_pairs={{96,0},{0,32},{32,64},{64,96},{97,1},{1,33},{33,65},{65,97},{98,2}... | collective-permute-start | bytes 442376 | tf_op jit(solution)/shard_map/ppermute | solution.py:19
  124.0 18.5 %collective-permute-start.27 = (f32[32,1152]{1,0:T(8,128)}, f32[32,1152]{1,0:T(8,128)}, u32[]{:S(2)}, u32[]{:S(2)}) collective-permute-start(f32[32,1152]{1,0:T(8,128)} %get-tuple-element.82), channel_id=1, source_target_pairs={{32,0},{64,32},{96,64},{0,96},{33,1},{65,33},{97,65},{1,97},{34,2}... | collective-permute-start | bytes 442376 | tf_op jit(solution)/shard_map/ppermute | solution.py:19
  131.6 10.9 %collective-permute-start.26 = (f32[32,1152]{1,0:T(8,128)}, f32[32,1152]{1,0:T(8,128)}, u32[]{:S(2)}, u32[]{:S(2)}) collective-permute-start(f32[32,1152]{1,0:T(8,128)} %get-tuple-element.83), channel_id=1, source_target_pairs={{64,0},{96,32},{0,64},{32,96},{65,1},{97,33},{1,65},{33,97},{66,2}... | collective-permute-start | bytes 442376 | tf_op jit(solution)/shard_map/ppermute | solution.py:19
  137.1 10.1 %collective-permute-start.22 = (f32[32,1152]{1,0:T(8,128)}, f32[32,1152]{1,0:T(8,128)S(1)}, u32[]{:S(2)}, u32[]{:S(2)}) collective-permute-start(f32[32,1152]{1,0:T(8,128)} %get-tuple-element.78), channel_id=1, source_target_pairs={{24,0},{0,8},{8,16},{16,24},{25,1},{1,9},{9,17},{17,25},{26,2},{2,... | collective-permute-start | bytes 442376 | tf_op jit(solution)/shard_map/ppermute | solution.py:19
  139.7 8.1 %collective-permute-start.24 = (f32[32,1152]{1,0:T(8,128)}, f32[32,1152]{1,0:T(8,128)S(1)}, u32[]{:S(2)}, u32[]{:S(2)}) collective-permute-start(f32[32,1152]{1,0:T(8,128)} %get-tuple-element.79), channel_id=1, source_target_pairs={{8,0},{16,8},{24,16},{0,24},{9,1},{17,9},{25,17},{1,25},{10,2},{18... | collective-permute-start | bytes 442376 | tf_op jit(solution)/shard_map/ppermute | solution.py:19
  139.7 8.1 %collective-permute-start.23 = (f32[32,1152]{1,0:T(8,128)}, f32[32,1152]{1,0:T(8,128)S(1)}, u32[]{:S(2)}, u32[]{:S(2)}) collective-permute-start(f32[32,1152]{1,0:T(8,128)} %get-tuple-element.80), channel_id=1, source_target_pairs={{16,0},{24,8},{0,16},{8,24},{17,1},{25,9},{1,17},{9,25},{18,2},{26... | collective-permute-start | bytes 442376 | tf_op jit(solution)/shard_map/ppermute | solution.py:19
  (20 other events, 97.3 us)

commit v4 on v3

--- a/solution.py
+++ b/solution.py
@@ -21,6 +21,12 @@
 
 def pulls(value, axis):
     return [value] + [pulled(value, axis, k) for k in (1, 2, 3)]
+
+
+def ring(value, axis):
+    half = value.shape[0] // 2
+    up, down = pulled(value, axis, 1), pulled(value, axis, -1)
+    return [value, up, pulled(up[:half], axis, 1), pulled(down[half:], axis, -1), down]
 
 
 def returned(terms, axis):
@@ -54,11 +60,11 @@
 
 
 def image_kernel(own, other, wanted, held, *refs):
-    blocks, grads, weights_out = refs[:8], refs[8:10], refs[10:]
+    blocks, grads, weights_out = refs[:10], refs[10:12], refs[12:]
     images = parts(jnp.concatenate([own[...], other[...]]))
     terms = 0.0
     for h, out in enumerate(weights_out):
-        captions = parts(jnp.concatenate([r[...] for r in blocks[4 * h : 4 * h + 4]]))
+        captions = parts(jnp.concatenate([r[...] for r in blocks[5 * h : 5 * h + 5]]))
         logits = LOGIT_SCALE * dot3(images, captions, ((1,), (1,))) + LOGIT_BIAS
         signs = jnp.where(wanted[:, :1] == held[h : h + 1, :], 1.0, -1.0).astype(jnp.float32)
         weights = (-LOGIT_SCALE * signs) * jax.nn.sigmoid(-signs * logits)
@@ -72,9 +78,10 @@
 def caption_kernel(own, other, weights, *sums):
     images = parts(jnp.concatenate([own[...], other[...]]))
     caption_terms = dot3(parts(weights[...].T), images, ((1,), (0,)))
-    size = sums[0].shape[0]
-    for k, ref in enumerate(sums):
-        ref[...] = caption_terms[k * size : (k + 1) * size]
+    start = 0
+    for ref in sums:
+        ref[...] = caption_terms[start : start + ref.shape[0]]
+        start += ref.shape[0]
 
 
 def called(kernel, name, shapes, *args, cost=None):
@@ -93,8 +100,9 @@
     return out[:2], out[2], out[3]
 
 
-def caption_terms(images, weights, shape, cost=None):
-    return called(caption_kernel, "caption_terms", [shape] * 4, *images, weights, cost=cost)
+def caption_terms(images, weights, blocks, cost=None):
+    shapes = [blocks[0].shape] * 4
+    return called(caption_kernel, "caption_terms", shapes, *images, weights, cost=cost)
 
 
 def sum_kernel(a, b, c, d, out):
@@ -151,8 +159,8 @@
     near_line = jnp.concatenate(pulls(captions, "x"))
     far_line = jnp.concatenate(pulls(moved, "y"))
     near_line, far_line, arrived = lax.optimization_barrier((near_line, far_line, arrived))
-    near = pulls(near_line, "y")
-    far = pulls(far_line, "x")
+    near = ring(near_line, "y")
+    far = ring(far_line, "x")
     images, image_scale, sent = called(
         image_unit_kernel, "image_rows", [(count, width), (count, 128), partial.shape], arrived
     )
@@ -177,10 +185,10 @@
     held = jnp.concatenate([near_held, far_held])
     grads, near_weights, far_weights = image_terms(chip_images, wanted, held, [*near, *far])
     grads, far_weights = lax.optimization_barrier((grads, far_weights))
-    far_sums = caption_terms(chip_images, far_weights, far[0].shape)
+    far_sums = caption_terms(chip_images, far_weights, far, cost=LONG)
     shard_grad = grads[0] + pulled(grads[1], "c", 1)
     shard_grad, near_weights = lax.optimization_barrier((shard_grad, near_weights))
-    near_sums = caption_terms(chip_images, near_weights, near[0].shape, cost=LONG)
+    near_sums = caption_terms(chip_images, near_weights, near, cost=LONG)
 
     (sent,) = called(
         raw_kernel,

time: 151 us -> 145 us (0.960)
  waiting for transfers between devices: 54.9 us -> 44.1 us
  starting transfers between devices: 60.4 us -> 63.6 us
  Pallas kernels: 16.2 us -> 18.4 us
    ppermute x29 -> x31, waiting for transfers between devices: 42.1 us -> 24.3 us  [pulled(): lax.ppermute(value, axis, [((i + steps) % count, i) for i in range(count)])]
    all_to_all x1, waiting for transfers between devices: 0.01 us -> 7.55 us  [local(): shard_images = lax.all_to_all(sent, 'zh', 0, 0, tiled=True)]
    ppermute x29 -> x31, starting transfers between devices: 36 us -> 41 us  [pulled(): lax.ppermute(value, axis, [((i + steps) % count, i) for i in range(count)])]
    unnamed x22 -> x14, local copies, waits for them, and re-layouts: 6.62 us -> 3.14 us
    slice x0 -> x4, local copies, waits for them, and re-layouts: none -> 2.96 us  [the longest x2 1.96 us: ring(): down[half:]]
    pallas_call x8, Pallas kernels: 16.2 us -> 18.4 us  [called(): pl.pallas_call(kernel, out_shape=[jax.ShapeDtypeStruct(shape, jnp.float32...]
    all_to_all x1, starting transfers between devices: 7.2 us -> 5.12 us  [local(): lax.all_to_all(shard_grad, 'zh', 0, 0, tiled=True)]
  transfers between devices with their start and end apart: 33 -> 35, of which waited for: 15 -> 16; matrix products, arithmetic and copies ran while one was open for 7% -> 9% of each run, Pallas kernels for 6% -> 8%
where the time goes in v4:
time: 145 us; the launch traced here: 144 us
  starting transfers between devices  63.6 us (44%)
  waiting for transfers between devices  44.1 us (30%)
  Pallas kernels  18.4 us (13%)
  local copies, waits for them, and re-layouts  8.03 us (6%)
  matrix products  4.89 us (3%)
  other arithmetic  4.12 us (3%)
    ppermute x31, starting transfers between devices, pulled(): lax.ppermute(value, axis, [((i + steps) % count, i) for i in range(count)])  41 us
    ppermute x31, waiting for transfers between devices, pulled(): lax.ppermute(value, axis, [((i + steps) % count, i) for i in range(count)])  24.3 us
    pallas_call x8, Pallas kernels, called(): pl.pallas_call(kernel, out_shape=[jax.ShapeDtypeStruct(shape, jnp.float32...  18.4 us
    all_to_all x1, waiting for transfers between devices, local(): lax.all_to_all(shard_grad, 'zh', 0, 0, tiled=True)  9.59 us
    all_to_all x1, starting transfers between devices, local(): arrived = lax.all_to_all(partial, 'zh', 0, 0, tiled=True)  8.28 us
    all_to_all x1, waiting for transfers between devices, local(): shard_images = lax.all_to_all(sent, 'zh', 0, 0, tiled=True)  7.55 us
    all_to_all x1, starting transfers between devices, local(): lax.all_to_all(shard_grad, 'zh', 0, 0, tiled=True)  5.12 us
    dot_general x2, matrix products, product(): lax.dot_general(left, right, (dims, ((), ())), precision=lax.Precision.HI...  4.89 us
  transfers between devices with their start and end apart: 35, of which 16 were waited for; matrix products, arithmetic and copies ran while one was open for 9% of the time, Pallas kernels for 8%

profile of v4, /device:TPU:6, one launch (start us, length us, event | category | flops | bytes accessed | tf_op | source)
XLA Modules:
  0.0 143.9 jit_solution(399435549081578949)
XLA Ops:
  1.8 2.0 %collective-permute-start.3 = (f32[32,1152]{1,0:T(8,128)S(1)}, f32[32,1152]{1,0:T(8,128)S(1)}, u32[]{:S(2)}, u32[]{:S(2)}) collective-permute-start(f32[32,1152]{1,0:T(8,128)S(1)} %get-tuple-element.39), channel_id=1, source_target_pairs={{128,0},{0,128},{129,1},{1,129},{130,2},{2,130},{131,3},{3,131},{1... | collective-permute-start | bytes 442376 | tf_op jit(solution)/shard_map/ppermute | solution.py:19
  3.8 3.0 %fusion.8 = f32[128,1152]{1,0:T(8,128)} fusion(f32[128,288]{0,1:T(8,128)} %param.4, f32[288,1152]{1,0:T(8,128)S(1)} %copy-done), kind=kOutput, calls=%fused_computation.28 | convolution fusion | flops 509607936 | bytes 2064384 | tf_op jit(solution)/shard_map/dot_general | solution.py:37
  7.6 8.3 %all-to-all-start = ((f32[4,32,1152]{2,1,0:T(8,128)}), f32[4,32,1152]{2,1,0:T(8,128)S(1)}, u32[]{:S(2)}, u32[]{:S(2)}) async-start(f32[4,32,1152]{2,1,0:T(8,128)} %bitcast), calls=%async_computation | async-start | bytes 1179648 | tf_op jit(solution)/shard_map/all_to_all | solution.py:157
  16.4 2.4 %collective-permute-start.1 = (f32[32,1152]{1,0:T(8,128)S(1)}, f32[32,1152]{1,0:T(8,128)S(1)}, u32[]{:S(2)}, u32[]{:S(2)}) collective-permute-start(f32[32,1152]{1,0:T(8,128)S(1)} %get-tuple-element.39), channel_id=1, source_target_pairs={{16,0},{24,8},{0,16},{8,24},{17,1},{25,9},{1,17},{9,25},{18,2},{26... | collective-permute-start | bytes 442376 | tf_op jit(solution)/shard_map/ppermute | solution.py:19
  20.4 2.9 %collective-permute-start.5 = (f32[32,1152]{1,0:T(8,128)S(1)}, f32[32,1152]{1,0:T(8,128)S(1)}, u32[]{:S(2)}, u32[]{:S(2)}) collective-permute-start(f32[32,1152]{1,0:T(8,128)S(1)} %collective-permute-done.3), channel_id=1, source_target_pairs={{64,0},{96,32},{0,64},{32,96},{65,1},{97,33},{1,65},{33,97},{66,2}... | collective-permute-start | bytes 442376 | tf_op jit(solution)/shard_map/ppermute | solution.py:19
  29.3 2.6 %all-to-all-done = f32[4,32,1152]{2,1,0:T(8,128)S(1)} async-done(((f32[4,32,1152]{2,1,0:T(8,128)}), f32[4,32,1152]{2,1,0:T(8,128)S(1)}, u32[]{:S(2)}, u32[]{:S(2)}) %all-to-all-start) | async-done | bytes 589856 | tf_op jit(solution)/shard_map/all_to_all | solution.py:157
  32.9 4.6 %all-to-all-start.1 = ((f32[4,32,1152]{2,1,0:T(8,128)}), f32[4,32,1152]{2,1,0:T(8,128)S(1)}, u32[]{:S(2)}, u32[]{:S(2)}) async-start(f32[4,32,1152]{2,1,0:T(8,128)} %bitcast.2), calls=%async_computation.1 | async-start | bytes 1179648 | tf_op jit(solution)/shard_map/all_to_all | solution.py:167
  40.8 3.2 %collective-permute-start.15 = (f32[128,1152]{1,0:T(8,128)}, f32[128,1152]{1,0:T(8,128)}, u32[]{:S(2)}, u32[]{:S(2)}) collective-permute-start(f32[128,1152]{1,0:T(8,128)} %pad_maximum_fusion.1.refs_5_), channel_id=1, source_target_pairs={{24,0},{0,8},{8,16},{16,24},{25,1},{1,9},{9,17},{17,25},{26,2},{2,... | collective-permute-start | bytes 1769480 | tf_op jit(solution)/shard_map/ppermute | solution.py:19
  44.1 7.6 %all-to-all-done.1 = f32[4,32,1152]{2,1,0:T(8,128)S(1)} async-done(((f32[4,32,1152]{2,1,0:T(8,128)}), f32[4,32,1152]{2,1,0:T(8,128)S(1)}, u32[]{:S(2)}, u32[]{:S(2)}) %all-to-all-start.1) | async-done | bytes 589856 | tf_op jit(solution)/shard_map/all_to_all | solution.py:167
  58.2 3.1 %collective-permute-start.16 = (f32[64,1152]{1,0:T(8,128)S(1)}, f32[64,1152]{1,0:T(8,128)S(1)}, u32[]{:S(2)}, u32[]{:S(2)}) collective-permute-start(f32[64,1152]{1,0:T(8,128)S(1)} %slice.55), channel_id=1, source_target_pairs={{24,0},{0,8},{8,16},{16,24},{25,1},{1,9},{9,17},{17,25},{26,2},{2,... | collective-permute-start | bytes 884744 | tf_op jit(solution)/shard_map/ppermute | solution.py:19
  64.2 2.9 %collective-permute-done.16.refs_8_ = f32[64,1152]{1,0:T(8,128)S(1)} collective-permute-done((f32[64,1152]{1,0:T(8,128)S(1)}, f32[64,1152]{1,0:T(8,128)S(1)}, u32[]{:S(2)}, u32[]{:S(2)}) %collective-permute-start.16) | collective-permute-done | bytes 294944 | tf_op jit(solution)/shard_map/ppermute | solution.py:19
  67.1 4.5 %collective-permute-done.14.refs_7_ = f32[64,1152]{1,0:T(8,128)S(1)} collective-permute-done((f32[64,1152]{1,0:T(8,128)S(1)}, f32[64,1152]{1,0:T(8,128)S(1)}, u32[]{:S(2)}, u32[]{:S(2)}) %collective-permute-start.14) | collective-permute-done | bytes 294944 | tf_op jit(solution)/shard_map/ppermute | solution.py:19
  71.7 6.4 %image_terms.1 = (f32[128,1152]{1,0:T(8,128)S(1)}, f32[128,1152]{1,0:T(8,128)S(1)}, f32[256,512]{1,0:T(8,128)S(1)}, f32[256,512]{1,0:T(8,128)S(1)}) custom-call(f32[128,1152]{1,0:T(8,128)S(1)} %bitcast.13, f32[128,1152]{1,0:T(8,128)} %collective-permute-done.7.other, f32[256,128]{1,0:T(8,128)S(1)} %broadcast_in_dim.2.wanted, ...), custom_call_target="tpu_custom_call" | custom-call | tf_op jit(solution)/shard_map/image_terms/pallas_call | solution.py:88
  78.2 3.6 %caption_terms.2 = (f32[128,1152]{1,0:T(8,128)S(1)}, f32[128,1152]{1,0:T(8,128)}, f32[128,1152]{1,0:T(8,128)}, f32[128,1152]{1,0:T(8,128)}) custom-call(f32[128,1152]{1,0:T(8,128)S(1)} %bitcast.14, f32[128,1152]{1,0:T(8,128)} %collective-permute-done.7.other, f32[256,512]{1,0:T(8,128)S(1)} %get-tuple-element.49.weights), custom_call_target="tpu_custom_call" | custom-call | flops 30000001024 | bytes 100000000 | tf_op jit(solution)/shard_map/caption_terms/pallas_call | solution.py:88
  84.8 5.1 %all-to-all-start.2 = ((f32[4,32,1152]{2,1,0:T(8,128)}), f32[4,32,1152]{2,1,0:T(8,128)S(1)}, u32[]{:S(2)}, u32[]{:S(2)}) async-start(f32[4,32,1152]{2,1,0:T(8,128)} %bitcast.18), calls=%async_computation.2 | async-start | bytes 1179648 | tf_op jit(solution)/shard_map/all_to_all | solution.py:197
  91.0 3.4 %caption_terms.3 = (f32[128,1152]{1,0:T(8,128)S(1)}, f32[128,1152]{1,0:T(8,128)}, f32[128,1152]{1,0:T(8,128)}, f32[128,1152]{1,0:T(8,128)}) custom-call(f32[128,1152]{1,0:T(8,128)S(1)} %bitcast.15, f32[128,1152]{1,0:T(8,128)} %collective-permute-done.7.other, f32[256,512]{1,0:T(8,128)S(1)} %copy-done.3), custom_call_target="tpu_custom_call" | custom-call | flops 30000001024 | bytes 100000000 | tf_op jit(solution)/shard_map/caption_terms/pallas_call | solution.py:88
  96.2 9.6 %all-to-all-done.2 = f32[4,32,1152]{2,1,0:T(8,128)S(1)} async-done(((f32[4,32,1152]{2,1,0:T(8,128)}), f32[4,32,1152]{2,1,0:T(8,128)S(1)}, u32[]{:S(2)}, u32[]{:S(2)}) %all-to-all-start.2) | async-done | bytes 589856 | tf_op jit(solution)/shard_map/all_to_all | solution.py:197
  106.7 4.6 %all-to-all-start.3 = ((f32[4,32,1152]{2,1,0:T(8,128)}), f32[4,32,1152]{2,1,0:T(8,128)S(1)}, u32[]{:S(2)}, u32[]{:S(2)}) async-start(f32[4,32,1152]{2,1,0:T(8,128)} %bitcast.6), calls=%async_computation.3 | async-start | bytes 1179648 | tf_op jit(solution)/shard_map/all_to_all | solution.py:203
  118.6 7.1 %collective-permute-done.21.b = f32[128,1152]{1,0:T(8,128)} collective-permute-done((f32[128,1152]{1,0:T(8,128)}, f32[128,1152]{1,0:T(8,128)}, u32[]{:S(2)}, u32[]{:S(2)}) %collective-permute-start.21) | collective-permute-done | bytes 589856 | tf_op jit(solution)/shard_map/ppermute | solution.py:19
  125.7 2.1 %collective-permute-done.23.d = f32[128,1152]{1,0:T(8,128)S(1)} collective-permute-done((f32[128,1152]{1,0:T(8,128)}, f32[128,1152]{1,0:T(8,128)S(1)}, u32[]{:S(2)}, u32[]{:S(2)}) %collective-permute-start.23) | collective-permute-done | bytes 589856 | tf_op jit(solution)/shard_map/ppermute | solution.py:19
  130.0 2.7 %collective-permute-start.24 = (f32[32,1152]{1,0:T(8,128)}, f32[32,1152]{1,0:T(8,128)S(1)}, u32[]{:S(2)}, u32[]{:S(2)}) collective-permute-start(f32[32,1152]{1,0:T(8,128)} %get-tuple-element.78), channel_id=1, source_target_pairs={{24,0},{0,8},{8,16},{16,24},{25,1},{1,9},{9,17},{17,25},{26,2},{2,... | collective-permute-start | bytes 442376 | tf_op jit(solution)/shard_map/ppermute | solution.py:19
  132.7 2.8 %collective-permute-start.25 = (f32[32,1152]{1,0:T(8,128)}, f32[32,1152]{1,0:T(8,128)S(1)}, u32[]{:S(2)}, u32[]{:S(2)}) collective-permute-start(f32[32,1152]{1,0:T(8,128)} %get-tuple-element.80), channel_id=1, source_target_pairs={{16,0},{24,8},{0,16},{8,24},{17,1},{25,9},{1,17},{9,25},{18,2},{26... | collective-permute-start | bytes 442376 | tf_op jit(solution)/shard_map/ppermute | solution.py:19
  136.5 3.3 %collective-permute-start.30 = (f32[32,1152]{1,0:T(8,128)S(1)}, f32[32,1152]{1,0:T(8,128)S(1)}, u32[]{:S(2)}, u32[]{:S(2)}) collective-permute-start(f32[32,1152]{1,0:T(8,128)S(1)} %add_add_fusion), channel_id=1, source_target_pairs={{128,0},{0,128},{129,1},{1,129},{130,2},{2,130},{131,3},{3,131},{1... | collective-permute-start | bytes 442376 | tf_op jit(solution)/shard_map/ppermute | solution.py:19
  139.9 1.9 %fusion.9 = f32[128,288]{0,1:T(8,128)} fusion(f32[128,1152]{1,0:T(8,128)S(1)} %bitcast.19, f32[288,1152]{1,0:T(8,128)S(1)} %copy-done), kind=kOutput, calls=%fused_computation.29 | convolution fusion | flops 509607936 | bytes 2064384 | tf_op jit(solution)/shard_map/dot_general | solution.py:37
  (94 shorter events, 43.4 us)
Async XLA Ops:
  7.6 24.3 %all-to-all-start = ((f32[4,32,1152]{2,1,0:T(8,128)}), f32[4,32,1152]{2,1,0:T(8,128)S(1)}, u32[]{:S(2)}, u32[]{:S(2)}) async-start(f32[4,32,1152]{2,1,0:T(8,128)} %bitcast), calls=%async_computation | async-start | bytes 1179648 | tf_op jit(solution)/shard_map/all_to_all | solution.py:157
  32.9 18.8 %all-to-all-start.1 = ((f32[4,32,1152]{2,1,0:T(8,128)}), f32[4,32,1152]{2,1,0:T(8,128)S(1)}, u32[]{:S(2)}, u32[]{:S(2)}) async-start(f32[4,32,1152]{2,1,0:T(8,128)} %bitcast.2), calls=%async_computation.1 | async-start | bytes 1179648 | tf_op jit(solution)/shard_map/all_to_all | solution.py:167
  37.5 14.5 %collective-permute-start.11 = (f32[128,1152]{1,0:T(8,128)S(1)}, f32[128,1152]{1,0:T(8,128)}, u32[]{:S(2)}, u32[]{:S(2)}) collective-permute-start(f32[128,1152]{1,0:T(8,128)S(1)} %pad_maximum_fusion.refs_0_), channel_id=1, source_target_pairs={{96,0},{0,32},{32,64},{64,96},{97,1},{1,33},{33,65},{65,97},{98,2}... | collective-permute-start | bytes 1769480 | tf_op jit(solution)/shard_map/ppermute | solution.py:19
  39.1 14.4 %collective-permute-start.9 = (f32[128,1152]{1,0:T(8,128)S(1)}, f32[128,1152]{1,0:T(8,128)S(1)}, u32[]{:S(2)}, u32[]{:S(2)}) collective-permute-start(f32[128,1152]{1,0:T(8,128)S(1)} %pad_maximum_fusion.refs_0_), channel_id=1, source_target_pairs={{32,0},{64,32},{96,64},{0,96},{33,1},{65,33},{97,65},{1,97},{34,2}... | collective-permute-start | bytes 1769480 | tf_op jit(solution)/shard_map/ppermute | solution.py:19
  40.8 14.4 %collective-permute-start.15 = (f32[128,1152]{1,0:T(8,128)}, f32[128,1152]{1,0:T(8,128)}, u32[]{:S(2)}, u32[]{:S(2)}) collective-permute-start(f32[128,1152]{1,0:T(8,128)} %pad_maximum_fusion.1.refs_5_), channel_id=1, source_target_pairs={{24,0},{0,8},{8,16},{16,24},{25,1},{1,9},{9,17},{17,25},{26,2},{2,... | collective-permute-start | bytes 1769480 | tf_op jit(solution)/shard_map/ppermute | solution.py:19
  44.1 14.1 %collective-permute-start.13 = (f32[128,1152]{1,0:T(8,128)}, f32[128,1152]{1,0:T(8,128)}, u32[]{:S(2)}, u32[]{:S(2)}) collective-permute-start(f32[128,1152]{1,0:T(8,128)} %pad_maximum_fusion.1.refs_5_), channel_id=1, source_target_pairs={{8,0},{16,8},{24,16},{0,24},{9,1},{17,9},{25,17},{1,25},{10,2},{18... | collective-permute-start | bytes 1769480 | tf_op jit(solution)/shard_map/ppermute | solution.py:19
  51.7 19.9 %collective-permute-start.7 = (f32[128,1152]{1,0:T(8,128)S(1)}, f32[128,1152]{1,0:T(8,128)}, u32[]{:S(2)}, u32[]{:S(2)}) collective-permute-start(f32[128,1152]{1,0:T(8,128)S(1)} %bitcast.12), channel_id=1, source_target_pairs={{4,0},{0,4},{5,1},{1,5},{6,2},{2,6},{7,3},{3,7},{12,8},{8,12},{13,... | collective-permute-start | bytes 1769480 | tf_op jit(solution)/shard_map/ppermute | solution.py:19
  52.0 10.2 %collective-permute-start.8 = (f32[128]{0:T(128)S(1)}, f32[128]{0:T(128)S(1)}, u32[]{:S(2)}, u32[]{:S(2)}) collective-permute-start(f32[128]{0:T(128)S(1)} %convert_element_type.31), channel_id=1, source_target_pairs={{4,0},{0,4},{5,1},{1,5},{6,2},{2,6},{7,3},{3,7},{12,8},{8,12},{13,... | collective-permute-start | bytes 1544 | tf_op jit(solution)/shard_map/ppermute | solution.py:19
  53.6 10.3 %collective-permute-start.12 = (f32[64,1152]{1,0:T(8,128)S(1)}, f32[64,1152]{1,0:T(8,128)S(1)}, u32[]{:S(2)}, u32[]{:S(2)}) collective-permute-start(f32[64,1152]{1,0:T(8,128)S(1)} %slice.53), channel_id=1, source_target_pairs={{96,0},{0,32},{32,64},{64,96},{97,1},{1,33},{33,65},{65,97},{98,2}... | collective-permute-start | bytes 884744 | tf_op jit(solution)/shard_map/ppermute | solution.py:19
  62.2 9.4 %collective-permute-start.14 = (f32[64,1152]{1,0:T(8,128)S(1)}, f32[64,1152]{1,0:T(8,128)S(1)}, u32[]{:S(2)}, u32[]{:S(2)}) collective-permute-start(f32[64,1152]{1,0:T(8,128)S(1)} %slice.54), channel_id=1, source_target_pairs={{8,0},{16,8},{24,16},{0,24},{9,1},{17,9},{25,17},{1,25},{10,2},{18... | collective-permute-start | bytes 884744 | tf_op jit(solution)/shard_map/ppermute | solution.py:19
  81.8 29.5 %collective-permute-start.17 = (f32[128,1152]{1,0:T(8,128)}, f32[128,1152]{1,0:T(8,128)}, u32[]{:S(2)}, u32[]{:S(2)}) collective-permute-start(f32[128,1152]{1,0:T(8,128)} %get-tuple-element.51), channel_id=1, source_target_pairs={{24,0},{0,8},{8,16},{16,24},{25,1},{1,9},{9,17},{17,25},{26,2},{2,... | collective-permute-start | bytes 1769480 | tf_op jit(solution)/shard_map/ppermute | solution.py:19
  81.8 29.8 %collective-permute-start.18 = (f32[128,1152]{1,0:T(8,128)}, f32[128,1152]{1,0:T(8,128)}, u32[]{:S(2)}, u32[]{:S(2)}) collective-permute-start(f32[128,1152]{1,0:T(8,128)} %get-tuple-element.52), channel_id=1, source_target_pairs={{16,0},{24,8},{0,16},{8,24},{17,1},{25,9},{1,17},{9,25},{18,2},{26... | collective-permute-start | bytes 1769480 | tf_op jit(solution)/shard_map/ppermute | solution.py:19
  82.9 29.1 %collective-permute-start.19 = (f32[128,1152]{1,0:T(8,128)}, f32[128,1152]{1,0:T(8,128)}, u32[]{:S(2)}, u32[]{:S(2)}) collective-permute-start(f32[128,1152]{1,0:T(8,128)} %get-tuple-element.53), channel_id=1, source_target_pairs={{8,0},{16,8},{24,16},{0,24},{9,1},{17,9},{25,17},{1,25},{10,2},{18... | collective-permute-start | bytes 1769480 | tf_op jit(solution)/shard_map/ppermute | solution.py:19
  84.8 21.0 %all-to-all-start.2 = ((f32[4,32,1152]{2,1,0:T(8,128)}), f32[4,32,1152]{2,1,0:T(8,128)S(1)}, u32[]{:S(2)}, u32[]{:S(2)}) async-start(f32[4,32,1152]{2,1,0:T(8,128)} %bitcast.18), calls=%async_computation.2 | async-start | bytes 1179648 | tf_op jit(solution)/shard_map/all_to_all | solution.py:197
  94.4 31.3 %collective-permute-start.21 = (f32[128,1152]{1,0:T(8,128)}, f32[128,1152]{1,0:T(8,128)}, u32[]{:S(2)}, u32[]{:S(2)}) collective-permute-start(f32[128,1152]{1,0:T(8,128)} %get-tuple-element.68), channel_id=1, source_target_pairs={{96,0},{0,32},{32,64},{64,96},{97,1},{1,33},{33,65},{65,97},{98,2}... | collective-permute-start | bytes 1769480 | tf_op jit(solution)/shard_map/ppermute | solution.py:19
  94.4 31.3 %collective-permute-start.22 = (f32[128,1152]{1,0:T(8,128)}, f32[128,1152]{1,0:T(8,128)}, u32[]{:S(2)}, u32[]{:S(2)}) collective-permute-start(f32[128,1152]{1,0:T(8,128)} %get-tuple-element.69), channel_id=1, source_target_pairs={{64,0},{96,32},{0,64},{32,96},{65,1},{97,33},{1,65},{33,97},{66,2}... | collective-permute-start | bytes 1769480 | tf_op jit(solution)/shard_map/ppermute | solution.py:19
  106.7 25.9 %all-to-all-start.3 = ((f32[4,32,1152]{2,1,0:T(8,128)}), f32[4,32,1152]{2,1,0:T(8,128)S(1)}, u32[]{:S(2)}, u32[]{:S(2)}) async-start(f32[4,32,1152]{2,1,0:T(8,128)} %bitcast.6), calls=%async_computation.3 | async-start | bytes 1179648 | tf_op jit(solution)/shard_map/all_to_all | solution.py:203
  111.3 16.5 %collective-permute-start.23 = (f32[128,1152]{1,0:T(8,128)}, f32[128,1152]{1,0:T(8,128)S(1)}, u32[]{:S(2)}, u32[]{:S(2)}) collective-permute-start(f32[128,1152]{1,0:T(8,128)} %get-tuple-element.70), channel_id=1, source_target_pairs={{32,0},{64,32},{96,64},{0,96},{33,1},{65,33},{97,65},{1,97},{34,2}... | collective-permute-start | bytes 1769480 | tf_op jit(solution)/shard_map/ppermute | solution.py:19
  115.4 17.3 %collective-permute-start.27 = (f32[32,1152]{1,0:T(8,128)}, f32[32,1152]{1,0:T(8,128)}, u32[]{:S(2)}, u32[]{:S(2)}) collective-permute-start(f32[32,1152]{1,0:T(8,128)} %get-tuple-element.81), channel_id=1, source_target_pairs={{96,0},{0,32},{32,64},{64,96},{97,1},{1,33},{33,65},{65,97},{98,2}... | collective-permute-start | bytes 442376 | tf_op jit(solution)/shard_map/ppermute | solution.py:19
  116.7 18.7 %collective-permute-start.29 = (f32[32,1152]{1,0:T(8,128)}, f32[32,1152]{1,0:T(8,128)}, u32[]{:S(2)}, u32[]{:S(2)}) collective-permute-start(f32[32,1152]{1,0:T(8,128)} %get-tuple-element.82), channel_id=1, source_target_pairs={{32,0},{64,32},{96,64},{0,96},{33,1},{65,33},{97,65},{1,97},{34,2}... | collective-permute-start | bytes 442376 | tf_op jit(solution)/shard_map/ppermute | solution.py:19
  125.7 9.7 %collective-permute-start.28 = (f32[32,1152]{1,0:T(8,128)}, f32[32,1152]{1,0:T(8,128)}, u32[]{:S(2)}, u32[]{:S(2)}) collective-permute-start(f32[32,1152]{1,0:T(8,128)} %get-tuple-element.83), channel_id=1, source_target_pairs={{64,0},{96,32},{0,64},{32,96},{65,1},{97,33},{1,65},{33,97},{66,2}... | collective-permute-start | bytes 442376 | tf_op jit(solution)/shard_map/ppermute | solution.py:19
  130.0 11.8 %collective-permute-start.24 = (f32[32,1152]{1,0:T(8,128)}, f32[32,1152]{1,0:T(8,128)S(1)}, u32[]{:S(2)}, u32[]{:S(2)}) collective-permute-start(f32[32,1152]{1,0:T(8,128)} %get-tuple-element.78), channel_id=1, source_target_pairs={{24,0},{0,8},{8,16},{16,24},{25,1},{1,9},{9,17},{17,25},{26,2},{2,... | collective-permute-start | bytes 442376 | tf_op jit(solution)/shard_map/ppermute | solution.py:19
  132.6 9.1 %collective-permute-start.26 = (f32[32,1152]{1,0:T(8,128)}, f32[32,1152]{1,0:T(8,128)S(1)}, u32[]{:S(2)}, u32[]{:S(2)}) collective-permute-start(f32[32,1152]{1,0:T(8,128)} %get-tuple-element.79), channel_id=1, source_target_pairs={{8,0},{16,8},{24,16},{0,24},{9,1},{17,9},{25,17},{1,25},{10,2},{18... | collective-permute-start | bytes 442376 | tf_op jit(solution)/shard_map/ppermute | solution.py:19
  132.7 9.1 %collective-permute-start.25 = (f32[32,1152]{1,0:T(8,128)}, f32[32,1152]{1,0:T(8,128)S(1)}, u32[]{:S(2)}, u32[]{:S(2)}) collective-permute-start(f32[32,1152]{1,0:T(8,128)} %get-tuple-element.80), channel_id=1, source_target_pairs={{16,0},{24,8},{0,16},{8,24},{17,1},{25,9},{1,17},{9,25},{18,2},{26... | collective-permute-start | bytes 442376 | tf_op jit(solution)/shard_map/ppermute | solution.py:19
  (18 other events, 118.7 us)

commit v5 on v4

--- a/solution.py
+++ b/solution.py
@@ -27,6 +27,14 @@
     half = value.shape[0] // 2
     up, down = pulled(value, axis, 1), pulled(value, axis, -1)
     return [value, up, pulled(up[:half], axis, 1), pulled(down[half:], axis, -1), down]
+
+
+def ring_back(terms, axis):
+    own, up, far_up, far_down, down = terms
+    half = far_up.shape[0]
+    up = jnp.concatenate([up[:half] + pulled(far_up, axis, -1), up[half:]])
+    down = jnp.concatenate([down[:half], down[half:] + pulled(far_down, axis, 1)])
+    return [own, pulled(up, axis, -1), pulled(down, axis, 1)]
 
 
 def returned(terms, axis):
@@ -101,12 +109,12 @@
 
 
 def caption_terms(images, weights, blocks, cost=None):
-    shapes = [blocks[0].shape] * 4
+    shapes = [block.shape for block in blocks]
     return called(caption_kernel, "caption_terms", shapes, *images, weights, cost=cost)
 
 
-def sum_kernel(a, b, c, d, out):
-    out[...] = (a[...] + b[...]) + (c[...] + d[...])
+def sum_kernel(*refs):
+    refs[-1][...] = sum(ref[...] for ref in refs[:-1])
 
 
 def summed(parts, cost=None):
@@ -185,7 +193,7 @@
     held = jnp.concatenate([near_held, far_held])
     grads, near_weights, far_weights = image_terms(chip_images, wanted, held, [*near, *far])
     grads, far_weights = lax.optimization_barrier((grads, far_weights))
-    far_sums = caption_terms(chip_images, far_weights, far, cost=LONG)
+    far_sums = caption_terms(chip_images, far_weights, far[:1] * 4, cost=LONG)
     shard_grad = grads[0] + pulled(grads[1], "c", 1)
     shard_grad, near_weights = lax.optimization_barrier((shard_grad, near_weights))
     near_sums = caption_terms(chip_images, near_weights, near, cost=LONG)
@@ -198,7 +206,7 @@
         images,
         image_scale,
     )
-    near_parts = [near_sums[0]] + [pulled(near_sums[k], "y", -k) for k in (1, 2, 3)]
+    near_parts = ring_back(near_sums, "y")
     far_parts = [far_sums[0]] + [pulled(far_sums[k], "x", -k) for k in (1, 2, 3)]
     raw_rows = lax.all_to_all(sent, "zh", 0, 0, tiled=True)
 

time: 145 us -> 148 us (1.021)
  waiting for transfers between devices: 44.1 us -> 36.2 us
  other arithmetic: 4.12 us -> 10.4 us
  local copies, waits for them, and re-layouts: 8.03 us -> 13.7 us
  starting transfers between devices: 63.6 us -> 61.8 us
    ppermute x31 -> x32, waiting for transfers between devices: 24.3 us -> 19.6 us  [pulled(): lax.ppermute(value, axis, [((i + steps) % count, i) for i in range(count)])]
    all_to_all x1, waiting for transfers between devices: 9.59 us -> 5.73 us  [local(): lax.all_to_all(shard_grad, 'zh', 0, 0, tiled=True)]
    convert_element_type x2, local copies, waits for them, and re-layouts: 0.17 us -> 2.71 us  [numbers(): return held.reshape(1, -1).astype(jnp.float32)]
    concatenate x0 -> x2, other arithmetic: none -> 1.72 us  [the longest x1 0.86 us: ring_back(): up = jnp.concatenate([up[:half] + pulled(far_up, axis, -1), up[half:]])]
    all_to_all x1, waiting for transfers between devices: 0.01 us -> 1.71 us  [local(): raw_rows = lax.all_to_all(sent, 'zh', 0, 0, tiled=True)]
    all_to_all x1, starting transfers between devices: 5.12 us -> 3.52 us  [local(): lax.all_to_all(shard_grad, 'zh', 0, 0, tiled=True)]
    unnamed x14 -> x26, local copies, waits for them, and re-layouts: 3.14 us -> 3.61 us
    ppermute x31 -> x32, starting transfers between devices: 41 us -> 41.2 us  [pulled(): lax.ppermute(value, axis, [((i + steps) % count, i) for i in range(count)])]
  transfers between devices with their start and end apart: 35 -> 36, of which waited for: 16 -> 15; matrix products, arithmetic and copies ran while one was open for 9% -> 17% of each run, Pallas kernels for 8% -> 5%
where the time goes in v5:
time: 148 us; the launch traced here: 147 us
  starting transfers between devices  61.8 us (42%)
  waiting for transfers between devices  36.2 us (24%)
  Pallas kernels  17.8 us (12%)
  local copies, waits for them, and re-layouts  13.7 us (9%)
  other arithmetic  10.4 us (7%)
  matrix products  5.97 us (4%)
    ppermute x32, starting transfers between devices, pulled(): lax.ppermute(value, axis, [((i + steps) % count, i) for i in range(count)])  41.2 us
    ppermute x32, waiting for transfers between devices, pulled(): lax.ppermute(value, axis, [((i + steps) % count, i) for i in range(count)])  19.6 us
    pallas_call x8, Pallas kernels, called(): pl.pallas_call(kernel, out_shape=[jax.ShapeDtypeStruct(shape, jnp.float32...  17.8 us
    all_to_all x1, starting transfers between devices, local(): arrived = lax.all_to_all(partial, 'zh', 0, 0, tiled=True)  8.28 us
    all_to_all x1, waiting for transfers between devices, local(): shard_images = lax.all_to_all(sent, 'zh', 0, 0, tiled=True)  6.52 us
    dot_general x2, matrix products, product(): lax.dot_general(left, right, (dims, ((), ())), precision=lax.Precision.HI...  5.97 us
    all_to_all x1, waiting for transfers between devices, local(): lax.all_to_all(shard_grad, 'zh', 0, 0, tiled=True)  5.73 us
    all_to_all x1, starting transfers between devices, local(): shard_images = lax.all_to_all(sent, 'zh', 0, 0, tiled=True)  4.56 us
  transfers between devices with their start and end apart: 36, of which 15 were waited for; matrix products, arithmetic and copies ran while one was open for 17% of the time, Pallas kernels for 5%

profile of v5, /device:TPU:6, one launch (start us, length us, event | category | flops | bytes accessed | tf_op | source)
XLA Modules:
  0.0 146.8 jit_solution(1322518907541443807)
XLA Ops:
  1.8 2.0 %collective-permute-start.3 = (f32[32,1152]{1,0:T(8,128)S(1)}, f32[32,1152]{1,0:T(8,128)S(1)}, u32[]{:S(2)}, u32[]{:S(2)}) collective-permute-start(f32[32,1152]{1,0:T(8,128)S(1)} %get-tuple-element.39), channel_id=1, source_target_pairs={{128,0},{0,128},{129,1},{1,129},{130,2},{2,130},{131,3},{3,131},{1... | collective-permute-start | bytes 442376 | tf_op jit(solution)/shard_map/ppermute | solution.py:19
  3.8 3.0 %fusion.9 = f32[128,1152]{1,0:T(8,128)} fusion(f32[128,288]{0,1:T(8,128)} %param.4, f32[288,1152]{1,0:T(8,128)S(1)} %copy-done), kind=kOutput, calls=%fused_computation.33 | convolution fusion | flops 509607936 | bytes 2064384 | tf_op jit(solution)/shard_map/dot_general | solution.py:45
  7.6 8.3 %all-to-all-start = ((f32[4,32,1152]{2,1,0:T(8,128)}), f32[4,32,1152]{2,1,0:T(8,128)S(1)}, u32[]{:S(2)}, u32[]{:S(2)}) async-start(f32[4,32,1152]{2,1,0:T(8,128)} %bitcast), calls=%async_computation | async-start | bytes 1179648 | tf_op jit(solution)/shard_map/all_to_all | solution.py:165
  16.4 2.4 %collective-permute-start.1 = (f32[32,1152]{1,0:T(8,128)S(1)}, f32[32,1152]{1,0:T(8,128)S(1)}, u32[]{:S(2)}, u32[]{:S(2)}) collective-permute-start(f32[32,1152]{1,0:T(8,128)S(1)} %get-tuple-element.39), channel_id=1, source_target_pairs={{16,0},{24,8},{0,16},{8,24},{17,1},{25,9},{1,17},{9,25},{18,2},{26... | collective-permute-start | bytes 442376 | tf_op jit(solution)/shard_map/ppermute | solution.py:19
  20.4 2.9 %collective-permute-start.5 = (f32[32,1152]{1,0:T(8,128)S(1)}, f32[32,1152]{1,0:T(8,128)S(1)}, u32[]{:S(2)}, u32[]{:S(2)}) collective-permute-start(f32[32,1152]{1,0:T(8,128)S(1)} %collective-permute-done.3), channel_id=1, source_target_pairs={{64,0},{96,32},{0,64},{32,96},{65,1},{97,33},{1,65},{33,97},{66,2}... | collective-permute-start | bytes 442376 | tf_op jit(solution)/shard_map/ppermute | solution.py:19
  29.3 2.6 %all-to-all-done = f32[4,32,1152]{2,1,0:T(8,128)S(1)} async-done(((f32[4,32,1152]{2,1,0:T(8,128)}), f32[4,32,1152]{2,1,0:T(8,128)S(1)}, u32[]{:S(2)}, u32[]{:S(2)}) %all-to-all-start) | async-done | bytes 589856 | tf_op jit(solution)/shard_map/all_to_all | solution.py:165
  33.6 4.6 %all-to-all-start.1 = ((f32[4,32,1152]{2,1,0:T(8,128)}), f32[4,32,1152]{2,1,0:T(8,128)S(1)}, u32[]{:S(2)}, u32[]{:S(2)}) async-start(f32[4,32,1152]{2,1,0:T(8,128)} %bitcast.2), calls=%async_computation.1 | async-start | bytes 1179648 | tf_op jit(solution)/shard_map/all_to_all | solution.py:175
  41.4 3.2 %collective-permute-start.15 = (f32[128,1152]{1,0:T(8,128)}, f32[128,1152]{1,0:T(8,128)}, u32[]{:S(2)}, u32[]{:S(2)}) collective-permute-start(f32[128,1152]{1,0:T(8,128)} %pad_maximum_fusion.1.refs_5_), channel_id=1, source_target_pairs={{24,0},{0,8},{8,16},{16,24},{25,1},{1,9},{9,17},{17,25},{26,2},{2,... | collective-permute-start | bytes 1769480 | tf_op jit(solution)/shard_map/ppermute | solution.py:19
  45.9 6.5 %all-to-all-done.1 = f32[4,32,1152]{2,1,0:T(8,128)S(1)} async-done(((f32[4,32,1152]{2,1,0:T(8,128)}), f32[4,32,1152]{2,1,0:T(8,128)S(1)}, u32[]{:S(2)}, u32[]{:S(2)}) %all-to-all-start.1) | async-done | bytes 589856 | tf_op jit(solution)/shard_map/all_to_all | solution.py:175
  61.0 3.0 %collective-permute-start.16 = (f32[64,1152]{1,0:T(8,128)}, f32[64,1152]{1,0:T(8,128)}, u32[]{:S(2)}, u32[]{:S(2)}) collective-permute-start(f32[64,1152]{1,0:T(8,128)} %slice.71), channel_id=1, source_target_pairs={{24,0},{0,8},{8,16},{16,24},{25,1},{1,9},{9,17},{17,25},{26,2},{2,... | collective-permute-start | bytes 884744 | tf_op jit(solution)/shard_map/ppermute | solution.py:19
  70.4 4.9 %collective-permute-done.14.refs_7_ = f32[64,1152]{1,0:T(8,128)} collective-permute-done((f32[64,1152]{1,0:T(8,128)}, f32[64,1152]{1,0:T(8,128)}, u32[]{:S(2)}, u32[]{:S(2)}) %collective-permute-start.14) | collective-permute-done | bytes 294944 | tf_op jit(solution)/shard_map/ppermute | solution.py:19
  75.3 6.7 %image_terms.1 = (f32[128,1152]{1,0:T(8,128)S(1)}, f32[128,1152]{1,0:T(8,128)S(1)}, f32[256,512]{1,0:T(8,128)S(1)}, f32[256,512]{1,0:T(8,128)S(1)}) custom-call(f32[128,1152]{1,0:T(8,128)S(1)} %bitcast.13, f32[128,1152]{1,0:T(8,128)} %collective-permute-done.7.other, f32[256,128]{1,0:T(8,128)S(1)} %broadcast_in_dim.2.wanted, ...), custom_call_target="tpu_custom_call" | custom-call | tf_op jit(solution)/shard_map/image_terms/pallas_call | solution.py:96
  85.0 3.0 %caption_terms.3 = (f32[128,1152]{1,0:T(8,128)S(1)}, f32[128,1152]{1,0:T(8,128)S(1)}, f32[64,1152]{1,0:T(8,128)S(1)}, f32[64,1152]{1,0:T(8,128)}, f32[128,1152]{1,0:T(8,128)S(1)}) custom-call(f32[128,1152]{1,0:T(8,128)S(1)} %bitcast.14, f32[128,1152]{1,0:T(8,128)} %collective-permute-done.7.other, f32[256,512]{1,0:T(8,128)S(1)} %get-tuple-element.66.weights), custom_call_target="tpu_custom_call" | custom-call | flops 30000001024 | bytes 100000000 | tf_op jit(solution)/shard_map/caption_terms/pallas_call | solution.py:96
  89.4 3.5 %caption_terms.2 = (f32[128,1152]{1,0:T(8,128)S(1)}, f32[128,1152]{1,0:T(8,128)}, f32[128,1152]{1,0:T(8,128)}, f32[128,1152]{1,0:T(8,128)}) custom-call(f32[128,1152]{1,0:T(8,128)S(1)} %bitcast.15, f32[128,1152]{1,0:T(8,128)} %collective-permute-done.7.other, f32[256,512]{1,0:T(8,128)S(1)} %get-tuple-element.49.weights), custom_call_target="tpu_custom_call" | custom-call | flops 30000001024 | bytes 100000000 | tf_op jit(solution)/shard_map/caption_terms/pallas_call | solution.py:96
  95.8 3.5 %all-to-all-start.2 = ((f32[4,32,1152]{2,1,0:T(8,128)}), f32[4,32,1152]{2,1,0:T(8,128)S(1)}, u32[]{:S(2)}, u32[]{:S(2)}) async-start(f32[4,32,1152]{2,1,0:T(8,128)} %bitcast.18), calls=%async_computation.2 | async-start | bytes 1179648 | tf_op jit(solution)/shard_map/all_to_all | solution.py:205
  104.5 4.2 %collective-permute-done.21 = f32[64,1152]{1,0:T(8,128)S(1)} collective-permute-done((f32[64,1152]{1,0:T(8,128)S(1)}, f32[64,1152]{1,0:T(8,128)S(1)}, u32[]{:S(2)}, u32[]{:S(2)}) %collective-permute-start.21) | collective-permute-done | bytes 294944 | tf_op jit(solution)/shard_map/ppermute | solution.py:19
  109.9 5.7 %all-to-all-done.2 = f32[4,32,1152]{2,1,0:T(8,128)S(1)} async-done(((f32[4,32,1152]{2,1,0:T(8,128)}), f32[4,32,1152]{2,1,0:T(8,128)S(1)}, u32[]{:S(2)}, u32[]{:S(2)}) %all-to-all-start.2) | async-done | bytes 589856 | tf_op jit(solution)/shard_map/all_to_all | solution.py:205
  116.6 4.2 %all-to-all-start.3 = ((f32[4,32,1152]{2,1,0:T(8,128)}), f32[4,32,1152]{2,1,0:T(8,128)}, u32[]{:S(2)}, u32[]{:S(2)}) async-start(f32[4,32,1152]{2,1,0:T(8,128)} %bitcast.6), calls=%async_computation.3 | async-start | bytes 1179648 | tf_op jit(solution)/shard_map/all_to_all | solution.py:211
  120.7 2.5 %collective-permute-done.19.refs_3_ = f32[128,1152]{1,0:T(8,128)} collective-permute-done((f32[128,1152]{1,0:T(8,128)}, f32[128,1152]{1,0:T(8,128)}, u32[]{:S(2)}, u32[]{:S(2)}) %collective-permute-start.19) | collective-permute-done | bytes 589856 | tf_op jit(solution)/shard_map/ppermute | solution.py:19
  127.2 2.7 %collective-permute-start.30 = (f32[32,1152]{1,0:T(8,128)}, f32[32,1152]{1,0:T(8,128)}, u32[]{:S(2)}, u32[]{:S(2)}) collective-permute-start(f32[32,1152]{1,0:T(8,128)} %get-tuple-element.86), channel_id=1, source_target_pairs={{32,0},{64,32},{96,64},{0,96},{33,1},{65,33},{97,65},{1,97},{34,2}... | collective-permute-start | bytes 442376 | tf_op jit(solution)/shard_map/ppermute | solution.py:19
  134.9 2.2 %collective-permute-done.28 = f32[32,1152]{1,0:T(8,128)} collective-permute-done((f32[32,1152]{1,0:T(8,128)}, f32[32,1152]{1,0:T(8,128)}, u32[]{:S(2)}, u32[]{:S(2)}) %collective-permute-start.28) | collective-permute-done | bytes 147488 | tf_op jit(solution)/shard_map/ppermute | solution.py:19
  137.1 1.9 %collective-permute-start.26 = (f32[32,1152]{1,0:T(8,128)S(1)}, f32[32,1152]{1,0:T(8,128)S(1)}, u32[]{:S(2)}, u32[]{:S(2)}) collective-permute-start(f32[32,1152]{1,0:T(8,128)S(1)} %get-tuple-element.80), channel_id=1, source_target_pairs={{16,0},{24,8},{0,16},{8,24},{17,1},{25,9},{1,17},{9,25},{18,2},{26... | collective-permute-start | bytes 442376 | tf_op jit(solution)/shard_map/ppermute | solution.py:19
  140.1 2.7 %collective-permute-start.31 = (f32[32,1152]{1,0:T(8,128)S(1)}, f32[32,1152]{1,0:T(8,128)S(1)}, u32[]{:S(2)}, u32[]{:S(2)}) collective-permute-start(f32[32,1152]{1,0:T(8,128)S(1)} %add_add_fusion), channel_id=1, source_target_pairs={{128,0},{0,128},{129,1},{1,129},{130,2},{2,130},{131,3},{3,131},{1... | collective-permute-start | bytes 442376 | tf_op jit(solution)/shard_map/ppermute | solution.py:19
  142.8 3.0 %fusion.10 = f32[128,288]{0,1:T(8,128)} fusion(f32[128,1152]{1,0:T(8,128)} %bitcast.7, f32[288,1152]{1,0:T(8,128)S(1)} %copy-done), kind=kOutput, calls=%fused_computation.34 | convolution fusion | flops 509607936 | bytes 2064384 | tf_op jit(solution)/shard_map/dot_general | solution.py:45
  (112 shorter events, 56.8 us)
Async XLA Ops:
  7.6 24.3 %all-to-all-start = ((f32[4,32,1152]{2,1,0:T(8,128)}), f32[4,32,1152]{2,1,0:T(8,128)S(1)}, u32[]{:S(2)}, u32[]{:S(2)}) async-start(f32[4,32,1152]{2,1,0:T(8,128)} %bitcast), calls=%async_computation | async-start | bytes 1179648 | tf_op jit(solution)/shard_map/all_to_all | solution.py:165
  33.6 18.8 %all-to-all-start.1 = ((f32[4,32,1152]{2,1,0:T(8,128)}), f32[4,32,1152]{2,1,0:T(8,128)S(1)}, u32[]{:S(2)}, u32[]{:S(2)}) async-start(f32[4,32,1152]{2,1,0:T(8,128)} %bitcast.2), calls=%async_computation.1 | async-start | bytes 1179648 | tf_op jit(solution)/shard_map/all_to_all | solution.py:175
  38.1 14.9 %collective-permute-start.11 = (f32[128,1152]{1,0:T(8,128)S(1)}, f32[128,1152]{1,0:T(8,128)}, u32[]{:S(2)}, u32[]{:S(2)}) collective-permute-start(f32[128,1152]{1,0:T(8,128)S(1)} %pad_maximum_fusion.refs_0_), channel_id=1, source_target_pairs={{96,0},{0,32},{32,64},{64,96},{97,1},{1,33},{33,65},{65,97},{98,2}... | collective-permute-start | bytes 1769480 | tf_op jit(solution)/shard_map/ppermute | solution.py:19
  39.7 15.6 %collective-permute-start.9 = (f32[128,1152]{1,0:T(8,128)S(1)}, f32[128,1152]{1,0:T(8,128)S(1)}, u32[]{:S(2)}, u32[]{:S(2)}) collective-permute-start(f32[128,1152]{1,0:T(8,128)S(1)} %pad_maximum_fusion.refs_0_), channel_id=1, source_target_pairs={{32,0},{64,32},{96,64},{0,96},{33,1},{65,33},{97,65},{1,97},{34,2}... | collective-permute-start | bytes 1769480 | tf_op jit(solution)/shard_map/ppermute | solution.py:19
  41.4 16.2 %collective-permute-start.15 = (f32[128,1152]{1,0:T(8,128)}, f32[128,1152]{1,0:T(8,128)}, u32[]{:S(2)}, u32[]{:S(2)}) collective-permute-start(f32[128,1152]{1,0:T(8,128)} %pad_maximum_fusion.1.refs_5_), channel_id=1, source_target_pairs={{24,0},{0,8},{8,16},{16,24},{25,1},{1,9},{9,17},{17,25},{26,2},{2,... | collective-permute-start | bytes 1769480 | tf_op jit(solution)/shard_map/ppermute | solution.py:19
  44.6 16.3 %collective-permute-start.13 = (f32[128,1152]{1,0:T(8,128)}, f32[128,1152]{1,0:T(8,128)}, u32[]{:S(2)}, u32[]{:S(2)}) collective-permute-start(f32[128,1152]{1,0:T(8,128)} %pad_maximum_fusion.1.refs_5_), channel_id=1, source_target_pairs={{8,0},{16,8},{24,16},{0,24},{9,1},{17,9},{25,17},{1,25},{10,2},{18... | collective-permute-start | bytes 1769480 | tf_op jit(solution)/shard_map/ppermute | solution.py:19
  52.4 22.8 %collective-permute-start.7 = (f32[128,1152]{1,0:T(8,128)S(1)}, f32[128,1152]{1,0:T(8,128)}, u32[]{:S(2)}, u32[]{:S(2)}) collective-permute-start(f32[128,1152]{1,0:T(8,128)S(1)} %bitcast.12), channel_id=1, source_target_pairs={{4,0},{0,4},{5,1},{1,5},{6,2},{2,6},{7,3},{3,7},{12,8},{8,12},{13,... | collective-permute-start | bytes 1769480 | tf_op jit(solution)/shard_map/ppermute | solution.py:19
  53.1 12.6 %collective-permute-start.8 = (f32[128]{0:T(128)}, f32[128]{0:T(128)}, u32[]{:S(2)}, u32[]{:S(2)}) collective-permute-start(f32[128]{0:T(128)} %convert_element_type.31), channel_id=1, source_target_pairs={{4,0},{0,4},{5,1},{1,5},{6,2},{2,6},{7,3},{3,7},{12,8},{8,12},{13,... | collective-permute-start | bytes 1544 | tf_op jit(solution)/shard_map/ppermute | solution.py:19
  55.3 15.1 %collective-permute-start.12 = (f32[64,1152]{1,0:T(8,128)}, f32[64,1152]{1,0:T(8,128)S(1)}, u32[]{:S(2)}, u32[]{:S(2)}) collective-permute-start(f32[64,1152]{1,0:T(8,128)} %slice.69), channel_id=1, source_target_pairs={{96,0},{0,32},{32,64},{64,96},{97,1},{1,33},{33,65},{65,97},{98,2}... | collective-permute-start | bytes 884744 | tf_op jit(solution)/shard_map/ppermute | solution.py:19
  57.6 12.7 %collective-permute-start.10 = (f32[64,1152]{1,0:T(8,128)}, f32[64,1152]{1,0:T(8,128)}, u32[]{:S(2)}, u32[]{:S(2)}) collective-permute-start(f32[64,1152]{1,0:T(8,128)} %slice.68), channel_id=1, source_target_pairs={{32,0},{64,32},{96,64},{0,96},{33,1},{65,33},{97,65},{1,97},{34,2}... | collective-permute-start | bytes 884744 | tf_op jit(solution)/shard_map/ppermute | solution.py:19
  65.6 9.6 %collective-permute-start.14 = (f32[64,1152]{1,0:T(8,128)}, f32[64,1152]{1,0:T(8,128)}, u32[]{:S(2)}, u32[]{:S(2)}) collective-permute-start(f32[64,1152]{1,0:T(8,128)} %slice.70), channel_id=1, source_target_pairs={{8,0},{16,8},{24,16},{0,24},{9,1},{17,9},{25,17},{1,25},{10,2},{18... | collective-permute-start | bytes 884744 | tf_op jit(solution)/shard_map/ppermute | solution.py:19
  88.0 13.1 %collective-permute-start.23 = (f32[64,1152]{1,0:T(8,128)}, f32[64,1152]{1,0:T(8,128)}, u32[]{:S(2)}, u32[]{:S(2)}) collective-permute-start(f32[64,1152]{1,0:T(8,128)} %get-tuple-element.71), channel_id=1, source_target_pairs={{32,0},{64,32},{96,64},{0,96},{33,1},{65,33},{97,65},{1,97},{34,2}... | collective-permute-start | bytes 884744 | tf_op jit(solution)/shard_map/ppermute | solution.py:19
  93.7 27.0 %collective-permute-start.17 = (f32[128,1152]{1,0:T(8,128)}, f32[128,1152]{1,0:T(8,128)}, u32[]{:S(2)}, u32[]{:S(2)}) collective-permute-start(f32[128,1152]{1,0:T(8,128)} %get-tuple-element.51), channel_id=1, source_target_pairs={{24,0},{0,8},{8,16},{16,24},{25,1},{1,9},{9,17},{17,25},{26,2},{2,... | collective-permute-start | bytes 1769480 | tf_op jit(solution)/shard_map/ppermute | solution.py:19
  93.7 27.0 %collective-permute-start.18 = (f32[128,1152]{1,0:T(8,128)}, f32[128,1152]{1,0:T(8,128)}, u32[]{:S(2)}, u32[]{:S(2)}) collective-permute-start(f32[128,1152]{1,0:T(8,128)} %get-tuple-element.52), channel_id=1, source_target_pairs={{16,0},{24,8},{0,16},{8,24},{17,1},{25,9},{1,17},{9,25},{18,2},{26... | collective-permute-start | bytes 1769480 | tf_op jit(solution)/shard_map/ppermute | solution.py:19
  94.9 28.4 %collective-permute-start.19 = (f32[128,1152]{1,0:T(8,128)}, f32[128,1152]{1,0:T(8,128)}, u32[]{:S(2)}, u32[]{:S(2)}) collective-permute-start(f32[128,1152]{1,0:T(8,128)} %get-tuple-element.53), channel_id=1, source_target_pairs={{8,0},{16,8},{24,16},{0,24},{9,1},{17,9},{25,17},{1,25},{10,2},{18... | collective-permute-start | bytes 1769480 | tf_op jit(solution)/shard_map/ppermute | solution.py:19
  95.8 19.8 %all-to-all-start.2 = ((f32[4,32,1152]{2,1,0:T(8,128)}), f32[4,32,1152]{2,1,0:T(8,128)S(1)}, u32[]{:S(2)}, u32[]{:S(2)}) async-start(f32[4,32,1152]{2,1,0:T(8,128)} %bitcast.18), calls=%async_computation.2 | async-start | bytes 1179648 | tf_op jit(solution)/shard_map/all_to_all | solution.py:205
  99.3 9.5 %collective-permute-start.21 = (f32[64,1152]{1,0:T(8,128)S(1)}, f32[64,1152]{1,0:T(8,128)S(1)}, u32[]{:S(2)}, u32[]{:S(2)}) collective-permute-start(f32[64,1152]{1,0:T(8,128)S(1)} %get-tuple-element.69), channel_id=1, source_target_pairs={{96,0},{0,32},{32,64},{64,96},{97,1},{1,33},{33,65},{65,97},{98,2}... | collective-permute-start | bytes 884744 | tf_op jit(solution)/shard_map/ppermute | solution.py:19
  103.0 26.9 %collective-permute-start.24 = (f32[128,1152]{1,0:T(8,128)}, f32[128,1152]{1,0:T(8,128)S(1)}, u32[]{:S(2)}, u32[]{:S(2)}) collective-permute-start(f32[128,1152]{1,0:T(8,128)} %pad_maximum_fusion.3), channel_id=1, source_target_pairs={{32,0},{64,32},{96,64},{0,96},{33,1},{65,33},{97,65},{1,97},{34,2}... | collective-permute-start | bytes 1769480 | tf_op jit(solution)/shard_map/ppermute | solution.py:19
  109.7 20.2 %collective-permute-start.22 = (f32[128,1152]{1,0:T(8,128)}, f32[128,1152]{1,0:T(8,128)}, u32[]{:S(2)}, u32[]{:S(2)}) collective-permute-start(f32[128,1152]{1,0:T(8,128)} %pad_maximum_fusion.2), channel_id=1, source_target_pairs={{96,0},{0,32},{32,64},{64,96},{97,1},{1,33},{33,65},{65,97},{98,2}... | collective-permute-start | bytes 1769480 | tf_op jit(solution)/shard_map/ppermute | solution.py:19
  116.6 18.3 %all-to-all-start.3 = ((f32[4,32,1152]{2,1,0:T(8,128)}), f32[4,32,1152]{2,1,0:T(8,128)}, u32[]{:S(2)}, u32[]{:S(2)}) async-start(f32[4,32,1152]{2,1,0:T(8,128)} %bitcast.6), calls=%async_computation.3 | async-start | bytes 1179648 | tf_op jit(solution)/shard_map/all_to_all | solution.py:211
  126.6 10.5 %collective-permute-start.28 = (f32[32,1152]{1,0:T(8,128)}, f32[32,1152]{1,0:T(8,128)}, u32[]{:S(2)}, u32[]{:S(2)}) collective-permute-start(f32[32,1152]{1,0:T(8,128)} %get-tuple-element.85), channel_id=1, source_target_pairs={{96,0},{0,32},{32,64},{64,96},{97,1},{1,33},{33,65},{65,97},{98,2}... | collective-permute-start | bytes 442376 | tf_op jit(solution)/shard_map/ppermute | solution.py:19
  127.2 11.8 %collective-permute-start.30 = (f32[32,1152]{1,0:T(8,128)}, f32[32,1152]{1,0:T(8,128)}, u32[]{:S(2)}, u32[]{:S(2)}) collective-permute-start(f32[32,1152]{1,0:T(8,128)} %get-tuple-element.86), channel_id=1, source_target_pairs={{32,0},{64,32},{96,64},{0,96},{33,1},{65,33},{97,65},{1,97},{34,2}... | collective-permute-start | bytes 442376 | tf_op jit(solution)/shard_map/ppermute | solution.py:19
  131.1 14.7 %collective-permute-start.25 = (f32[32,1152]{1,0:T(8,128)S(1)}, f32[32,1152]{1,0:T(8,128)S(1)}, u32[]{:S(2)}, u32[]{:S(2)}) collective-permute-start(f32[32,1152]{1,0:T(8,128)S(1)} %get-tuple-element.78), channel_id=1, source_target_pairs={{24,0},{0,8},{8,16},{16,24},{25,1},{1,9},{9,17},{17,25},{26,2},{2,... | collective-permute-start | bytes 442376 | tf_op jit(solution)/shard_map/ppermute | solution.py:19
  132.3 13.4 %collective-permute-start.27 = (f32[32,1152]{1,0:T(8,128)S(1)}, f32[32,1152]{1,0:T(8,128)S(1)}, u32[]{:S(2)}, u32[]{:S(2)}) collective-permute-start(f32[32,1152]{1,0:T(8,128)S(1)} %get-tuple-element.79), channel_id=1, source_target_pairs={{8,0},{16,8},{24,16},{0,24},{9,1},{17,9},{25,17},{1,25},{10,2},{18... | collective-permute-start | bytes 442376 | tf_op jit(solution)/shard_map/ppermute | solution.py:19
  (25 other events, 161.8 us)
